TPU v7x, 256 devices: a whole 4x4x8 slice. The times are simulated.
256 devices in a mesh: tgt: 32 (over y, x, z_lo), src: 8 (over z_hi, core).
Axes of the slice: x: 4, y: 4, z: 8 (z_hi: 4, z_lo: 2; z = z_hi * 2 + z_lo), core: 2. Of those that a mesh axis runs over, the one named last changes fastest.
Arguments:
- connectome: bfloat16 [4096, 51200], P('tgt', 'src'), may hold values from -0.02734375 to 0.02734375
- history: bfloat16 [32, 32, 51200], P('tgt', None, 'src'), may hold values from 0 to 5
- delays: int32 [32, 400], P('tgt', 'src'), may hold values from 16 to 32
- cycle_head: int32 [1], replicated, may hold values from 0 to 31
- outside_afferent: float32 [32], replicated, may hold values from 120 to 320
- init_state: float32 [6, 32, 4096], P(None, None, 'tgt'), may hold values from -4 to 4
- lead_field: bfloat16 [4096, 256], P('tgt'), may hold values from -0.09375 to 0.09375
Outputs:
- sensor_signal: float32 [32, 16, 256], P('tgt')
- final_state: float32 [6, 32, 4096], P(None, None, ('tgt', 'src'))
Inputs may be any that keep to these rules, and one draw needn't show every extreme that they name: `cycle_head`: a slot of the history cycle.
All inputs are finite; a program needn't handle non-finite values.
Results may differ from a plain program's by a relative error of at most 0.003.
Values may be sent and summed in bfloat16 or wider, within the bound.
No kernel may reach another device: no remote copies, remote signals or barrier semaphores. Data moves between devices by JAX's collectives and lax.ppermute only.
A program may use at most 128 MiB of HBM per device.

v0:
```python
import jax
import jax.numpy as jnp
from jax import lax
from jax.sharding import PartitionSpec as P

STEPS = 16


integrator_step_width = 0.1
positive_synaptic_amplitude = 0.0325
negative_synaptic_amplitude = 0.11
interneuron_fraction = 0.5
global_link_scale = 30.0
stellate_contact_count = 135.0
recurrent_loop_contacts = 108.0
interneuron_contact_count = 33.75
peak_spike_rate = 5.0
logistic_slope_factor = 0.56
logistic_midpoint = 6.0


def spike_rate_response(cell_depolarization):
    return peak_spike_rate * jax.nn.sigmoid(
        logistic_slope_factor * (cell_depolarization - logistic_midpoint)
    )


def advance(carry, applied_stimulus, outside_afferent):
    (
        principal_cell_depolarization,
        stellate_mean_depolarization,
        interneuron_mean_depolarization,
        principal_cell_slope,
        excite_rate,
        interneuron_slope,
    ) = carry
    next_principal_cell_slope = principal_cell_slope + integrator_step_width * (
        positive_synaptic_amplitude
        * spike_rate_response(stellate_mean_depolarization - interneuron_mean_depolarization)
        - 2.0 * principal_cell_slope
        - principal_cell_depolarization
    )
    summed_afferent_rate = (
        outside_afferent[:, None]
        + recurrent_loop_contacts
        * spike_rate_response(stellate_contact_count * principal_cell_depolarization)
        + global_link_scale * applied_stimulus
    )
    new_excite_rate = excite_rate + integrator_step_width * (
        positive_synaptic_amplitude * summed_afferent_rate
        - 2.0 * excite_rate
        - stellate_mean_depolarization
    )
    next_interneuron_slope = interneuron_slope + integrator_step_width * (
        negative_synaptic_amplitude
        * interneuron_contact_count
        * spike_rate_response(interneuron_contact_count * principal_cell_depolarization)
        - 2.0 * interneuron_fraction * interneuron_slope
        - interneuron_fraction * interneuron_fraction * interneuron_mean_depolarization
    )
    return (
        principal_cell_depolarization + integrator_step_width * principal_cell_slope,
        stellate_mean_depolarization + integrator_step_width * excite_rate,
        interneuron_mean_depolarization + integrator_step_width * interneuron_slope,
        next_principal_cell_slope,
        new_excite_rate,
        next_interneuron_slope,
    )


def integrate(init_state, outside_afferent, coupling):

    def one_step(carry, applied_stimulus):
        fresh = advance(carry, applied_stimulus, outside_afferent)
        return (fresh, fresh[1] - fresh[2])

    begin = tuple((init_state[member] for member in range(6)))
    final, potentials = lax.scan(one_step, begin, coupling)
    return (jnp.stack(final), potentials)


def body(connectome, history, delays, cycle_head, outside_afferent, init_state, lead_field):
    tgt_rows = connectome.shape[0]
    target_blocks = delays.shape[0]
    source_blocks = delays.shape[1]
    block_rows = tgt_rows // target_blocks
    block_cols = connectome.shape[1] // source_blocks
    members = history.shape[1]
    slots_all = history.shape[0] * lax.axis_size("tgt")
    tiles = connectome.reshape(target_blocks, block_rows, source_blocks, block_cols)
    moments = jnp.arange(STEPS, dtype=jnp.int32)
    lag_slot = (cycle_head[0] + moments[None, None, :] - delays[:, :, None]) % slots_all
    whole = lax.all_gather(history, "tgt", axis=0, tiled=True)
    stacked = whole.reshape(slots_all, members, source_blocks, block_cols)
    slot_ids = jnp.arange(slots_all, dtype=jnp.int32)
    wanted = lag_slot[0].T
    picker = (wanted[:, None, :] == slot_ids[None, :, None]).astype(jnp.bfloat16)
    window = jnp.einsum(
        "tkb,kmbs->tmbs", picker, stacked, preferred_element_type=jnp.float32
    ).astype(jnp.bfloat16)
    pieces = jnp.einsum("rbs,tmbs->tmr", tiles[0], window, preferred_element_type=jnp.float32)
    share = tgt_rows // lax.axis_size("src")
    offset_rows = lax.axis_index("src") * share
    summed = lax.psum(pieces, "src")
    final_full, potentials = integrate(init_state, outside_afferent, summed)
    final_state = lax.dynamic_slice_in_dim(final_full, offset_rows, share, 2)
    potential = potentials.astype(jnp.bfloat16)
    signal = lax.psum_scatter(
        jnp.einsum("tmr,rs->mts", potential, lead_field, preferred_element_type=jnp.float32),
        "tgt",
        scatter_dimension=0,
        tiled=True,
    )
    return (signal, final_state)


def solution(mesh):
    in_specs = (
        P("tgt", "src"),
        P("tgt", None, "src"),
        P("tgt", "src"),
        P(),
        P(),
        P(None, None, "tgt"),
        P("tgt", None),
    )
    out_specs = (P("tgt", None, None), P(None, None, ("tgt", "src")))
    return jax.shard_map(body, mesh=mesh, in_specs=in_specs, out_specs=out_specs, check_vma=False)
```

profile of v0, /device:TPU:64, one launch (start us, length us, event | category | flops | bytes accessed | tf_op | source)
XLA Modules:
  0.0 601.3 jit_solution(12034502340109940469)
XLA Ops:
  7.2 0.7 all-gather.2.cloned.1.call-update
  7.9 0.0 all-reduce.2.cloned.1.call-start
  8.0 2.9 copy.27
  11.5 0.7 add_select_fusion
  12.3 290.1 %all-gather.2.cloned.1.call-done = bf16[32,32,6400]{2,1,0:T(8,128)(2,1)} async-done(((bf16[1,32,6400]{2,1,0:T(8,128)(2,1)}), bf16[32,32,6400]{2,1,0:T(8,128)(2,1)}) %all-gather.2.cloned.1.call-update) | async-done | bytes 13107216 | tf_op jit(solution)/shard_map/all_gather | solution.py:93
  302.3 21.3 %reshape.45 = bf16[32,32,50,128]{3,2,1,0:T(8,128)(2,1)} reshape(bf16[32,32,6400]{2,1,0:T(8,128)(2,1)} %all-gather.2.cloned.1.call-done) | data formatting | bytes 26214400 | tf_op jit(solution)/shard_map/reshape | solution.py:94
  323.6 23.8 %fusion.10 = f32[16,32,128,1]{2,0,1,3:T(8,128)S(1)} fusion(bf16[128,50,128,1]{0,2,3,1:T(8,128)(2,1)S(1)} %bitcast.67, bf16[32,32,50,128]{3,2,1,0:T(8,128)(2,1)} %reshape.45, s32[16,50]{0,1:T(8,128)S(1)} %add_select_fusion), kind=kOutput, calls=%fused_computation.15 | convolution fusion | flops 1051878400 | bytes 15010944 | tf_op jit(solution)/shard_map/rbs,tmbs->tmr/dot_general | solution.py:101
  347.4 0.8 copy.47
  348.2 0.0 reduce-scatter.2.cloned.1.call-start
  348.3 67.0 %all-reduce.2.cloned.1.call-done = f32[16,32,128]{2,1,0:T(8,128)} async-done(((f32[16,32,128]{2,1,0:T(8,128)}), f32[16,32,128]{2,1,0:T(8,128)}) %all-reduce.2.cloned.1.call-update) | async-done | bytes 262160 | tf_op jit(solution)/shard_map/psum | solution.py:104
  415.3 13.6 %while.25 = (s32[]{:T(128)}, f32[32,128]{1,0:T(8,128)S(1)}, f32[32,128]{1,0:T(8,128)S(1)}, f32[32,128]{1,0:T(8,128)S(1)}, f32[32,128]{1,0:T(8,128)S(1)}, /*index...) while((s32[]{:T(128)}, f32[32,128]{1,0:T(8,128)S(1)}, ...), condition=%wide.region_2.3_spmd, body=%wide.region_1.2_spmd.sunk | while | flops 192514 | bytes 360693 | solution.py:78
  415.3 0.8 multiply_add_fusion.8
  416.2 0.8 multiply_add_fusion.8
  417.0 0.8 multiply_add_fusion.8
  417.9 0.8 multiply_add_fusion.8
  418.7 0.8 multiply_add_fusion.8
  419.6 0.8 multiply_add_fusion.8
  420.4 0.8 multiply_add_fusion.8
  421.3 0.8 multiply_add_fusion.8
  422.1 0.8 multiply_add_fusion.8
  423.0 0.8 multiply_add_fusion.8
  423.8 0.8 multiply_add_fusion.8
  424.7 0.8 multiply_add_fusion.8
  425.5 0.8 multiply_add_fusion.8
  426.4 0.8 multiply_add_fusion.8
  427.2 0.8 multiply_add_fusion.8
  428.1 0.8 multiply_add_fusion.8
  429.0 0.2 convolution_bitcast_fusion
  429.2 1.1 copy.30
  430.4 0.1 constant_dynamic-slice_fusion
  430.5 0.7 copy.31
  431.2 163.6 %reduce-scatter.2.cloned.1.call-done = f32[1,16,256]{2,1,0:T(8,128)} async-done(((f32[32,16,256]{2,1,0:T(8,128)}), f32[1,16,256]{2,1,0:T(8,128)}) %reduce-scatter.2.cloned.1.call-update) | async-done | bytes 16400 | tf_op jit(solution)/shard_map/reduce_scatter | solution.py:108
  (66 shorter events, 0.5 us)
Async XLA Ops:
  7.2 421.8 %copy-start = (bf16[128,256]{1,0:T(8,128)(2,1)S(1)}, bf16[128,256]{1,0:T(8,128)(2,1)}, u32[]{:S(2)}) copy-start(bf16[128,256]{1,0:T(8,128)(2,1)} %param.15) | copy-start | bytes 196612
  7.2 295.2 %all-gather.2.cloned.1.call-start = ((), (), s32[]{:S(2)}) async-start(), calls=%async_computation.1 | async-start | bytes 13516800 | tf_op jit(solution)/shard_map/all_gather | solution.py:93
  7.9 407.4 %all-reduce.2.cloned.1.call-start = ((), (), s32[]{:S(2)}) async-start(), calls=%async_computation.2 | async-start | bytes 524288 | tf_op jit(solution)/shard_map/psum | solution.py:104
  323.6 24.7 %copy-start.1 = (f32[6,32,128]{2,1,0:T(8,128)S(1)}, f32[6,32,128]{2,1,0:T(8,128)}, u32[]{:S(2)}) copy-start(f32[6,32,128]{2,1,0:T(8,128)} %param.14) | copy-start | bytes 294916
  323.6 91.7 %copy-start.2 = (f32[32]{0:T(128)S(1)}, f32[32]{0:T(128)}, u32[]{:S(2)}) copy-start(f32[32]{0:T(128)} %param.13) | copy-start | bytes 388
  348.2 246.6 %reduce-scatter.2.cloned.1.call-start = ((), (), s32[]{:S(2)}) async-start(), calls=%async_computation.3 | async-start | bytes 540672 | tf_op jit(solution)/shard_map/reduce_scatter | solution.py:108
Sparse Core Ops, SparseCore 0:
  9.8 292.4 all-gather.1
  348.3 66.9 all-reduce.1
  430.4 164.3 reduce-scatter.1
where the time goes:
time: 603 us; the launch traced here: 601 us
  waiting for transfers between devices  521 us (86%)
  local copies, waits for them, and re-layouts  27 us (4%)
  matrix products  24 us (4%)
  between operations  14.5 us (2%)
  other arithmetic  13.7 us (2%)
    all_gather x1, waiting for transfers between devices, body(): whole = lax.all_gather(history, 'tgt', axis=0, tiled=True)  290 us
    reduce_scatter x1, waiting for transfers between devices, body(): lax.psum_scatter(jnp.einsum('tmr,rs->mts', potential, lead_field, preferr...  164 us
    psum x1, waiting for transfers between devices, body(): summed = lax.psum(pieces, 'src')  67 us
    dot_general x1, matrix products, body(): jnp.einsum('rbs,tmbs->tmr', tiles[0], window, preferred_element_type=jnp....  23.8 us
    reshape x1, local copies, waits for them, and re-layouts, body(): stacked = whole.reshape(slots_all, members, source_blocks, block_cols)  21.3 us
    add x16, other arithmetic, advance(): interneuron_slope + integrator_step_width * (negative_synaptic_amplitude...  12.7 us
  transfers between devices with their start and end apart: 3, of which 3 were waited for; matrix products, arithmetic and copies ran while one was open for 1% of the time, Pallas kernels for 0%

commit v1 on v0

v1 whole, which is shorter than its diff:
```python
import jax
import jax.numpy as jnp
from jax import lax
from jax.experimental import pallas as pl
from jax.experimental.pallas import tpu as pltpu
from jax.sharding import Mesh, PartitionSpec as P

STEPS = 16
MEM = 32
SLOTS = 32
BLOCK = 128
HALF = 3200
BLOCKS = HALF // BLOCK
WIDE = HALF + 128
OFFSETS = (0, -1, 1, 2)
TGT = ("y", "x", "zl")
SRC = ("zh", "c")

step_width = 0.1
positive_amplitude = 0.0325
negative_amplitude = 0.11
interneuron_fraction = 0.5
link_scale = 30.0
stellate_contacts = 135.0
loop_contacts = 108.0
interneuron_contacts = 33.75
peak_rate = 5.0
slope_factor = 0.56
midpoint = 6.0


def up(v, axis):
    return lax.ppermute(v, axis, [(i, (i + 1) % 4) for i in range(4)])


def down(v, axis):
    return lax.ppermute(v, axis, [(i, (i + 3) % 4) for i in range(4)])


def swap(v, axis):
    return lax.ppermute(v, axis, [(0, 1), (1, 0)])


def ring_gather(piece, first, second):
    left, right = up(piece, first), down(piece, first)
    low, high = up(left[:, :16], first), down(right[:, 16:], first)
    row = jnp.concatenate([piece, left, right, jnp.concatenate([low, high], axis=1)], axis=0)
    row_left, row_right = up(row, second), down(row, second)
    far_low, far_high = up(row_left[:2], second), down(row_right[2:], second)
    return [row, row_left, row_right, far_low, far_high]


def coupling_kernel(slots, starts, place, *refs):
    pieces = refs[:10]
    tiles = refs[10:12]
    keep, send, lead, ordered, total = refs[12:]
    at = 0
    for ref in pieces:
        for i in range(ref.shape[0]):
            slot = slots[at]
            row = pl.multiple_of(slot * MEM, MEM)
            ordered[pl.ds(row, MEM), :] = ref[i, :, :HALF]

            @pl.when(slot < STEPS)
            def _():
                ordered[pl.ds(row + SLOTS * MEM, MEM), :] = ref[i, :, :HALF]

            tg = pl.multiple_of(slot * 16, 16)
            lead[pl.ds(tg, 16), :BLOCK] = ref[i, :16, HALF:]
            lead[pl.ds(tg, 16), BLOCK:] = ref[i, 16:, HALF:]
            at += 1
    zl = place[0]
    core = place[1]
    for h in range(2):

        def window(b):
            row = pl.multiple_of(starts[h, b] * MEM, MEM)
            return ordered[pl.ds(row, STEPS * MEM), b * BLOCK:(b + 1) * BLOCK]

        for b in range(0, BLOCKS, 2):
            if b + 1 < BLOCKS:
                rates = jnp.concatenate([window(b), window(b + 1)], axis=1)
                weights = tiles[h][:, b * BLOCK:(b + 2) * BLOCK]
            else:
                rates = window(b)
                weights = tiles[h][:, b * BLOCK:(b + 1) * BLOCK]
            part = lax.dot_general(
                weights, rates, (((1,), (1,)), ((), ())), preferred_element_type=jnp.float32
            )
            if b == 0:
                total[...] = part
            else:
                total[...] += part
        z = zl if h == 0 else 1 - zl
        for q in range(4):
            mine = pl.multiple_of(q * 32 + core * 16, 16)
            other = pl.multiple_of(q * 32 + (1 - core) * 16, 16)
            keep[pl.ds(z * 4 + q, 1)] = total[pl.ds(mine, 16), :][None]
            send[pl.ds(z * 4 + q, 1)] = total[pl.ds(other, 16), :][None]


def spike_rate(v):
    return peak_rate * jax.nn.sigmoid(slope_factor * (v - midpoint))


def integrate_kernel(parts, afferent, begin, final, potential, rows):
    coupling = parts[0]
    for i in range(1, 8):
        coupling = coupling + parts[i]
    outside = afferent[...]
    y0, y1, y2, y3, y4, y5 = (begin[i] for i in range(6))
    for t in range(STEPS):
        applied = coupling[:, t * MEM:(t + 1) * MEM]
        n3 = y3 + step_width * (positive_amplitude * spike_rate(y1 - y2) - 2.0 * y3 - y0)
        summed = outside + loop_contacts * spike_rate(stellate_contacts * y0) + link_scale * applied
        n4 = y4 + step_width * (positive_amplitude * summed - 2.0 * y4 - y1)
        n5 = y5 + step_width * (
            negative_amplitude * interneuron_contacts * spike_rate(interneuron_contacts * y0)
            - 2.0 * interneuron_fraction * y5
            - interneuron_fraction * interneuron_fraction * y2
        )
        y0, y1, y2 = y0 + step_width * y3, y1 + step_width * y4, y2 + step_width * y5
        y3, y4, y5 = n3, n4, n5
        rows[pl.ds(t, 16, stride=STEPS), :] = y1 - y2
    for i, v in enumerate((y0, y1, y2, y3, y4, y5)):
        final[i] = v
    potential[...] = rows[...].astype(jnp.bfloat16)


def vmem(n):
    return [pl.BlockSpec(memory_space=pltpu.VMEM)] * n


def smem(n):
    return [pl.BlockSpec(memory_space=pltpu.SMEM)] * n


def body(connectome, history, delays, cycle_head, outside_afferent, init_state, lead_field):
    y, x, zl = lax.axis_index("y"), lax.axis_index("x"), lax.axis_index("zl")
    zh, core = lax.axis_index("zh"), lax.axis_index("c")
    part = zh * 2 + core
    near, far = zl * HALF, (1 - zl) * HALF

    lead_rows = lax.dynamic_slice_in_dim(lead_field, part * 16, 16, 0)
    extra = jnp.concatenate([lead_rows[:, :128], lead_rows[:, 128:]], axis=0)[None]

    def cut(column):
        rates = lax.dynamic_slice_in_dim(history, column, HALF, 2)
        return jnp.concatenate([rates, extra], axis=2)

    own = cut(near)
    partner = swap(cut(far), "zl")
    start = (cycle_head[0] - delays) & (SLOTS - 1)
    start_own = lax.dynamic_slice_in_dim(start, zl * BLOCKS, BLOCKS, 1)
    start_other = swap(lax.dynamic_slice_in_dim(start, (1 - zl) * BLOCKS, BLOCKS, 1), "zl")
    tile_own = lax.dynamic_slice_in_dim(connectome, near, HALF, 1)
    tile_other = swap(lax.dynamic_slice_in_dim(connectome, far, HALF, 1), "zl")

    pieces = ring_gather(own, "x", "y") + ring_gather(partner, "y", "x")
    offsets = jnp.array(OFFSETS, jnp.int32)
    ys, xs = (y + offsets) & 3, (x + offsets) & 3
    slots = jnp.concatenate(
        [
            (ys[:, None] * 8 + xs[None, :] * 2 + zl).reshape(-1),
            (ys[None, :] * 8 + xs[:, None] * 2 + (1 - zl)).reshape(-1),
        ]
    )
    starts = jnp.concatenate([start_own, start_other], axis=0)
    place = jnp.stack([zl, core])

    keep, send, lead = pl.pallas_call(
        coupling_kernel,
        out_shape=(
            jax.ShapeDtypeStruct((8, 16, STEPS * MEM), jnp.float32),
            jax.ShapeDtypeStruct((8, 16, STEPS * MEM), jnp.float32),
            jax.ShapeDtypeStruct((SLOTS * 16, 256), jnp.bfloat16),
        ),
        in_specs=smem(3) + vmem(12),
        out_specs=tuple(vmem(3)),
        scratch_shapes=[
            pltpu.VMEM(((SLOTS + STEPS) * MEM, HALF), jnp.bfloat16),
            pltpu.VMEM((BLOCK, STEPS * MEM), jnp.float32),
        ],
        compiler_params=pltpu.CompilerParams(vmem_limit_bytes=40 << 20),
        name="coupling",
    )(slots, starts, place, *pieces, tile_own, tile_other)

    joined = keep + swap(send, "c")
    parts = lax.all_to_all(joined, ("zl", "zh"), 0, 0, tiled=True)

    begin = jnp.transpose(lax.dynamic_slice_in_dim(init_state, part * 16, 16, 2), (0, 2, 1))
    final, potential = pl.pallas_call(
        integrate_kernel,
        out_shape=(
            jax.ShapeDtypeStruct((6, 16, MEM), jnp.float32),
            jax.ShapeDtypeStruct((16 * STEPS, MEM), jnp.bfloat16),
        ),
        in_specs=vmem(3),
        out_specs=tuple(vmem(2)),
        scratch_shapes=[pltpu.VMEM((16 * STEPS, MEM), jnp.float32)],
        name="integrate",
    )(parts, outside_afferent[None, :], begin)
    final_state = jnp.transpose(final, (0, 2, 1))

    sent = potential.T
    got = lax.all_to_all(sent, TGT, 0, 0, tiled=True)
    signal = lax.dot_general(
        got.reshape(SLOTS * 16, STEPS), lead, (((0,), (0,)), ((), ())), preferred_element_type=jnp.float32
    )
    signal = signal + swap(signal, "c")
    ahead, behind = up(signal, "zh"), down(signal, "zh")
    across = lax.ppermute(signal, "zh", [(i, (i + 2) % 4) for i in range(4)])
    signal = (signal + across) + (ahead + behind)
    return signal[None], final_state


def solution(mesh):
    fine = Mesh(mesh.devices.reshape(4, 4, 2, 4, 2), TGT + SRC)
    in_specs = (
        P(TGT, SRC),
        P(TGT, None, SRC),
        P(TGT, SRC),
        P(),
        P(),
        P(None, None, TGT),
        P(TGT, None),
    )
    out_specs = (P(TGT, None, None), P(None, None, TGT + SRC))
    return jax.shard_map(body, mesh=fine, in_specs=in_specs, out_specs=out_specs, check_vma=False)
```

time: 603 us -> 123 us (0.20)
  the two profiles are of different devices: /device:TPU:64 before, /device:TPU:1 now
where the time goes in v1:
time: 123 us
  starting transfers between devices  49.2 us (40%)
  waiting for transfers between devices  34.2 us (28%)
  blocking collectives  14.6 us (12%)
  local copies, waits for them, and re-layouts  12.3 us (10%)
  Pallas kernels  7.45 us (6%)
  other arithmetic  3.38 us (3%)
  between operations  1.5 us (1%)
    ppermute x9, starting transfers between devices, down(): return lax.ppermute(v, axis, [(i, (i + 3) % 4) for i in range(4)])  24 us
    ppermute x9, waiting for transfers between devices, up(): return lax.ppermute(v, axis, [(i, (i + 1) % 4) for i in range(4)])  16.5 us
    all_to_all x1, blocking collectives, body(): got = lax.all_to_all(sent, TGT, 0, 0, tiled=True)  14.6 us
    ppermute x5, starting transfers between devices, swap(): return lax.ppermute(v, axis, [(0, 1), (1, 0)])  13.9 us
    all_to_all x1, starting transfers between devices, body(): parts = lax.all_to_all(joined, ('zl', 'zh'), 0, 0, tiled=True)  7.28 us
    all_to_all x1, waiting for transfers between devices, body(): parts = lax.all_to_all(joined, ('zl', 'zh'), 0, 0, tiled=True)  6.78 us
    slice x4, local copies, waits for them, and re-layouts, ring_gather(): far_low, far_high = (up(row_left[:2], second), down(row_right[2:], second))  6.19 us
    pallas_call x1, Pallas kernels, body(): pl.pallas_call(coupling_kernel, out_shape=(jax.ShapeDtypeStruct((8, 16, S...  5.58 us
  transfers between devices with their start and end apart: 25, of which 11 were waited for; matrix products, arithmetic and copies ran while one was open for 7% of the time, Pallas kernels for 0%

profile of v1, /device:TPU:1, one launch (start us, length us, event | category | flops | bytes accessed | tf_op | source)
XLA Modules:
  0.0 122.8 jit_solution(9178972466005965581)
XLA Ops:
  1.4 1.1 constant_dynamic-slice_fusion.4
  2.5 2.6 %collective-permute-start.9 = (bf16[1,32,3328]{2,1,0:T(8,128)(2,1)S(1)}, bf16[1,32,3328]{2,1,0:T(8,128)(2,1)S(1)}, u32[]{:S(2)}, u32[]{:S(2)}) collective-permute-start(bf16[1,32,3328]{2,1,0:T(8,128)(2,1)S(1)} %get-tuple-element.18), channel_id=1, source_target_pairs={{0,8},{8,0},{1,9},{9,1},{2,10},{10,2},{3,11},{11,3},{4,12},{12,4},... | collective-permute-start | bytes 638984 | tf_op jit(solution)/shard_map/ppermute | solution.py:41
  5.1 2.5 %collective-permute-start.2 = (bf16[1,32,3328]{2,1,0:T(8,128)(2,1)S(1)}, bf16[1,32,3328]{2,1,0:T(8,128)(2,1)S(1)}, u32[]{:S(2)}, u32[]{:S(2)}) collective-permute-start(bf16[1,32,3328]{2,1,0:T(8,128)(2,1)S(1)} %get-tuple-element.19), channel_id=1, source_target_pairs={{0,48},{16,0},{32,16},{48,32},{1,49},{17,1},{33,17},{49,33},{2,50}... | collective-permute-start | bytes 638984 | tf_op jit(solution)/shard_map/ppermute | solution.py:37
  7.5 1.4 %collective-permute-done.9 = bf16[1,32,3328]{2,1,0:T(8,128)(2,1)S(1)} collective-permute-done((bf16[1,32,3328]{2,1,0:T(8,128)(2,1)S(1)}, bf16[1,32,3328]{2,1,0:T(8,128)(2,1)S(1)}, u32[]{:S(2)}, u32[]{:S(2)}) %collective-permute-start.9) | collective-permute-done | bytes 213024 | tf_op jit(solution)/shard_map/ppermute | solution.py:41
  9.0 3.7 %collective-permute-start.11 = (bf16[1,32,3328]{2,1,0:T(8,128)(2,1)S(1)}, bf16[1,32,3328]{2,1,0:T(8,128)(2,1)S(1)}, u32[]{:S(2)}, u32[]{:S(2)}) collective-permute-start(bf16[1,32,3328]{2,1,0:T(8,128)(2,1)S(1)} %collective-permute-done.9), channel_id=1, source_target_pairs={{0,192},{64,0},{128,64},{192,128},{1,193},{65,1},{129,65},{193,129... | collective-permute-start | bytes 638984 | tf_op jit(solution)/shard_map/ppermute | solution.py:37
  12.7 2.6 %collective-permute-start.4 = (bf16[1,16,3328]{2,1,0:T(8,128)(2,1)S(1)}, bf16[1,16,3328]{2,1,0:T(8,128)(2,1)S(1)}, u32[]{:S(2)}, u32[]{:S(2)}) collective-permute-start(bf16[1,16,3328]{2,1,0:T(8,128)(2,1)S(1)} %slice.41), channel_id=1, source_target_pairs={{0,48},{16,0},{32,16},{48,32},{1,49},{17,1},{33,17},{49,33},{2,50}... | collective-permute-start | bytes 319496 | tf_op jit(solution)/shard_map/ppermute | solution.py:37
  15.9 3.5 %collective-permute-start.13 = (bf16[1,16,3328]{2,1,0:T(8,128)(2,1)S(1)}, bf16[1,16,3328]{2,1,0:T(8,128)(2,1)S(1)}, u32[]{:S(2)}, u32[]{:S(2)}) collective-permute-start(bf16[1,16,3328]{2,1,0:T(8,128)(2,1)S(1)} %slice.45), channel_id=1, source_target_pairs={{0,192},{64,0},{128,64},{192,128},{1,193},{65,1},{129,65},{193,129... | collective-permute-start | bytes 319496 | tf_op jit(solution)/shard_map/ppermute | solution.py:37
  20.9 2.3 %collective-permute-start.6 = (bf16[4,32,3328]{2,1,0:T(8,128)(2,1)S(1)}, bf16[4,32,3328]{2,1,0:T(8,128)(2,1)}, u32[]{:S(2)}, u32[]{:S(2)}) collective-permute-start(bf16[4,32,3328]{2,1,0:T(8,128)(2,1)S(1)} %maximum_maximum_fusion.refs_0_), channel_id=1, source_target_pairs={{0,192},{64,0},{128,64},{192,128},{1,193},{65,1},{129,65},{193,129... | collective-permute-start | bytes 2555912 | tf_op jit(solution)/shard_map/ppermute | solution.py:37
  24.3 1.3 %collective-permute-start.14 = (bf16[4,32,3328]{2,1,0:T(8,128)(2,1)S(1)}, bf16[4,32,3328]{2,1,0:T(8,128)(2,1)}, u32[]{:S(2)}, u32[]{:S(2)}) collective-permute-start(bf16[4,32,3328]{2,1,0:T(8,128)(2,1)S(1)} %maximum_maximum_fusion.1.refs_5_), channel_id=1, source_target_pairs={{0,16},{16,32},{32,48},{48,0},{1,17},{17,33},{33,49},{49,1},{2,18}... | collective-permute-start | bytes 2555912 | tf_op jit(solution)/shard_map/ppermute | solution.py:33
  25.6 1.5 %collective-permute-start.15 = (bf16[4,32,3328]{2,1,0:T(8,128)(2,1)S(1)}, bf16[4,32,3328]{2,1,0:T(8,128)(2,1)}, u32[]{:S(2)}, u32[]{:S(2)}) collective-permute-start(bf16[4,32,3328]{2,1,0:T(8,128)(2,1)S(1)} %maximum_maximum_fusion.1.refs_5_), channel_id=1, source_target_pairs={{0,48},{16,0},{32,16},{48,32},{1,49},{17,1},{33,17},{49,33},{2,50}... | collective-permute-start | bytes 2555912 | tf_op jit(solution)/shard_map/ppermute | solution.py:37
  28.1 1.2 collective-permute-start.18
  30.0 10.9 %collective-permute-done.5.refs_1_ = bf16[4,32,3328]{2,1,0:T(8,128)(2,1)S(1)} collective-permute-done((bf16[4,32,3328]{2,1,0:T(8,128)(2,1)S(1)}, bf16[4,32,3328]{2,1,0:T(8,128)(2,1)S(1)}, u32[]{:S(2)}, u32[]{:S(2)}) %collective-permute-start.5) | collective-permute-done | bytes 852000 | tf_op jit(solution)/shard_map/ppermute | solution.py:33
  40.9 1.1 collective-permute-start
  42.9 1.8 %slice.43 = bf16[2,32,3328]{2,1,0:T(8,128)(2,1)} slice(bf16[4,32,3328]{2,1,0:T(8,128)(2,1)} %collective-permute-done.6.refs_2_), slice={[2:4], [0:32], [0:3328]} | slice | bytes 851968 | tf_op jit(solution)/shard_map/slice | solution.py:49
  44.7 2.7 %collective-permute-start.8 = (bf16[2,32,3328]{2,1,0:T(8,128)(2,1)}, bf16[2,32,3328]{2,1,0:T(8,128)(2,1)}, u32[]{:S(2)}, u32[]{:S(2)}) collective-permute-start(bf16[2,32,3328]{2,1,0:T(8,128)(2,1)} %slice.43), channel_id=1, source_target_pairs={{0,192},{64,0},{128,64},{192,128},{1,193},{65,1},{129,65},{193,129... | collective-permute-start | bytes 1277960 | tf_op jit(solution)/shard_map/ppermute | solution.py:37
  47.4 1.8 %slice.46 = bf16[2,32,3328]{2,1,0:T(8,128)(2,1)} slice(bf16[4,32,3328]{2,1,0:T(8,128)(2,1)} %collective-permute-done.14.refs_6_), slice={[0:2], [0:32], [0:3328]} | slice | bytes 851968 | tf_op jit(solution)/shard_map/slice | solution.py:49
  50.0 1.8 %slice.47 = bf16[2,32,3328]{2,1,0:T(8,128)(2,1)} slice(bf16[4,32,3328]{2,1,0:T(8,128)(2,1)} %collective-permute-done.15.refs_7_), slice={[2:4], [0:32], [0:3328]} | slice | bytes 851968 | tf_op jit(solution)/shard_map/slice | solution.py:49
  51.8 1.8 %collective-permute-start.17 = (bf16[2,32,3328]{2,1,0:T(8,128)(2,1)}, bf16[2,32,3328]{2,1,0:T(8,128)(2,1)}, u32[]{:S(2)}, u32[]{:S(2)}) collective-permute-start(bf16[2,32,3328]{2,1,0:T(8,128)(2,1)} %slice.47), channel_id=1, source_target_pairs={{0,48},{16,0},{32,16},{48,32},{1,49},{17,1},{33,17},{49,33},{2,50}... | collective-permute-start | bytes 1277960 | tf_op jit(solution)/shard_map/ppermute | solution.py:37
  54.1 3.6 %collective-permute-done.16.refs_8_ = bf16[2,32,3328]{2,1,0:T(8,128)(2,1)} collective-permute-done((bf16[2,32,3328]{2,1,0:T(8,128)(2,1)}, bf16[2,32,3328]{2,1,0:T(8,128)(2,1)}, u32[]{:S(2)}, u32[]{:S(2)}) %collective-permute-start.16) | collective-permute-done | bytes 426016 | tf_op jit(solution)/shard_map/ppermute | solution.py:33
  57.7 1.7 %collective-permute-done.17.refs_9_ = bf16[2,32,3328]{2,1,0:T(8,128)(2,1)} collective-permute-done((bf16[2,32,3328]{2,1,0:T(8,128)(2,1)}, bf16[2,32,3328]{2,1,0:T(8,128)(2,1)}, u32[]{:S(2)}, u32[]{:S(2)}) %collective-permute-start.17) | collective-permute-done | bytes 426016 | tf_op jit(solution)/shard_map/ppermute | solution.py:37
  59.4 5.6 %coupling.1 = (f32[8,16,512]{2,1,0:T(8,128)S(1)}, f32[8,16,512]{2,1,0:T(8,128)S(1)}, bf16[512,256]{1,0:T(8,128)(2,1)S(1)}) custom-call(s32[32]{0:T(128)S(1)} %pad_add_fusion.1.slots, s32[2,25]{1,0:T(2,128)S(1)} %pad_add_fusion.starts, s32[2]{0:T(128)S(1)} %pad_add_fusion.2.place, bf16[4,32,3328]{2,1,0:T(8,128)(2,1)S(1)} %maximum_maximum_fusion.refs_0_, ...), custom_call_target="tpu_custom_call" | custom-call | tf_op jit(solution)/shard_map/coupling/pallas_call | solution.py:171
  65.7 5.7 %collective-permute-start.19 = (f32[8,16,512]{2,1,0:T(8,128)S(1)}, f32[8,16,512]{2,1,0:T(8,128)S(1)}, u32[]{:S(2)}, u32[]{:S(2)}) collective-permute-start(f32[8,16,512]{2,1,0:T(8,128)S(1)} %get-tuple-element.8), channel_id=1, source_target_pairs={{0,1},{1,0},{2,3},{3,2},{4,5},{5,4},{6,7},{7,6},{8,9},{9,8},{10,11... | collective-permute-start | bytes 786440 | tf_op jit(solution)/shard_map/ppermute | solution.py:41
  71.3 1.2 collective-permute-done.19
  73.2 7.3 %all-to-all-start = ((f32[8,16,512]{2,1,0:T(8,128)}), f32[8,16,512]{2,1,0:T(8,128)S(1)}, u32[]{:S(2)}, u32[]{:S(2)}) async-start(f32[8,16,512]{2,1,0:T(8,128)} %add.120), calls=%async_computation | async-start | bytes 524288 | tf_op jit(solution)/shard_map/all_to_all | solution.py:189
  81.3 6.8 %all-to-all-done.parts = f32[8,16,512]{2,1,0:T(8,128)S(1)} async-done(((f32[8,16,512]{2,1,0:T(8,128)}), f32[8,16,512]{2,1,0:T(8,128)S(1)}, u32[]{:S(2)}, u32[]{:S(2)}) %all-to-all-start) | async-done | bytes 262176 | tf_op jit(solution)/shard_map/all_to_all | solution.py:189
  88.8 1.9 %integrate.1 = (f32[6,16,32]{2,1,0:T(8,128)}, bf16[256,32]{1,0:T(8,128)(2,1)}) custom-call(f32[8,16,512]{2,1,0:T(8,128)} %copy-done.4, f32[1,32]{1,0:T(1,128)} %bitcast.18, f32[6,16,32]{2,1,0:T(8,128)} %bitcast.16), custom_call_target="tpu_custom_call" | custom-call | tf_op jit(solution)/shard_map/integrate/pallas_call | solution.py:192
  91.2 1.5 %reduce.1 = bf16[32,256]{0,1:T(8,128)(2,1)S(1)} reduce(bf16[32,1,256]{0,2,1:T(8,128)(2,1)} %bitcast.17, bf16[]{:T(256)} %broadcast.37), dimensions={1}, to_apply=%copy.14.reduce_sub_computation | reduce | bytes 32770 | tf_op jit(solution)/shard_map/all_to_all | solution.py:206
  92.8 14.6 %all_to_all.14 = bf16[32,2,128]{2,1,0:T(2,128)(2,1)S(1)} all-to-all(bf16[32,2,128]{2,1,0:T(2,128)(2,1)S(1)} %reshape.32), channel_id=1, replica_groups=mesh['y'=4,'x'=4,'zl'=2,'zh'=4,'c'=2] {'y','x','zl'}, dimensions={0} | all-to-all | bytes 32768 | tf_op jit(solution)/shard_map/all_to_all | solution.py:206
  107.9 3.4 %collective-permute-start.20 = (f32[16,256]{1,0:T(8,128)S(1)}, f32[16,256]{1,0:T(8,128)S(1)}, u32[]{:S(2)}, u32[]{:S(2)}) collective-permute-start(f32[16,256]{1,0:T(8,128)S(1)} %fusion), channel_id=1, source_target_pairs={{0,1},{1,0},{2,3},{3,2},{4,5},{5,4},{6,7},{7,6},{8,9},{9,8},{10,11... | collective-permute-start | bytes 49160 | tf_op jit(solution)/shard_map/ppermute | solution.py:41
  112.1 3.6 %collective-permute-start.23 = (f32[16,256]{1,0:T(8,128)S(1)}, f32[16,256]{1,0:T(8,128)S(1)}, u32[]{:S(2)}, u32[]{:S(2)}) collective-permute-start(f32[16,256]{1,0:T(8,128)S(1)} %add.121), channel_id=1, source_target_pairs={{0,6},{2,0},{4,2},{6,4},{1,7},{3,1},{5,3},{7,5},{8,14},{10,8},{12,... | collective-permute-start | bytes 49160 | tf_op jit(solution)/shard_map/ppermute | solution.py:37
  115.7 1.2 collective-permute-start.21
  116.9 5.3 %collective-permute-done.21 = f32[16,256]{1,0:T(8,128)S(1)} collective-permute-done((f32[16,256]{1,0:T(8,128)S(1)}, f32[16,256]{1,0:T(8,128)S(1)}, u32[]{:S(2)}, u32[]{:S(2)}) %collective-permute-start.21) | collective-permute-done | bytes 16416 | tf_op jit(solution)/shard_map/ppermute | solution.py:212
  (72 shorter events, 12.7 us)
Async XLA Ops:
  0.6 79.9 %copy-start = (f32[6,32,128]{2,1,0:T(8,128)S(1)}, f32[6,32,128]{2,1,0:T(8,128)}, u32[]{:S(2)}) copy-start(f32[6,32,128]{2,1,0:T(8,128)} %param.13) | copy-start | bytes 294916
  2.5 6.5 %collective-permute-start.9 = (bf16[1,32,3328]{2,1,0:T(8,128)(2,1)S(1)}, bf16[1,32,3328]{2,1,0:T(8,128)(2,1)S(1)}, u32[]{:S(2)}, u32[]{:S(2)}) collective-permute-start(bf16[1,32,3328]{2,1,0:T(8,128)(2,1)S(1)} %get-tuple-element.18), channel_id=1, source_target_pairs={{0,8},{8,0},{1,9},{9,1},{2,10},{10,2},{3,11},{11,3},{4,12},{12,4},... | collective-permute-start | bytes 638984 | tf_op jit(solution)/shard_map/ppermute | solution.py:41
  5.1 7.6 %collective-permute-start.2 = (bf16[1,32,3328]{2,1,0:T(8,128)(2,1)S(1)}, bf16[1,32,3328]{2,1,0:T(8,128)(2,1)S(1)}, u32[]{:S(2)}, u32[]{:S(2)}) collective-permute-start(bf16[1,32,3328]{2,1,0:T(8,128)(2,1)S(1)} %get-tuple-element.19), channel_id=1, source_target_pairs={{0,48},{16,0},{32,16},{48,32},{1,49},{17,1},{33,17},{49,33},{2,50}... | collective-permute-start | bytes 638984 | tf_op jit(solution)/shard_map/ppermute | solution.py:37
  7.5 7.7 %collective-permute-start.1 = (bf16[1,32,3328]{2,1,0:T(8,128)(2,1)S(1)}, bf16[1,32,3328]{2,1,0:T(8,128)(2,1)S(1)}, u32[]{:S(2)}, u32[]{:S(2)}) collective-permute-start(bf16[1,32,3328]{2,1,0:T(8,128)(2,1)S(1)} %get-tuple-element.19), channel_id=1, source_target_pairs={{0,16},{16,32},{32,48},{48,0},{1,17},{17,33},{33,49},{49,1},{2,18}... | collective-permute-start | bytes 638984 | tf_op jit(solution)/shard_map/ppermute | solution.py:33
  9.0 6.9 %collective-permute-start.11 = (bf16[1,32,3328]{2,1,0:T(8,128)(2,1)S(1)}, bf16[1,32,3328]{2,1,0:T(8,128)(2,1)S(1)}, u32[]{:S(2)}, u32[]{:S(2)}) collective-permute-start(bf16[1,32,3328]{2,1,0:T(8,128)(2,1)S(1)} %collective-permute-done.9), channel_id=1, source_target_pairs={{0,192},{64,0},{128,64},{192,128},{1,193},{65,1},{129,65},{193,129... | collective-permute-start | bytes 638984 | tf_op jit(solution)/shard_map/ppermute | solution.py:37
  12.6 6.7 %collective-permute-start.10 = (bf16[1,32,3328]{2,1,0:T(8,128)(2,1)S(1)}, bf16[1,32,3328]{2,1,0:T(8,128)(2,1)S(1)}, u32[]{:S(2)}, u32[]{:S(2)}) collective-permute-start(bf16[1,32,3328]{2,1,0:T(8,128)(2,1)S(1)} %collective-permute-done.9), channel_id=1, source_target_pairs={{0,64},{64,128},{128,192},{192,0},{1,65},{65,129},{129,193},{193,1... | collective-permute-start | bytes 638984 | tf_op jit(solution)/shard_map/ppermute | solution.py:33
  12.7 6.8 %collective-permute-start.4 = (bf16[1,16,3328]{2,1,0:T(8,128)(2,1)S(1)}, bf16[1,16,3328]{2,1,0:T(8,128)(2,1)S(1)}, u32[]{:S(2)}, u32[]{:S(2)}) collective-permute-start(bf16[1,16,3328]{2,1,0:T(8,128)(2,1)S(1)} %slice.41), channel_id=1, source_target_pairs={{0,48},{16,0},{32,16},{48,32},{1,49},{17,1},{33,17},{49,33},{2,50}... | collective-permute-start | bytes 319496 | tf_op jit(solution)/shard_map/ppermute | solution.py:37
  15.2 5.1 %collective-permute-start.3 = (bf16[1,16,3328]{2,1,0:T(8,128)(2,1)S(1)}, bf16[1,16,3328]{2,1,0:T(8,128)(2,1)S(1)}, u32[]{:S(2)}, u32[]{:S(2)}) collective-permute-start(bf16[1,16,3328]{2,1,0:T(8,128)(2,1)S(1)} %slice.40), channel_id=1, source_target_pairs={{0,16},{16,32},{32,48},{48,0},{1,17},{17,33},{33,49},{49,1},{2,18}... | collective-permute-start | bytes 319496 | tf_op jit(solution)/shard_map/ppermute | solution.py:33
  15.9 7.4 %collective-permute-start.13 = (bf16[1,16,3328]{2,1,0:T(8,128)(2,1)S(1)}, bf16[1,16,3328]{2,1,0:T(8,128)(2,1)S(1)}, u32[]{:S(2)}, u32[]{:S(2)}) collective-permute-start(bf16[1,16,3328]{2,1,0:T(8,128)(2,1)S(1)} %slice.45), channel_id=1, source_target_pairs={{0,192},{64,0},{128,64},{192,128},{1,193},{65,1},{129,65},{193,129... | collective-permute-start | bytes 319496 | tf_op jit(solution)/shard_map/ppermute | solution.py:37
  19.4 7.7 %copy-start.3 = (bf16[128,6400]{1,0:T(8,128)(2,1)S(1)}, bf16[128,6400]{1,0:T(8,128)(2,1)}, u32[]{:S(2)}) copy-start(bf16[128,6400]{1,0:T(8,128)(2,1)} %param.8) | copy-start | bytes 4915204
  19.4 4.8 %collective-permute-start.12 = (bf16[1,16,3328]{2,1,0:T(8,128)(2,1)S(1)}, bf16[1,16,3328]{2,1,0:T(8,128)(2,1)S(1)}, u32[]{:S(2)}, u32[]{:S(2)}) collective-permute-start(bf16[1,16,3328]{2,1,0:T(8,128)(2,1)S(1)} %slice.44), channel_id=1, source_target_pairs={{0,64},{64,128},{128,192},{192,0},{1,65},{65,129},{129,193},{193,1... | collective-permute-start | bytes 319496 | tf_op jit(solution)/shard_map/ppermute | solution.py:33
  20.4 20.5 %collective-permute-start.5 = (bf16[4,32,3328]{2,1,0:T(8,128)(2,1)S(1)}, bf16[4,32,3328]{2,1,0:T(8,128)(2,1)S(1)}, u32[]{:S(2)}, u32[]{:S(2)}) collective-permute-start(bf16[4,32,3328]{2,1,0:T(8,128)(2,1)S(1)} %maximum_maximum_fusion.refs_0_), channel_id=1, source_target_pairs={{0,64},{64,128},{128,192},{192,0},{1,65},{65,129},{129,193},{193,1... | collective-permute-start | bytes 2555912 | tf_op jit(solution)/shard_map/ppermute | solution.py:33
  20.9 21.9 %collective-permute-start.6 = (bf16[4,32,3328]{2,1,0:T(8,128)(2,1)S(1)}, bf16[4,32,3328]{2,1,0:T(8,128)(2,1)}, u32[]{:S(2)}, u32[]{:S(2)}) collective-permute-start(bf16[4,32,3328]{2,1,0:T(8,128)(2,1)S(1)} %maximum_maximum_fusion.refs_0_), channel_id=1, source_target_pairs={{0,192},{64,0},{128,64},{192,128},{1,193},{65,1},{129,65},{193,129... | collective-permute-start | bytes 2555912 | tf_op jit(solution)/shard_map/ppermute | solution.py:37
  24.3 5.6 %copy-start.6 = (s32[1,50]{1,0:T(1,128)S(1)}, s32[1,50]{1,0:T(1,128)}, u32[]{:S(2)}) copy-start(s32[1,50]{1,0:T(1,128)} %param.10) | copy-start | bytes 604
  24.3 5.7 %copy-start.5 = (s32[4]{0:T(128)S(1)}, s32[4]{0:T(128)}, u32[]{:S(2)}) copy-start(s32[4]{0:T(128)} %constant.48.clone) | copy-start | bytes 52
  24.3 20.4 %collective-permute-start.14 = (bf16[4,32,3328]{2,1,0:T(8,128)(2,1)S(1)}, bf16[4,32,3328]{2,1,0:T(8,128)(2,1)}, u32[]{:S(2)}, u32[]{:S(2)}) collective-permute-start(bf16[4,32,3328]{2,1,0:T(8,128)(2,1)S(1)} %maximum_maximum_fusion.1.refs_5_), channel_id=1, source_target_pairs={{0,16},{16,32},{32,48},{48,0},{1,17},{17,33},{33,49},{49,1},{2,18}... | collective-permute-start | bytes 2555912 | tf_op jit(solution)/shard_map/ppermute | solution.py:33
  25.6 23.6 %collective-permute-start.15 = (bf16[4,32,3328]{2,1,0:T(8,128)(2,1)S(1)}, bf16[4,32,3328]{2,1,0:T(8,128)(2,1)}, u32[]{:S(2)}, u32[]{:S(2)}) collective-permute-start(bf16[4,32,3328]{2,1,0:T(8,128)(2,1)S(1)} %maximum_maximum_fusion.1.refs_5_), channel_id=1, source_target_pairs={{0,48},{16,0},{32,16},{48,32},{1,49},{17,1},{33,17},{49,33},{2,50}... | collective-permute-start | bytes 2555912 | tf_op jit(solution)/shard_map/ppermute | solution.py:37
  28.1 26.0 %collective-permute-start.18 = (bf16[128,3200]{1,0:T(8,128)(2,1)}, bf16[128,3200]{1,0:T(8,128)(2,1)}, u32[]{:S(2)}, u32[]{:S(2)}) collective-permute-start(bf16[128,3200]{1,0:T(8,128)(2,1)} %get-tuple-element.12), channel_id=1, source_target_pairs={{0,8},{8,0},{1,9},{9,1},{2,10},{10,2},{3,11},{11,3},{4,12},{12,4},... | collective-permute-start | bytes 2457608 | tf_op jit(solution)/shard_map/ppermute | solution.py:41
  40.9 10.9 %collective-permute-start = (s32[1,25]{1,0:T(1,128)S(1)}, s32[1,25]{1,0:T(1,128)S(1)}, u32[]{:S(2)}, u32[]{:S(2)}) collective-permute-start(s32[1,25]{1,0:T(1,128)S(1)} %get-tuple-element.23), channel_id=1, source_target_pairs={{0,8},{8,0},{1,9},{9,1},{2,10},{10,2},{3,11},{11,3},{4,12},{12,4},... | collective-permute-start | bytes 308 | tf_op jit(solution)/shard_map/ppermute | solution.py:41
  42.9 11.2 %collective-permute-start.7 = (bf16[2,32,3328]{2,1,0:T(8,128)(2,1)}, bf16[2,32,3328]{2,1,0:T(8,128)(2,1)}, u32[]{:S(2)}, u32[]{:S(2)}) collective-permute-start(bf16[2,32,3328]{2,1,0:T(8,128)(2,1)} %slice.42), channel_id=1, source_target_pairs={{0,64},{64,128},{128,192},{192,0},{1,65},{65,129},{129,193},{193,1... | collective-permute-start | bytes 1277960 | tf_op jit(solution)/shard_map/ppermute | solution.py:33
  44.7 9.4 %collective-permute-start.8 = (bf16[2,32,3328]{2,1,0:T(8,128)(2,1)}, bf16[2,32,3328]{2,1,0:T(8,128)(2,1)}, u32[]{:S(2)}, u32[]{:S(2)}) collective-permute-start(bf16[2,32,3328]{2,1,0:T(8,128)(2,1)} %slice.43), channel_id=1, source_target_pairs={{0,192},{64,0},{128,64},{192,128},{1,193},{65,1},{129,65},{193,129... | collective-permute-start | bytes 1277960 | tf_op jit(solution)/shard_map/ppermute | solution.py:37
  49.2 8.5 %collective-permute-start.16 = (bf16[2,32,3328]{2,1,0:T(8,128)(2,1)}, bf16[2,32,3328]{2,1,0:T(8,128)(2,1)}, u32[]{:S(2)}, u32[]{:S(2)}) collective-permute-start(bf16[2,32,3328]{2,1,0:T(8,128)(2,1)} %slice.46), channel_id=1, source_target_pairs={{0,16},{16,32},{32,48},{48,0},{1,17},{17,33},{33,49},{49,1},{2,18}... | collective-permute-start | bytes 1277960 | tf_op jit(solution)/shard_map/ppermute | solution.py:33
  51.8 7.6 %collective-permute-start.17 = (bf16[2,32,3328]{2,1,0:T(8,128)(2,1)}, bf16[2,32,3328]{2,1,0:T(8,128)(2,1)}, u32[]{:S(2)}, u32[]{:S(2)}) collective-permute-start(bf16[2,32,3328]{2,1,0:T(8,128)(2,1)} %slice.47), channel_id=1, source_target_pairs={{0,48},{16,0},{32,16},{48,32},{1,49},{17,1},{33,17},{49,33},{2,50}... | collective-permute-start | bytes 1277960 | tf_op jit(solution)/shard_map/ppermute | solution.py:37
  65.0 0.7 copy-start.1
  65.7 42.0 %copy-start.2 = (bf16[512,256]{1,0:T(8,128)(2,1)S(1)}, bf16[512,256]{1,0:T(8,128)(2,1)}, u32[]{:S(2)}) copy-start(bf16[512,256]{1,0:T(8,128)(2,1)} %copy-done.1) | copy-start | bytes 786436
  65.7 6.8 %collective-permute-start.19 = (f32[8,16,512]{2,1,0:T(8,128)S(1)}, f32[8,16,512]{2,1,0:T(8,128)S(1)}, u32[]{:S(2)}, u32[]{:S(2)}) collective-permute-start(f32[8,16,512]{2,1,0:T(8,128)S(1)} %get-tuple-element.8), channel_id=1, source_target_pairs={{0,1},{1,0},{2,3},{3,2},{4,5},{5,4},{6,7},{7,6},{8,9},{9,8},{10,11... | collective-permute-start | bytes 786440 | tf_op jit(solution)/shard_map/ppermute | solution.py:41
  73.2 14.9 %all-to-all-start = ((f32[8,16,512]{2,1,0:T(8,128)}), f32[8,16,512]{2,1,0:T(8,128)S(1)}, u32[]{:S(2)}, u32[]{:S(2)}) async-start(f32[8,16,512]{2,1,0:T(8,128)} %add.120), calls=%async_computation | async-start | bytes 524288 | tf_op jit(solution)/shard_map/all_to_all | solution.py:189
  88.1 0.7 copy-start.4
  107.9 4.3 %collective-permute-start.20 = (f32[16,256]{1,0:T(8,128)S(1)}, f32[16,256]{1,0:T(8,128)S(1)}, u32[]{:S(2)}, u32[]{:S(2)}) collective-permute-start(f32[16,256]{1,0:T(8,128)S(1)} %fusion), channel_id=1, source_target_pairs={{0,1},{1,0},{2,3},{3,2},{4,5},{5,4},{6,7},{7,6},{8,9},{9,8},{10,11... | collective-permute-start | bytes 49160 | tf_op jit(solution)/shard_map/ppermute | solution.py:41
  112.1 4.8 %collective-permute-start.22 = (f32[16,256]{1,0:T(8,128)S(1)}, f32[16,256]{1,0:T(8,128)S(1)}, u32[]{:S(2)}, u32[]{:S(2)}) collective-permute-start(f32[16,256]{1,0:T(8,128)S(1)} %add.121), channel_id=1, source_target_pairs={{0,2},{2,4},{4,6},{6,0},{1,3},{3,5},{5,7},{7,1},{8,10},{10,12},{12... | collective-permute-start | bytes 49160 | tf_op jit(solution)/shard_map/ppermute | solution.py:33
  112.1 4.8 %collective-permute-start.23 = (f32[16,256]{1,0:T(8,128)S(1)}, f32[16,256]{1,0:T(8,128)S(1)}, u32[]{:S(2)}, u32[]{:S(2)}) collective-permute-start(f32[16,256]{1,0:T(8,128)S(1)} %add.121), channel_id=1, source_target_pairs={{0,6},{2,0},{4,2},{6,4},{1,7},{3,1},{5,3},{7,5},{8,14},{10,8},{12,... | collective-permute-start | bytes 49160 | tf_op jit(solution)/shard_map/ppermute | solution.py:37
  115.7 6.5 %collective-permute-start.21 = (f32[16,256]{1,0:T(8,128)S(1)}, f32[16,256]{1,0:T(8,128)S(1)}, u32[]{:S(2)}, u32[]{:S(2)}) collective-permute-start(f32[16,256]{1,0:T(8,128)S(1)} %add.121), channel_id=1, source_target_pairs={{0,4},{2,6},{4,0},{6,2},{1,5},{3,7},{5,1},{7,3},{8,12},{10,14},{12... | collective-permute-start | bytes 49160 | tf_op jit(solution)/shard_map/ppermute | solution.py:212

commit v2 on v1

--- a/solution.py
+++ b/solution.py
@@ -11,7 +11,7 @@
 BLOCK = 128
 HALF = 3200
 BLOCKS = HALF // BLOCK
-WIDE = HALF + 128
+SENSORS = 256
 OFFSETS = (0, -1, 1, 2)
 TGT = ("y", "x", "zl")
 SRC = ("zh", "c")
@@ -47,7 +47,7 @@
     row = jnp.concatenate([piece, left, right, jnp.concatenate([low, high], axis=1)], axis=0)
     row_left, row_right = up(row, second), down(row, second)
     far_low, far_high = up(row_left[:2], second), down(row_right[2:], second)
-    return [row, row_left, row_right, far_low, far_high]
+    return [row, row_left, row_right, far_low, far_high], left
 
 
 def coupling_kernel(slots, starts, place, *refs):
@@ -65,9 +65,9 @@
             def _():
                 ordered[pl.ds(row + SLOTS * MEM, MEM), :] = ref[i, :, :HALF]
 
-            tg = pl.multiple_of(slot * 16, 16)
-            lead[pl.ds(tg, 16), :BLOCK] = ref[i, :16, HALF:]
-            lead[pl.ds(tg, 16), BLOCK:] = ref[i, 16:, HALF:]
+            tg = pl.multiple_of(slot * 64, 64)
+            lead[pl.ds(tg, MEM), :] = ref[i, :, HALF:HALF + SENSORS]
+            lead[pl.ds(tg + MEM, MEM), :] = ref[i, :, HALF + SENSORS:]
             at += 1
     zl = place[0]
     core = place[1]
@@ -108,7 +108,7 @@
     for i in range(1, 8):
         coupling = coupling + parts[i]
     outside = afferent[...]
-    y0, y1, y2, y3, y4, y5 = (begin[i] for i in range(6))
+    y0, y1, y2, y3, y4, y5 = (begin[i].T for i in range(6))
     for t in range(STEPS):
         applied = coupling[:, t * MEM:(t + 1) * MEM]
         n3 = y3 + step_width * (positive_amplitude * spike_rate(y1 - y2) - 2.0 * y3 - y0)
@@ -123,8 +123,11 @@
         y3, y4, y5 = n3, n4, n5
         rows[pl.ds(t, 16, stride=STEPS), :] = y1 - y2
     for i, v in enumerate((y0, y1, y2, y3, y4, y5)):
-        final[i] = v
-    potential[...] = rows[...].astype(jnp.bfloat16)
+        final[i] = v.T
+    flat = rows[...].T.astype(jnp.bfloat16)
+    for i in range(4):
+        potential[:, i, 0, :] = flat[:, :128]
+        potential[:, i, 1, :] = flat[:, 128:]
 
 
 def vmem(n):
@@ -141,22 +144,26 @@
     part = zh * 2 + core
     near, far = zl * HALF, (1 - zl) * HALF
 
-    lead_rows = lax.dynamic_slice_in_dim(lead_field, part * 16, 16, 0)
-    extra = jnp.concatenate([lead_rows[:, :128], lead_rows[:, 128:]], axis=0)[None]
-
-    def cut(column):
-        rates = lax.dynamic_slice_in_dim(history, column, HALF, 2)
-        return jnp.concatenate([rates, extra], axis=2)
-
-    own = cut(near)
-    partner = swap(cut(far), "zl")
+    lead_rows = lax.dynamic_index_in_dim(lead_field.reshape(4, 2, 16, SENSORS), core, 1, False)
+    lead_rows = lead_rows.reshape(2, 32, SENSORS)
+    extra = jnp.concatenate([lead_rows[0], lead_rows[1]], axis=1)[None]
+
+    partner = swap(jnp.concatenate([lax.dynamic_slice_in_dim(history, far, HALF, 2), extra], axis=2), "zl")
+    own = jnp.concatenate([lax.dynamic_slice_in_dim(history, near, HALF, 2), extra], axis=2)
     start = (cycle_head[0] - delays) & (SLOTS - 1)
     start_own = lax.dynamic_slice_in_dim(start, zl * BLOCKS, BLOCKS, 1)
-    start_other = swap(lax.dynamic_slice_in_dim(start, (1 - zl) * BLOCKS, BLOCKS, 1), "zl")
+    start_far = lax.dynamic_slice_in_dim(start, (1 - zl) * BLOCKS, BLOCKS, 1)
     tile_own = lax.dynamic_slice_in_dim(connectome, near, HALF, 1)
-    tile_other = swap(lax.dynamic_slice_in_dim(connectome, far, HALF, 1), "zl")
-
-    pieces = ring_gather(own, "x", "y") + ring_gather(partner, "y", "x")
+    tile_far = lax.dynamic_slice_in_dim(connectome, far, HALF, 1)
+    note = jnp.pad(start_far.astype(jnp.bfloat16), ((0, 0), (0, BLOCK - BLOCKS)))
+    tile_far = jnp.concatenate([tile_far, jnp.broadcast_to(note, (BLOCK, BLOCK))], axis=1)
+
+    own_pieces, _ = ring_gather(own, "x", "y")
+    other_pieces, early = ring_gather(partner, "y", "x")
+    pieces = own_pieces + other_pieces
+    tile_far, _ = lax.optimization_barrier((tile_far, early))
+    tile_other = swap(tile_far, "zl")
+    start_other = tile_other[:1, HALF:HALF + BLOCKS].astype(jnp.int32)
     offsets = jnp.array(OFFSETS, jnp.int32)
     ys, xs = (y + offsets) & 3, (x + offsets) & 3
     slots = jnp.concatenate(
@@ -173,7 +180,7 @@
         out_shape=(
             jax.ShapeDtypeStruct((8, 16, STEPS * MEM), jnp.float32),
             jax.ShapeDtypeStruct((8, 16, STEPS * MEM), jnp.float32),
-            jax.ShapeDtypeStruct((SLOTS * 16, 256), jnp.bfloat16),
+            jax.ShapeDtypeStruct((SLOTS * 64, SENSORS), jnp.bfloat16),
         ),
         in_specs=smem(3) + vmem(12),
         out_specs=tuple(vmem(3)),
@@ -181,36 +188,32 @@
             pltpu.VMEM(((SLOTS + STEPS) * MEM, HALF), jnp.bfloat16),
             pltpu.VMEM((BLOCK, STEPS * MEM), jnp.float32),
         ],
-        compiler_params=pltpu.CompilerParams(vmem_limit_bytes=40 << 20),
+        compiler_params=pltpu.CompilerParams(vmem_limit_bytes=24 << 20),
         name="coupling",
     )(slots, starts, place, *pieces, tile_own, tile_other)
 
     joined = keep + swap(send, "c")
+    begin = lax.dynamic_slice_in_dim(init_state, part * 16, 16, 2)
+    joined, begin, outside = lax.optimization_barrier((joined, begin, outside_afferent[None, :]))
     parts = lax.all_to_all(joined, ("zl", "zh"), 0, 0, tiled=True)
-
-    begin = jnp.transpose(lax.dynamic_slice_in_dim(init_state, part * 16, 16, 2), (0, 2, 1))
-    final, potential = pl.pallas_call(
+    final_state, potential = pl.pallas_call(
         integrate_kernel,
         out_shape=(
-            jax.ShapeDtypeStruct((6, 16, MEM), jnp.float32),
-            jax.ShapeDtypeStruct((16 * STEPS, MEM), jnp.bfloat16),
+            jax.ShapeDtypeStruct((6, MEM, 16), jnp.float32),
+            jax.ShapeDtypeStruct((MEM, 4, 2, 128), jnp.bfloat16),
         ),
         in_specs=vmem(3),
         out_specs=tuple(vmem(2)),
         scratch_shapes=[pltpu.VMEM((16 * STEPS, MEM), jnp.float32)],
+        compiler_params=pltpu.CompilerParams(vmem_limit_bytes=4 << 20),
         name="integrate",
-    )(parts, outside_afferent[None, :], begin)
-    final_state = jnp.transpose(final, (0, 2, 1))
-
-    sent = potential.T
-    got = lax.all_to_all(sent, TGT, 0, 0, tiled=True)
+    )(parts, outside, begin)
+
+    got = lax.all_to_all(potential.reshape(MEM * 4, 2, 128), TGT + ("zh",), 0, 0, tiled=True)
     signal = lax.dot_general(
-        got.reshape(SLOTS * 16, STEPS), lead, (((0,), (0,)), ((), ())), preferred_element_type=jnp.float32
+        got.reshape(SLOTS * 64, STEPS), lead, (((0,), (0,)), ((), ())), preferred_element_type=jnp.float32
     )
     signal = signal + swap(signal, "c")
-    ahead, behind = up(signal, "zh"), down(signal, "zh")
-    across = lax.ppermute(signal, "zh", [(i, (i + 2) % 4) for i in range(4)])
-    signal = (signal + across) + (ahead + behind)
     return signal[None], final_state
 
 

time: 123 us -> 116 us (0.943)
  blocking collectives: 14.6 us -> 39.2 us
  starting transfers between devices: 49.2 us -> 33 us
  waiting for transfers between devices: 34.2 us -> 23.1 us
  local copies, waits for them, and re-layouts: 12.3 us -> 9.65 us
  Pallas kernels: 7.45 us -> 5.99 us
    all_to_all x1 -> x2, blocking collectives: 14.6 us -> 39.2 us  [the longest x1 24.1 us: body(): lax.all_to_all(potential.reshape(MEM * 4, 2, 128), TGT + ('zh',), 0, 0, t...]
    ppermute x9 -> x8, waiting for transfers between devices: 2.26 us -> 14.1 us  [down(): return lax.ppermute(v, axis, [(i, (i + 3) % 4) for i in range(4)])]
    ppermute x9 -> x8, waiting for transfers between devices: 16.5 us -> 5.68 us  [up(): return lax.ppermute(v, axis, [(i, (i + 1) % 4) for i in range(4)])]
    ppermute x9 -> x8, starting transfers between devices: 24 us -> 14.6 us  [down(): return lax.ppermute(v, axis, [(i, (i + 3) % 4) for i in range(4)])]
    all_to_all x1 -> x0, starting transfers between devices: 7.28 us -> none  [body(): parts = lax.all_to_all(joined, ('zl', 'zh'), 0, 0, tiled=True)]
    all_to_all x1 -> x0, waiting for transfers between devices: 6.78 us -> none  [body(): parts = lax.all_to_all(joined, ('zl', 'zh'), 0, 0, tiled=True)]
    ppermute x1 -> x0, waiting for transfers between devices: 5.27 us -> none  [body(): across = lax.ppermute(signal, 'zh', [(i, (i + 2) % 4) for i in range(4)])]
    ppermute x9 -> x8, starting transfers between devices: 2.8 us -> 7.71 us  [up(): return lax.ppermute(v, axis, [(i, (i + 1) % 4) for i in range(4)])]
  transfers between devices with their start and end apart: 25 -> 20, of which waited for: 11 -> 9; matrix products, arithmetic and copies ran while one was open for 7% -> 7% of each run, Pallas kernels for 0% -> 0%
where the time goes in v2:
time: 116 us
  blocking collectives  39.2 us (34%)
  starting transfers between devices  33 us (28%)
  waiting for transfers between devices  23.1 us (20%)
  local copies, waits for them, and re-layouts  9.65 us (8%)
  Pallas kernels  5.99 us (5%)
  other arithmetic  2.92 us (3%)
  between operations  1.48 us (1%)
    all_to_all x1, blocking collectives, body(): lax.all_to_all(potential.reshape(MEM * 4, 2, 128), TGT + ('zh',), 0, 0, t...  24.1 us
    all_to_all x1, blocking collectives, body(): parts = lax.all_to_all(joined, ('zl', 'zh'), 0, 0, tiled=True)  15.2 us
    ppermute x8, starting transfers between devices, down(): return lax.ppermute(v, axis, [(i, (i + 3) % 4) for i in range(4)])  14.6 us
    ppermute x8, waiting for transfers between devices, down(): return lax.ppermute(v, axis, [(i, (i + 3) % 4) for i in range(4)])  14.1 us
    ppermute x4, starting transfers between devices, swap(): return lax.ppermute(v, axis, [(0, 1), (1, 0)])  10.7 us
    ppermute x8, starting transfers between devices, up(): return lax.ppermute(v, axis, [(i, (i + 1) % 4) for i in range(4)])  7.71 us
    ppermute x8, waiting for transfers between devices, up(): return lax.ppermute(v, axis, [(i, (i + 1) % 4) for i in range(4)])  5.68 us
    pallas_call x1, Pallas kernels, body(): pl.pallas_call(coupling_kernel, out_shape=(jax.ShapeDtypeStruct((8, 16, S...  5.47 us
  transfers between devices with their start and end apart: 20, of which 9 were waited for; matrix products, arithmetic and copies ran while one was open for 7% of the time, Pallas kernels for 0%

profile of v2, /device:TPU:1, one launch (start us, length us, event | category | flops | bytes accessed | tf_op | source)
XLA Modules:
  0.0 115.6 jit_solution(518004042712422029)
XLA Ops:
  0.7 0.9 constant_dynamic-slice_fusion
  1.5 1.1 constant_dynamic-slice_fusion.3
  2.6 2.1 %collective-permute-start.3 = (bf16[1,32,3712]{2,1,0:T(8,128)(2,1)S(1)}, bf16[1,32,3712]{2,1,0:T(8,128)(2,1)S(1)}, u32[]{:S(2)}, u32[]{:S(2)}) collective-permute-start(bf16[1,32,3712]{2,1,0:T(8,128)(2,1)S(1)} %get-tuple-element.30), channel_id=1, source_target_pairs={{0,16},{16,32},{32,48},{48,0},{1,17},{17,33},{33,49},{49,1},{2,18}... | collective-permute-start | bytes 712712 | tf_op jit(solution)/shard_map/ppermute | solution.py:33
  4.8 1.4 %collective-permute-start.4 = (bf16[1,32,3712]{2,1,0:T(8,128)(2,1)S(1)}, bf16[1,32,3712]{2,1,0:T(8,128)(2,1)S(1)}, u32[]{:S(2)}, u32[]{:S(2)}) collective-permute-start(bf16[1,32,3712]{2,1,0:T(8,128)(2,1)S(1)} %get-tuple-element.30), channel_id=1, source_target_pairs={{0,48},{16,0},{32,16},{48,32},{1,49},{17,1},{33,17},{49,33},{2,50}... | collective-permute-start | bytes 712712 | tf_op jit(solution)/shard_map/ppermute | solution.py:37
  6.1 1.7 %collective-permute-start = (bf16[1,32,3712]{2,1,0:T(8,128)(2,1)S(1)}, bf16[1,32,3712]{2,1,0:T(8,128)(2,1)S(1)}, u32[]{:S(2)}, u32[]{:S(2)}) collective-permute-start(bf16[1,32,3712]{2,1,0:T(8,128)(2,1)S(1)} %get-tuple-element.31), channel_id=1, source_target_pairs={{0,8},{8,0},{1,9},{9,1},{2,10},{10,2},{3,11},{11,3},{4,12},{12,4},... | collective-permute-start | bytes 712712 | tf_op jit(solution)/shard_map/ppermute | solution.py:41
  7.9 1.1 constant_dynamic-slice_fusion.2
  9.6 2.1 %collective-permute-done = bf16[1,32,3712]{2,1,0:T(8,128)(2,1)S(1)} collective-permute-done((bf16[1,32,3712]{2,1,0:T(8,128)(2,1)S(1)}, bf16[1,32,3712]{2,1,0:T(8,128)(2,1)S(1)}, u32[]{:S(2)}, u32[]{:S(2)}) %collective-permute-start) | collective-permute-done | bytes 237600 | tf_op jit(solution)/shard_map/ppermute | solution.py:41
  11.7 2.2 %collective-permute-start.1 = (bf16[1,32,3712]{2,1,0:T(8,128)(2,1)S(1)}, bf16[1,32,3712]{2,1,0:T(8,128)(2,1)S(1)}, u32[]{:S(2)}, u32[]{:S(2)}) collective-permute-start(bf16[1,32,3712]{2,1,0:T(8,128)(2,1)S(1)} %collective-permute-done), channel_id=1, source_target_pairs={{0,64},{64,128},{128,192},{192,0},{1,65},{65,129},{129,193},{193,1... | collective-permute-start | bytes 712712 | tf_op jit(solution)/shard_map/ppermute | solution.py:33
  13.9 1.4 %collective-permute-start.11 = (bf16[1,32,3712]{2,1,0:T(8,128)(2,1)S(1)}, bf16[1,32,3712]{2,1,0:T(8,128)(2,1)S(1)}, u32[]{:S(2)}, u32[]{:S(2)}) collective-permute-start(bf16[1,32,3712]{2,1,0:T(8,128)(2,1)S(1)} %collective-permute-done), channel_id=1, source_target_pairs={{0,192},{64,0},{128,64},{192,128},{1,193},{65,1},{129,65},{193,129... | collective-permute-start | bytes 712712 | tf_op jit(solution)/shard_map/ppermute | solution.py:37
  15.5 2.7 %collective-permute-start.6 = (bf16[1,16,3712]{2,1,0:T(8,128)(2,1)S(1)}, bf16[1,16,3712]{2,1,0:T(8,128)(2,1)S(1)}, u32[]{:S(2)}, u32[]{:S(2)}) collective-permute-start(bf16[1,16,3712]{2,1,0:T(8,128)(2,1)S(1)} %slice.48), channel_id=1, source_target_pairs={{0,48},{16,0},{32,16},{48,32},{1,49},{17,1},{33,17},{49,33},{2,50}... | collective-permute-start | bytes 356360 | tf_op jit(solution)/shard_map/ppermute | solution.py:37
  19.3 2.4 %collective-permute-start.13 = (bf16[1,16,3712]{2,1,0:T(8,128)(2,1)S(1)}, bf16[1,16,3712]{2,1,0:T(8,128)(2,1)S(1)}, u32[]{:S(2)}, u32[]{:S(2)}) collective-permute-start(bf16[1,16,3712]{2,1,0:T(8,128)(2,1)S(1)} %slice.52), channel_id=1, source_target_pairs={{0,192},{64,0},{128,64},{192,128},{1,193},{65,1},{129,65},{193,129... | collective-permute-start | bytes 356360 | tf_op jit(solution)/shard_map/ppermute | solution.py:37
  22.5 0.9 collective-permute-start.7
  24.4 2.6 %collective-permute-start.15 = (bf16[4,32,3712]{2,1,0:T(8,128)(2,1)S(1)}, bf16[4,32,3712]{2,1,0:T(8,128)(2,1)}, u32[]{:S(2)}, u32[]{:S(2)}) collective-permute-start(bf16[4,32,3712]{2,1,0:T(8,128)(2,1)S(1)} %maximum_maximum_fusion.1.refs_5_), channel_id=1, source_target_pairs={{0,48},{16,0},{32,16},{48,32},{1,49},{17,1},{33,17},{49,33},{2,50}... | collective-permute-start | bytes 2850824 | tf_op jit(solution)/shard_map/ppermute | solution.py:37
  27.0 1.1 pad_maximum_fusion
  28.1 1.0 collective-permute-start.2
  29.3 13.4 %collective-permute-done.8.refs_2_ = bf16[4,32,3712]{2,1,0:T(8,128)(2,1)} collective-permute-done((bf16[4,32,3712]{2,1,0:T(8,128)(2,1)S(1)}, bf16[4,32,3712]{2,1,0:T(8,128)(2,1)}, u32[]{:S(2)}, u32[]{:S(2)}) %collective-permute-start.8) | collective-permute-done | bytes 950304 | tf_op jit(solution)/shard_map/ppermute | solution.py:37
  42.7 1.1 slice.50
  43.8 1.4 %collective-permute-start.10 = (bf16[2,32,3712]{2,1,0:T(8,128)(2,1)S(1)}, bf16[2,32,3712]{2,1,0:T(8,128)(2,1)S(1)}, u32[]{:S(2)}, u32[]{:S(2)}) collective-permute-start(bf16[2,32,3712]{2,1,0:T(8,128)(2,1)S(1)} %slice.50), channel_id=1, source_target_pairs={{0,192},{64,0},{128,64},{192,128},{1,193},{65,1},{129,65},{193,129... | collective-permute-start | bytes 1425416 | tf_op jit(solution)/shard_map/ppermute | solution.py:37
  45.2 1.1 slice.49
  46.7 1.1 slice.53
  47.7 1.4 %collective-permute-start.16 = (bf16[2,32,3712]{2,1,0:T(8,128)(2,1)S(1)}, bf16[2,32,3712]{2,1,0:T(8,128)(2,1)S(1)}, u32[]{:S(2)}, u32[]{:S(2)}) collective-permute-start(bf16[2,32,3712]{2,1,0:T(8,128)(2,1)S(1)} %slice.53), channel_id=1, source_target_pairs={{0,16},{16,32},{32,48},{48,0},{1,17},{17,33},{33,49},{49,1},{2,18}... | collective-permute-start | bytes 1425416 | tf_op jit(solution)/shard_map/ppermute | solution.py:33
  49.1 1.1 slice.54
  50.2 2.0 %collective-permute-start.17 = (bf16[2,32,3712]{2,1,0:T(8,128)(2,1)S(1)}, bf16[2,32,3712]{2,1,0:T(8,128)(2,1)S(1)}, u32[]{:S(2)}, u32[]{:S(2)}) collective-permute-start(bf16[2,32,3712]{2,1,0:T(8,128)(2,1)S(1)} %slice.54), channel_id=1, source_target_pairs={{0,48},{16,0},{32,16},{48,32},{1,49},{17,1},{33,17},{49,33},{2,50}... | collective-permute-start | bytes 1425416 | tf_op jit(solution)/shard_map/ppermute | solution.py:37
  53.1 2.1 %collective-permute-done.9.refs_3_ = bf16[2,32,3712]{2,1,0:T(8,128)(2,1)S(1)} collective-permute-done((bf16[2,32,3712]{2,1,0:T(8,128)(2,1)S(1)}, bf16[2,32,3712]{2,1,0:T(8,128)(2,1)S(1)}, u32[]{:S(2)}, u32[]{:S(2)}) %collective-permute-start.9) | collective-permute-done | bytes 475168 | tf_op jit(solution)/shard_map/ppermute | solution.py:33
  55.2 2.2 %collective-permute-done.16.refs_8_ = bf16[2,32,3712]{2,1,0:T(8,128)(2,1)S(1)} collective-permute-done((bf16[2,32,3712]{2,1,0:T(8,128)(2,1)S(1)}, bf16[2,32,3712]{2,1,0:T(8,128)(2,1)S(1)}, u32[]{:S(2)}, u32[]{:S(2)}) %collective-permute-start.16) | collective-permute-done | bytes 475168 | tf_op jit(solution)/shard_map/ppermute | solution.py:33
  58.2 5.5 %coupling.1 = (f32[8,16,512]{2,1,0:T(8,128)S(1)}, f32[8,16,512]{2,1,0:T(8,128)S(1)}, bf16[2048,256]{1,0:T(8,128)(2,1)S(1)}) custom-call(s32[32]{0:T(128)S(1)} %pad_add_fusion.1.slots, s32[2,25]{1,0:T(2,128)S(1)} %pad_add_fusion.starts, s32[2]{0:T(128)S(1)} %pad_add_fusion.2.place, bf16[4,32,3712]{2,1,0:T(8,128)(2,1)S(1)} %maximum_maximum_fusion.refs_0_, ...), custom_call_target="tpu_custom_call" | custom-call | tf_op jit(solution)/shard_map/coupling/pallas_call | solution.py:178
  63.7 1.0 copy-done.1
  64.6 5.4 %collective-permute-start.18 = (f32[8,16,512]{2,1,0:T(8,128)S(1)}, f32[8,16,512]{2,1,0:T(8,128)S(1)}, u32[]{:S(2)}, u32[]{:S(2)}) collective-permute-start(f32[8,16,512]{2,1,0:T(8,128)S(1)} %get-tuple-element.13), channel_id=1, source_target_pairs={{0,1},{1,0},{2,3},{3,2},{4,5},{5,4},{6,7},{7,6},{8,9},{9,8},{10,11... | collective-permute-start | bytes 786440 | tf_op jit(solution)/shard_map/ppermute | solution.py:41
  70.1 1.1 collective-permute-done.18
  71.2 15.2 %all_to_all.10.parts = f32[8,16,512]{2,1,0:T(8,128)S(1)} all-to-all(f32[8,16,512]{2,1,0:T(8,128)S(1)} %add.115), channel_id=1, replica_groups=mesh['y'=4,'x'=4,'zl'=2,'zh'=4,'c'=2] {'zl','zh'}, dimensions={0} | all-to-all | bytes 524288 | tf_op jit(solution)/shard_map/all_to_all | solution.py:198
  86.9 24.1 %all_to_all.11 = bf16[128,2,128]{2,1,0:T(2,128)(2,1)S(1)} all-to-all(bf16[128,2,128]{2,1,0:T(2,128)(2,1)S(1)} %bitcast.22), channel_id=1, replica_groups=mesh['y'=4,'x'=4,'zl'=2,'zh'=4,'c'=2] {'y','x','zl','zh'}, dimensions={0} | all-to-all | bytes 131072 | tf_op jit(solution)/shard_map/all_to_all | solution.py:212
  111.6 2.6 %collective-permute-start.19 = (f32[16,256]{1,0:T(8,128)S(1)}, f32[16,256]{1,0:T(8,128)S(1)}, u32[]{:S(2)}, u32[]{:S(2)}) collective-permute-start(f32[16,256]{1,0:T(8,128)S(1)} %fusion.1), channel_id=1, source_target_pairs={{0,1},{1,0},{2,3},{3,2},{4,5},{5,4},{6,7},{7,6},{8,9},{9,8},{10,11... | collective-permute-start | bytes 49160 | tf_op jit(solution)/shard_map/ppermute | solution.py:41
  (62 shorter events, 7.9 us)
Async XLA Ops:
  0.6 69.4 %copy-start = (f32[6,32,128]{2,1,0:T(8,128)S(1)}, f32[6,32,128]{2,1,0:T(8,128)}, u32[]{:S(2)}) copy-start(f32[6,32,128]{2,1,0:T(8,128)} %param.13) | copy-start | bytes 294916
  0.7 7.2 %copy-start.5 = (bf16[128,6400]{1,0:T(8,128)(2,1)S(1)}, bf16[128,6400]{1,0:T(8,128)(2,1)}, u32[]{:S(2)}) copy-start(bf16[128,6400]{1,0:T(8,128)(2,1)} %param.8) | copy-start | bytes 4915204
  2.6 12.7 %collective-permute-start.3 = (bf16[1,32,3712]{2,1,0:T(8,128)(2,1)S(1)}, bf16[1,32,3712]{2,1,0:T(8,128)(2,1)S(1)}, u32[]{:S(2)}, u32[]{:S(2)}) collective-permute-start(bf16[1,32,3712]{2,1,0:T(8,128)(2,1)S(1)} %get-tuple-element.30), channel_id=1, source_target_pairs={{0,16},{16,32},{32,48},{48,0},{1,17},{17,33},{33,49},{49,1},{2,18}... | collective-permute-start | bytes 712712 | tf_op jit(solution)/shard_map/ppermute | solution.py:33
  4.8 10.7 %collective-permute-start.4 = (bf16[1,32,3712]{2,1,0:T(8,128)(2,1)S(1)}, bf16[1,32,3712]{2,1,0:T(8,128)(2,1)S(1)}, u32[]{:S(2)}, u32[]{:S(2)}) collective-permute-start(bf16[1,32,3712]{2,1,0:T(8,128)(2,1)S(1)} %get-tuple-element.30), channel_id=1, source_target_pairs={{0,48},{16,0},{32,16},{48,32},{1,49},{17,1},{33,17},{49,33},{2,50}... | collective-permute-start | bytes 712712 | tf_op jit(solution)/shard_map/ppermute | solution.py:37
  6.1 9.2 %copy-start.7 = (s32[1,50]{1,0:T(1,128)S(1)}, s32[1,50]{1,0:T(1,128)}, u32[]{:S(2)}) copy-start(s32[1,50]{1,0:T(1,128)} %param.10) | copy-start | bytes 604
  6.1 5.6 %collective-permute-start = (bf16[1,32,3712]{2,1,0:T(8,128)(2,1)S(1)}, bf16[1,32,3712]{2,1,0:T(8,128)(2,1)S(1)}, u32[]{:S(2)}, u32[]{:S(2)}) collective-permute-start(bf16[1,32,3712]{2,1,0:T(8,128)(2,1)S(1)} %get-tuple-element.31), channel_id=1, source_target_pairs={{0,8},{8,0},{1,9},{9,1},{2,10},{10,2},{3,11},{11,3},{4,12},{12,4},... | collective-permute-start | bytes 712712 | tf_op jit(solution)/shard_map/ppermute | solution.py:41
  11.7 7.1 %collective-permute-start.1 = (bf16[1,32,3712]{2,1,0:T(8,128)(2,1)S(1)}, bf16[1,32,3712]{2,1,0:T(8,128)(2,1)S(1)}, u32[]{:S(2)}, u32[]{:S(2)}) collective-permute-start(bf16[1,32,3712]{2,1,0:T(8,128)(2,1)S(1)} %collective-permute-done), channel_id=1, source_target_pairs={{0,64},{64,128},{128,192},{192,0},{1,65},{65,129},{129,193},{193,1... | collective-permute-start | bytes 712712 | tf_op jit(solution)/shard_map/ppermute | solution.py:33
  13.9 5.4 %collective-permute-start.11 = (bf16[1,32,3712]{2,1,0:T(8,128)(2,1)S(1)}, bf16[1,32,3712]{2,1,0:T(8,128)(2,1)S(1)}, u32[]{:S(2)}, u32[]{:S(2)}) collective-permute-start(bf16[1,32,3712]{2,1,0:T(8,128)(2,1)S(1)} %collective-permute-done), channel_id=1, source_target_pairs={{0,192},{64,0},{128,64},{192,128},{1,193},{65,1},{129,65},{193,129... | collective-permute-start | bytes 712712 | tf_op jit(solution)/shard_map/ppermute | solution.py:37
  15.4 6.3 %collective-permute-start.5 = (bf16[1,16,3712]{2,1,0:T(8,128)(2,1)S(1)}, bf16[1,16,3712]{2,1,0:T(8,128)(2,1)S(1)}, u32[]{:S(2)}, u32[]{:S(2)}) collective-permute-start(bf16[1,16,3712]{2,1,0:T(8,128)(2,1)S(1)} %slice.47), channel_id=1, source_target_pairs={{0,16},{16,32},{32,48},{48,0},{1,17},{17,33},{33,49},{49,1},{2,18}... | collective-permute-start | bytes 356360 | tf_op jit(solution)/shard_map/ppermute | solution.py:33
  15.5 6.2 %collective-permute-start.6 = (bf16[1,16,3712]{2,1,0:T(8,128)(2,1)S(1)}, bf16[1,16,3712]{2,1,0:T(8,128)(2,1)S(1)}, u32[]{:S(2)}, u32[]{:S(2)}) collective-permute-start(bf16[1,16,3712]{2,1,0:T(8,128)(2,1)S(1)} %slice.48), channel_id=1, source_target_pairs={{0,48},{16,0},{32,16},{48,32},{1,49},{17,1},{33,17},{49,33},{2,50}... | collective-permute-start | bytes 356360 | tf_op jit(solution)/shard_map/ppermute | solution.py:37
  18.9 5.3 %collective-permute-start.12 = (bf16[1,16,3712]{2,1,0:T(8,128)(2,1)S(1)}, bf16[1,16,3712]{2,1,0:T(8,128)(2,1)S(1)}, u32[]{:S(2)}, u32[]{:S(2)}) collective-permute-start(bf16[1,16,3712]{2,1,0:T(8,128)(2,1)S(1)} %slice.51), channel_id=1, source_target_pairs={{0,64},{64,128},{128,192},{192,0},{1,65},{65,129},{129,193},{193,1... | collective-permute-start | bytes 356360 | tf_op jit(solution)/shard_map/ppermute | solution.py:33
  19.3 7.7 %copy-start.4 = (bf16[128,3200]{1,0:T(8,128)(2,1)S(1)}, bf16[128,3200]{1,0:T(8,128)(2,1)}, u32[]{:S(2)}) copy-start(bf16[128,3200]{1,0:T(8,128)(2,1)} %get-tuple-element.25) | copy-start | bytes 2457604
  19.3 4.8 %collective-permute-start.13 = (bf16[1,16,3712]{2,1,0:T(8,128)(2,1)S(1)}, bf16[1,16,3712]{2,1,0:T(8,128)(2,1)S(1)}, u32[]{:S(2)}, u32[]{:S(2)}) collective-permute-start(bf16[1,16,3712]{2,1,0:T(8,128)(2,1)S(1)} %slice.52), channel_id=1, source_target_pairs={{0,192},{64,0},{128,64},{192,128},{1,193},{65,1},{129,65},{193,129... | collective-permute-start | bytes 356360 | tf_op jit(solution)/shard_map/ppermute | solution.py:37
  21.8 7.3 %copy-start.6 = (s32[4]{0:T(128)S(1)}, s32[4]{0:T(128)}, u32[]{:S(2)}) copy-start(s32[4]{0:T(128)} %constant.54.clone) | copy-start | bytes 52
  21.8 20.9 %collective-permute-start.8 = (bf16[4,32,3712]{2,1,0:T(8,128)(2,1)S(1)}, bf16[4,32,3712]{2,1,0:T(8,128)(2,1)}, u32[]{:S(2)}, u32[]{:S(2)}) collective-permute-start(bf16[4,32,3712]{2,1,0:T(8,128)(2,1)S(1)} %maximum_maximum_fusion.refs_0_), channel_id=1, source_target_pairs={{0,192},{64,0},{128,64},{192,128},{1,193},{65,1},{129,65},{193,129... | collective-permute-start | bytes 2850824 | tf_op jit(solution)/shard_map/ppermute | solution.py:37
  22.5 22.7 %collective-permute-start.7 = (bf16[4,32,3712]{2,1,0:T(8,128)(2,1)S(1)}, bf16[4,32,3712]{2,1,0:T(8,128)(2,1)}, u32[]{:S(2)}, u32[]{:S(2)}) collective-permute-start(bf16[4,32,3712]{2,1,0:T(8,128)(2,1)S(1)} %maximum_maximum_fusion.refs_0_), channel_id=1, source_target_pairs={{0,64},{64,128},{128,192},{192,0},{1,65},{65,129},{129,193},{193,1... | collective-permute-start | bytes 2850824 | tf_op jit(solution)/shard_map/ppermute | solution.py:33
  24.2 22.4 %collective-permute-start.14 = (bf16[4,32,3712]{2,1,0:T(8,128)(2,1)S(1)}, bf16[4,32,3712]{2,1,0:T(8,128)(2,1)}, u32[]{:S(2)}, u32[]{:S(2)}) collective-permute-start(bf16[4,32,3712]{2,1,0:T(8,128)(2,1)S(1)} %maximum_maximum_fusion.1.refs_5_), channel_id=1, source_target_pairs={{0,16},{16,32},{32,48},{48,0},{1,17},{17,33},{33,49},{49,1},{2,18}... | collective-permute-start | bytes 2850824 | tf_op jit(solution)/shard_map/ppermute | solution.py:33
  24.4 24.7 %collective-permute-start.15 = (bf16[4,32,3712]{2,1,0:T(8,128)(2,1)S(1)}, bf16[4,32,3712]{2,1,0:T(8,128)(2,1)}, u32[]{:S(2)}, u32[]{:S(2)}) collective-permute-start(bf16[4,32,3712]{2,1,0:T(8,128)(2,1)S(1)} %maximum_maximum_fusion.1.refs_5_), channel_id=1, source_target_pairs={{0,48},{16,0},{32,16},{48,32},{1,49},{17,1},{33,17},{49,33},{2,50}... | collective-permute-start | bytes 2850824 | tf_op jit(solution)/shard_map/ppermute | solution.py:37
  28.1 24.3 %collective-permute-start.2 = (bf16[128,3328]{1,0:T(8,128)(2,1)}, bf16[128,3328]{1,0:T(8,128)(2,1)}, u32[]{:S(2)}, u32[]{:S(2)}) collective-permute-start(bf16[128,3328]{1,0:T(8,128)(2,1)} %pad_maximum_fusion), channel_id=1, source_target_pairs={{0,8},{8,0},{1,9},{9,1},{2,10},{10,2},{3,11},{11,3},{4,12},{12,4},... | collective-permute-start | bytes 2555912 | tf_op jit(solution)/shard_map/ppermute | solution.py:41
  43.8 9.3 %collective-permute-start.10 = (bf16[2,32,3712]{2,1,0:T(8,128)(2,1)S(1)}, bf16[2,32,3712]{2,1,0:T(8,128)(2,1)S(1)}, u32[]{:S(2)}, u32[]{:S(2)}) collective-permute-start(bf16[2,32,3712]{2,1,0:T(8,128)(2,1)S(1)} %slice.50), channel_id=1, source_target_pairs={{0,192},{64,0},{128,64},{192,128},{1,193},{65,1},{129,65},{193,129... | collective-permute-start | bytes 1425416 | tf_op jit(solution)/shard_map/ppermute | solution.py:37
  46.3 9.0 %collective-permute-start.9 = (bf16[2,32,3712]{2,1,0:T(8,128)(2,1)S(1)}, bf16[2,32,3712]{2,1,0:T(8,128)(2,1)S(1)}, u32[]{:S(2)}, u32[]{:S(2)}) collective-permute-start(bf16[2,32,3712]{2,1,0:T(8,128)(2,1)S(1)} %slice.49), channel_id=1, source_target_pairs={{0,64},{64,128},{128,192},{192,0},{1,65},{65,129},{129,193},{193,1... | collective-permute-start | bytes 1425416 | tf_op jit(solution)/shard_map/ppermute | solution.py:33
  47.7 9.7 %collective-permute-start.16 = (bf16[2,32,3712]{2,1,0:T(8,128)(2,1)S(1)}, bf16[2,32,3712]{2,1,0:T(8,128)(2,1)S(1)}, u32[]{:S(2)}, u32[]{:S(2)}) collective-permute-start(bf16[2,32,3712]{2,1,0:T(8,128)(2,1)S(1)} %slice.53), channel_id=1, source_target_pairs={{0,16},{16,32},{32,48},{48,0},{1,17},{17,33},{33,49},{49,1},{2,18}... | collective-permute-start | bytes 1425416 | tf_op jit(solution)/shard_map/ppermute | solution.py:33
  50.2 8.0 %collective-permute-start.17 = (bf16[2,32,3712]{2,1,0:T(8,128)(2,1)S(1)}, bf16[2,32,3712]{2,1,0:T(8,128)(2,1)S(1)}, u32[]{:S(2)}, u32[]{:S(2)}) collective-permute-start(bf16[2,32,3712]{2,1,0:T(8,128)(2,1)S(1)} %slice.54), channel_id=1, source_target_pairs={{0,48},{16,0},{32,16},{48,32},{1,49},{17,1},{33,17},{49,33},{2,50}... | collective-permute-start | bytes 1425416 | tf_op jit(solution)/shard_map/ppermute | solution.py:37
  58.2 28.2 %copy-start.3 = (f32[32]{0:T(128)S(1)}, f32[32]{0:T(128)}, u32[]{:S(2)}) copy-start(f32[32]{0:T(128)} %param.12) | copy-start | bytes 388
  63.7 1.0 copy-start.1
  64.6 46.7 %copy-start.2 = (bf16[2048,256]{1,0:T(8,128)(2,1)S(1)}, bf16[2048,256]{1,0:T(8,128)(2,1)}, u32[]{:S(2)}) copy-start(bf16[2048,256]{1,0:T(8,128)(2,1)} %copy-done.1) | copy-start | bytes 3145732
  64.6 6.6 %collective-permute-start.18 = (f32[8,16,512]{2,1,0:T(8,128)S(1)}, f32[8,16,512]{2,1,0:T(8,128)S(1)}, u32[]{:S(2)}, u32[]{:S(2)}) collective-permute-start(f32[8,16,512]{2,1,0:T(8,128)S(1)} %get-tuple-element.13), channel_id=1, source_target_pairs={{0,1},{1,0},{2,3},{3,2},{4,5},{5,4},{6,7},{7,6},{8,9},{9,8},{10,11... | collective-permute-start | bytes 786440 | tf_op jit(solution)/shard_map/ppermute | solution.py:41
  111.6 3.4 %collective-permute-start.19 = (f32[16,256]{1,0:T(8,128)S(1)}, f32[16,256]{1,0:T(8,128)S(1)}, u32[]{:S(2)}, u32[]{:S(2)}) collective-permute-start(f32[16,256]{1,0:T(8,128)S(1)} %fusion.1), channel_id=1, source_target_pairs={{0,1},{1,0},{2,3},{3,2},{4,5},{5,4},{6,7},{7,6},{8,9},{9,8},{10,11... | collective-permute-start | bytes 49160 | tf_op jit(solution)/shard_map/ppermute | solution.py:41

commit v3 on v2

--- a/solution.py
+++ b/solution.py
@@ -1,5 +1,6 @@
 import jax
 import jax.numpy as jnp
+import numpy as np
 from jax import lax
 from jax.experimental import pallas as pl
 from jax.experimental.pallas import tpu as pltpu
@@ -29,6 +30,12 @@
 midpoint = 6.0
 
 
+OUTER, INNER = np.repeat(OFFSETS, 4), np.tile(OFFSETS, 4)
+PLACE_Y = np.concatenate([OUTER, INNER]).astype(np.int32)
+PLACE_X = np.concatenate([INNER, OUTER]).astype(np.int32)
+PLACE_Z = np.repeat(np.arange(2), 16).astype(np.int32)
+
+
 def up(v, axis):
     return lax.ppermute(v, axis, [(i, (i + 1) % 4) for i in range(4)])
 
@@ -37,12 +44,22 @@
     return lax.ppermute(v, axis, [(i, (i + 3) % 4) for i in range(4)])
 
 
+def cut(v, at, size, axis):
+    begin = [0] * v.ndim
+    begin[axis] = at
+    sizes = list(v.shape)
+    sizes[axis] = size
+    return lax.dynamic_slice(v, begin, sizes, allow_negative_indices=False)
+
+
 def swap(v, axis):
     return lax.ppermute(v, axis, [(0, 1), (1, 0)])
 
 
-def ring_gather(piece, first, second):
+def ring_gather(piece, first, second, mark=None):
     left, right = up(piece, first), down(piece, first)
+    if mark is not None:
+        left, right, _ = lax.optimization_barrier((left, right, mark))
     low, high = up(left[:, :16], first), down(right[:, 16:], first)
     row = jnp.concatenate([piece, left, right, jnp.concatenate([low, high], axis=1)], axis=0)
     row_left, row_right = up(row, second), down(row, second)
@@ -53,7 +70,7 @@
 def coupling_kernel(slots, starts, place, *refs):
     pieces = refs[:10]
     tiles = refs[10:12]
-    keep, send, lead, ordered, total = refs[12:]
+    keep, send, lead_out, ordered, total, lead, done = refs[12:]
     at = 0
     for ref in pieces:
         for i in range(ref.shape[0]):
@@ -69,6 +86,8 @@
             lead[pl.ds(tg, MEM), :] = ref[i, :, HALF:HALF + SENSORS]
             lead[pl.ds(tg + MEM, MEM), :] = ref[i, :, HALF + SENSORS:]
             at += 1
+    store = pltpu.make_async_copy(lead, lead_out, done)
+    store.start()
     zl = place[0]
     core = place[1]
     for h in range(2):
@@ -97,6 +116,7 @@
             other = pl.multiple_of(q * 32 + (1 - core) * 16, 16)
             keep[pl.ds(z * 4 + q, 1)] = total[pl.ds(mine, 16), :][None]
             send[pl.ds(z * 4 + q, 1)] = total[pl.ds(other, 16), :][None]
+    store.wait()
 
 
 def spike_rate(v):
@@ -123,7 +143,7 @@
         y3, y4, y5 = n3, n4, n5
         rows[pl.ds(t, 16, stride=STEPS), :] = y1 - y2
     for i, v in enumerate((y0, y1, y2, y3, y4, y5)):
-        final[i] = v.T
+        final[i] = v
     flat = rows[...].T.astype(jnp.bfloat16)
     for i in range(4):
         potential[:, i, 0, :] = flat[:, :128]
@@ -141,39 +161,43 @@
 def body(connectome, history, delays, cycle_head, outside_afferent, init_state, lead_field):
     y, x, zl = lax.axis_index("y"), lax.axis_index("x"), lax.axis_index("zl")
     zh, core = lax.axis_index("zh"), lax.axis_index("c")
-    part = zh * 2 + core
-    near, far = zl * HALF, (1 - zl) * HALF
-
-    lead_rows = lax.dynamic_index_in_dim(lead_field.reshape(4, 2, 16, SENSORS), core, 1, False)
-    lead_rows = lead_rows.reshape(2, 32, SENSORS)
+    near, far, part = zl * HALF, (1 - zl) * HALF, (zh * 2 + core) * 16
+    near_block, far_block, other_zl = zl * BLOCKS, (1 - zl) * BLOCKS, 1 - zl
+    (
+        history, connectome, lead_field, delays, init_state,
+        y, x, zl, core, near, far, part, near_block, far_block, other_zl,
+    ) = lax.optimization_barrier(
+        (
+            history, connectome, lead_field, delays, init_state,
+            y, x, zl, core, near, far, part, near_block, far_block, other_zl,
+        )
+    )
+
+    lead_rows = cut(lead_field.reshape(4, 2, 16, SENSORS), core, 1, 1).reshape(2, 32, SENSORS)
     extra = jnp.concatenate([lead_rows[0], lead_rows[1]], axis=1)[None]
-
-    partner = swap(jnp.concatenate([lax.dynamic_slice_in_dim(history, far, HALF, 2), extra], axis=2), "zl")
-    own = jnp.concatenate([lax.dynamic_slice_in_dim(history, near, HALF, 2), extra], axis=2)
+    sent = jnp.concatenate([cut(history, far, HALF, 2), extra], axis=2)
+    history, sent = lax.optimization_barrier((history, sent))
+    partner = swap(sent, "zl")
+    own = jnp.concatenate([cut(history, near, HALF, 2), extra], axis=2)
+
+    slots = ((y + PLACE_Y) & 3) * 8 + ((x + PLACE_X) & 3) * 2 + (zl ^ PLACE_Z)
+    place = jnp.stack([zl, core])
     start = (cycle_head[0] - delays) & (SLOTS - 1)
-    start_own = lax.dynamic_slice_in_dim(start, zl * BLOCKS, BLOCKS, 1)
-    start_far = lax.dynamic_slice_in_dim(start, (1 - zl) * BLOCKS, BLOCKS, 1)
-    tile_own = lax.dynamic_slice_in_dim(connectome, near, HALF, 1)
-    tile_far = lax.dynamic_slice_in_dim(connectome, far, HALF, 1)
+    start_own = cut(start, near_block, BLOCKS, 1)
+    start_far = cut(start, far_block, BLOCKS, 1)
     note = jnp.pad(start_far.astype(jnp.bfloat16), ((0, 0), (0, BLOCK - BLOCKS)))
+    begin = cut(init_state, part, 16, 2)
+    tile_own = cut(connectome, near, HALF, 1)
+    tile_far = cut(connectome, far, HALF, 1)
     tile_far = jnp.concatenate([tile_far, jnp.broadcast_to(note, (BLOCK, BLOCK))], axis=1)
 
-    own_pieces, _ = ring_gather(own, "x", "y")
+    own_pieces, _ = ring_gather(own, "x", "y", partner)
     other_pieces, early = ring_gather(partner, "y", "x")
     pieces = own_pieces + other_pieces
     tile_far, _ = lax.optimization_barrier((tile_far, early))
     tile_other = swap(tile_far, "zl")
     start_other = tile_other[:1, HALF:HALF + BLOCKS].astype(jnp.int32)
-    offsets = jnp.array(OFFSETS, jnp.int32)
-    ys, xs = (y + offsets) & 3, (x + offsets) & 3
-    slots = jnp.concatenate(
-        [
-            (ys[:, None] * 8 + xs[None, :] * 2 + zl).reshape(-1),
-            (ys[None, :] * 8 + xs[:, None] * 2 + (1 - zl)).reshape(-1),
-        ]
-    )
     starts = jnp.concatenate([start_own, start_other], axis=0)
-    place = jnp.stack([zl, core])
 
     keep, send, lead = pl.pallas_call(
         coupling_kernel,
@@ -183,23 +207,24 @@
             jax.ShapeDtypeStruct((SLOTS * 64, SENSORS), jnp.bfloat16),
         ),
         in_specs=smem(3) + vmem(12),
-        out_specs=tuple(vmem(3)),
+        out_specs=(*vmem(2), pl.BlockSpec(memory_space=pl.ANY)),
         scratch_shapes=[
             pltpu.VMEM(((SLOTS + STEPS) * MEM, HALF), jnp.bfloat16),
             pltpu.VMEM((BLOCK, STEPS * MEM), jnp.float32),
+            pltpu.VMEM((SLOTS * 64, SENSORS), jnp.bfloat16),
+            pltpu.SemaphoreType.DMA,
         ],
         compiler_params=pltpu.CompilerParams(vmem_limit_bytes=24 << 20),
         name="coupling",
     )(slots, starts, place, *pieces, tile_own, tile_other)
 
     joined = keep + swap(send, "c")
-    begin = lax.dynamic_slice_in_dim(init_state, part * 16, 16, 2)
     joined, begin, outside = lax.optimization_barrier((joined, begin, outside_afferent[None, :]))
     parts = lax.all_to_all(joined, ("zl", "zh"), 0, 0, tiled=True)
-    final_state, potential = pl.pallas_call(
+    final, potential = pl.pallas_call(
         integrate_kernel,
         out_shape=(
-            jax.ShapeDtypeStruct((6, MEM, 16), jnp.float32),
+            jax.ShapeDtypeStruct((6, 16, MEM), jnp.float32),
             jax.ShapeDtypeStruct((MEM, 4, 2, 128), jnp.bfloat16),
         ),
         in_specs=vmem(3),
@@ -214,7 +239,7 @@
         got.reshape(SLOTS * 64, STEPS), lead, (((0,), (0,)), ((), ())), preferred_element_type=jnp.float32
     )
     signal = signal + swap(signal, "c")
-    return signal[None], final_state
+    return signal[None], jnp.transpose(final, (0, 2, 1))
 
 
 def solution(mesh):

time: 116 us -> 109 us (0.940)
  local copies, waits for them, and re-layouts: 9.65 us -> 2.52 us
  waiting for transfers between devices: 23.1 us -> 26.6 us
  other arithmetic: 2.92 us -> 1.17 us
  Pallas kernels: 5.99 us -> 4.78 us
    slice x4, local copies, waits for them, and re-layouts: 4.23 us -> 0.13 us  [ring_gather(): far_low, far_high = (up(row_left[:2], second), down(row_right[2:], second))]
    ppermute x8, waiting for transfers between devices: 14.1 us -> 18.1 us  [down(): return lax.ppermute(v, axis, [(i, (i + 3) % 4) for i in range(4)])]
    ppermute x8, waiting for transfers between devices: 5.68 us -> 4 us  [up(): return lax.ppermute(v, axis, [(i, (i + 1) % 4) for i in range(4)])]
    pallas_call x1, Pallas kernels: 5.47 us -> 3.82 us  [body(): pl.pallas_call(coupling_kernel, out_shape=(jax.ShapeDtypeStruct((8, 16, S...]
    unnamed x17 -> x16, local copies, waits for them, and re-layouts: 1.71 us -> 0.12 us
    dynamic_slice x3 -> x4, local copies, waits for them, and re-layouts: 2.26 us -> 0.97 us  [cut(): return lax.dynamic_slice(v, begin, sizes, allow_negative_indices=False)]
    ppermute x4, waiting for transfers between devices: 3.26 us -> 4.44 us  [swap(): return lax.ppermute(v, axis, [(0, 1), (1, 0)])]
  transfers between devices with their start and end apart: 20 -> 20, of which waited for: 9 -> 10; matrix products, arithmetic and copies ran while one was open for 7% -> 1% of each run, Pallas kernels for 0% -> 0%
where the time goes in v3:
time: 109 us
  blocking collectives  38.7 us (36%)
  starting transfers between devices  33.1 us (30%)
  waiting for transfers between devices  26.6 us (24%)
  Pallas kernels  4.78 us (4%)
  local copies, waits for them, and re-layouts  2.52 us (2%)
  between operations  1.54 us (1%)
  other arithmetic  1.17 us (1%)
    all_to_all x1, blocking collectives, body(): lax.all_to_all(potential.reshape(MEM * 4, 2, 128), TGT + ('zh',), 0, 0, t...  23.6 us
    ppermute x8, waiting for transfers between devices, down(): return lax.ppermute(v, axis, [(i, (i + 3) % 4) for i in range(4)])  18.1 us
    all_to_all x1, blocking collectives, body(): parts = lax.all_to_all(joined, ('zl', 'zh'), 0, 0, tiled=True)  15.1 us
    ppermute x8, starting transfers between devices, down(): return lax.ppermute(v, axis, [(i, (i + 3) % 4) for i in range(4)])  14.8 us
    ppermute x4, starting transfers between devices, swap(): return lax.ppermute(v, axis, [(0, 1), (1, 0)])  11.4 us
    ppermute x8, starting transfers between devices, up(): return lax.ppermute(v, axis, [(i, (i + 1) % 4) for i in range(4)])  6.88 us
    ppermute x4, waiting for transfers between devices, swap(): return lax.ppermute(v, axis, [(0, 1), (1, 0)])  4.44 us
    ppermute x8, waiting for transfers between devices, up(): return lax.ppermute(v, axis, [(i, (i + 1) % 4) for i in range(4)])  4 us
  transfers between devices with their start and end apart: 20, of which 10 were waited for; matrix products, arithmetic and copies ran while one was open for 1% of the time, Pallas kernels for 0%

profile of v3, /device:TPU:1, one launch (start us, length us, event | category | flops | bytes accessed | tf_op | source)
XLA Modules:
  0.0 108.7 jit_solution(12478244622346739919)
XLA Ops:
  0.7 0.9 constant_dynamic-slice_fusion
  2.0 2.1 %collective-permute-start.3 = (bf16[1,32,3712]{2,1,0:T(8,128)(2,1)S(1)}, bf16[1,32,3712]{2,1,0:T(8,128)(2,1)S(1)}, u32[]{:S(2)}, u32[]{:S(2)}) collective-permute-start(bf16[1,32,3712]{2,1,0:T(8,128)(2,1)S(1)} %pad_maximum_fusion.1), channel_id=1, source_target_pairs={{0,16},{16,32},{32,48},{48,0},{1,17},{17,33},{33,49},{49,1},{2,18}... | collective-permute-start | bytes 712712 | tf_op jit(solution)/shard_map/ppermute | solution.py:40
  4.1 1.4 %collective-permute-start.4 = (bf16[1,32,3712]{2,1,0:T(8,128)(2,1)S(1)}, bf16[1,32,3712]{2,1,0:T(8,128)(2,1)S(1)}, u32[]{:S(2)}, u32[]{:S(2)}) collective-permute-start(bf16[1,32,3712]{2,1,0:T(8,128)(2,1)S(1)} %pad_maximum_fusion.1), channel_id=1, source_target_pairs={{0,48},{16,0},{32,16},{48,32},{1,49},{17,1},{33,17},{49,33},{2,50}... | collective-permute-start | bytes 712712 | tf_op jit(solution)/shard_map/ppermute | solution.py:44
  5.4 1.7 %collective-permute-start = (bf16[1,32,3712]{2,1,0:T(8,128)(2,1)S(1)}, bf16[1,32,3712]{2,1,0:T(8,128)(2,1)S(1)}, u32[]{:S(2)}, u32[]{:S(2)}) collective-permute-start(bf16[1,32,3712]{2,1,0:T(8,128)(2,1)S(1)} %pad_maximum_fusion.2), channel_id=1, source_target_pairs={{0,8},{8,0},{1,9},{9,1},{2,10},{10,2},{3,11},{11,3},{4,12},{12,4},... | collective-permute-start | bytes 712712 | tf_op jit(solution)/shard_map/ppermute | solution.py:56
  7.2 0.6 constant_dynamic-slice_fusion.2
  8.5 2.5 %collective-permute-done = bf16[1,32,3712]{2,1,0:T(8,128)(2,1)S(1)} collective-permute-done((bf16[1,32,3712]{2,1,0:T(8,128)(2,1)S(1)}, bf16[1,32,3712]{2,1,0:T(8,128)(2,1)S(1)}, u32[]{:S(2)}, u32[]{:S(2)}) %collective-permute-start) | collective-permute-done | bytes 237600 | tf_op jit(solution)/shard_map/ppermute | solution.py:56
  11.0 2.2 %collective-permute-start.1 = (bf16[1,32,3712]{2,1,0:T(8,128)(2,1)S(1)}, bf16[1,32,3712]{2,1,0:T(8,128)(2,1)S(1)}, u32[]{:S(2)}, u32[]{:S(2)}) collective-permute-start(bf16[1,32,3712]{2,1,0:T(8,128)(2,1)S(1)} %collective-permute-done), channel_id=1, source_target_pairs={{0,64},{64,128},{128,192},{192,0},{1,65},{65,129},{129,193},{193,1... | collective-permute-start | bytes 712712 | tf_op jit(solution)/shard_map/ppermute | solution.py:40
  13.2 1.4 %collective-permute-start.11 = (bf16[1,32,3712]{2,1,0:T(8,128)(2,1)S(1)}, bf16[1,32,3712]{2,1,0:T(8,128)(2,1)S(1)}, u32[]{:S(2)}, u32[]{:S(2)}) collective-permute-start(bf16[1,32,3712]{2,1,0:T(8,128)(2,1)S(1)} %collective-permute-done), channel_id=1, source_target_pairs={{0,192},{64,0},{128,64},{192,128},{1,193},{65,1},{129,65},{193,129... | collective-permute-start | bytes 712712 | tf_op jit(solution)/shard_map/ppermute | solution.py:44
  14.8 2.7 %collective-permute-start.6 = (bf16[1,16,3712]{2,1,0:T(8,128)(2,1)S(1)}, bf16[1,16,3712]{2,1,0:T(8,128)(2,1)S(1)}, u32[]{:S(2)}, u32[]{:S(2)}) collective-permute-start(bf16[1,16,3712]{2,1,0:T(8,128)(2,1)S(1)} %slice.39), channel_id=1, source_target_pairs={{0,48},{16,0},{32,16},{48,32},{1,49},{17,1},{33,17},{49,33},{2,50}... | collective-permute-start | bytes 356360 | tf_op jit(solution)/shard_map/ppermute | solution.py:44
  17.7 0.5 collective-permute-done.1
  18.6 2.4 %collective-permute-start.13 = (bf16[1,16,3712]{2,1,0:T(8,128)(2,1)S(1)}, bf16[1,16,3712]{2,1,0:T(8,128)(2,1)S(1)}, u32[]{:S(2)}, u32[]{:S(2)}) collective-permute-start(bf16[1,16,3712]{2,1,0:T(8,128)(2,1)S(1)} %slice.50), channel_id=1, source_target_pairs={{0,192},{64,0},{128,64},{192,128},{1,193},{65,1},{129,65},{193,129... | collective-permute-start | bytes 356360 | tf_op jit(solution)/shard_map/ppermute | solution.py:44
  21.1 0.7 collective-permute-start.8
  21.8 0.9 collective-permute-start.7
  22.7 0.8 collective-permute-done.12
  23.7 2.6 %collective-permute-start.15 = (bf16[4,32,3712]{2,1,0:T(8,128)(2,1)S(1)}, bf16[4,32,3712]{2,1,0:T(8,128)(2,1)S(1)}, u32[]{:S(2)}, u32[]{:S(2)}) collective-permute-start(bf16[4,32,3712]{2,1,0:T(8,128)(2,1)S(1)} %maximum_maximum_fusion.1.refs_5_), channel_id=1, source_target_pairs={{0,48},{16,0},{32,16},{48,32},{1,49},{17,1},{33,17},{49,33},{2,50}... | collective-permute-start | bytes 2850824 | tf_op jit(solution)/shard_map/ppermute | solution.py:44
  26.4 1.1 collective-permute-start.2
  27.5 14.4 %collective-permute-done.8.refs_2_ = bf16[4,32,3712]{2,1,0:T(8,128)(2,1)S(1)} collective-permute-done((bf16[4,32,3712]{2,1,0:T(8,128)(2,1)S(1)}, bf16[4,32,3712]{2,1,0:T(8,128)(2,1)S(1)}, u32[]{:S(2)}, u32[]{:S(2)}) %collective-permute-start.8) | collective-permute-done | bytes 950304 | tf_op jit(solution)/shard_map/ppermute | solution.py:44
  42.0 1.6 %collective-permute-start.10 = (bf16[2,32,3712]{2,1,0:T(8,128)(2,1)S(1)}, bf16[2,32,3712]{2,1,0:T(8,128)(2,1)S(1)}, u32[]{:S(2)}, u32[]{:S(2)}) collective-permute-start(bf16[2,32,3712]{2,1,0:T(8,128)(2,1)S(1)} %slice.48), channel_id=1, source_target_pairs={{0,192},{64,0},{128,64},{192,128},{1,193},{65,1},{129,65},{193,129... | collective-permute-start | bytes 1425416 | tf_op jit(solution)/shard_map/ppermute | solution.py:44
  43.6 0.6 collective-permute-done.7.refs_1_
  44.4 0.9 collective-permute-start.16
  45.3 2.1 %collective-permute-start.17 = (bf16[2,32,3712]{2,1,0:T(8,128)(2,1)S(1)}, bf16[2,32,3712]{2,1,0:T(8,128)(2,1)S(1)}, u32[]{:S(2)}, u32[]{:S(2)}) collective-permute-start(bf16[2,32,3712]{2,1,0:T(8,128)(2,1)S(1)} %slice.52), channel_id=1, source_target_pairs={{0,48},{16,0},{32,16},{48,32},{1,49},{17,1},{33,17},{49,33},{2,50}... | collective-permute-start | bytes 1425416 | tf_op jit(solution)/shard_map/ppermute | solution.py:44
  47.6 3.7 %collective-permute-done.10.refs_4_ = bf16[2,32,3712]{2,1,0:T(8,128)(2,1)S(1)} collective-permute-done((bf16[2,32,3712]{2,1,0:T(8,128)(2,1)S(1)}, bf16[2,32,3712]{2,1,0:T(8,128)(2,1)S(1)}, u32[]{:S(2)}, u32[]{:S(2)}) %collective-permute-start.10) | collective-permute-done | bytes 475168 | tf_op jit(solution)/shard_map/ppermute | solution.py:44
  51.3 1.8 %collective-permute-done.9.refs_3_ = bf16[2,32,3712]{2,1,0:T(8,128)(2,1)S(1)} collective-permute-done((bf16[2,32,3712]{2,1,0:T(8,128)(2,1)S(1)}, bf16[2,32,3712]{2,1,0:T(8,128)(2,1)S(1)}, u32[]{:S(2)}, u32[]{:S(2)}) %collective-permute-start.9) | collective-permute-done | bytes 475168 | tf_op jit(solution)/shard_map/ppermute | solution.py:40
  53.3 3.8 %coupling.1 = (f32[8,16,512]{2,1,0:T(8,128)S(1)}, f32[8,16,512]{2,1,0:T(8,128)S(1)}, bf16[2048,256]{1,0:T(8,128)(2,1)S(1)}) custom-call(s32[32]{0:T(128)S(1)} %xor_add_fusion.slots, s32[2,25]{1,0:T(2,128)S(1)} %pad_add_fusion.starts, s32[2]{0:T(128)S(1)} %pad_add_fusion.1.place, bf16[4,32,3712]{2,1,0:T(8,128)(2,1)S(1)} %maximum_maximum_fusion.refs_0_, ...), custom_call_target="tpu_custom_call" | custom-call | tf_op jit(solution)/shard_map/coupling/pallas_call | solution.py:202
  57.2 6.0 %collective-permute-start.18 = (f32[8,16,512]{2,1,0:T(8,128)S(1)}, f32[8,16,512]{2,1,0:T(8,128)S(1)}, u32[]{:S(2)}, u32[]{:S(2)}) collective-permute-start(f32[8,16,512]{2,1,0:T(8,128)S(1)} %get-tuple-element.47), channel_id=1, source_target_pairs={{0,1},{1,0},{2,3},{3,2},{4,5},{5,4},{6,7},{7,6},{8,9},{9,8},{10,11... | collective-permute-start | bytes 786440 | tf_op jit(solution)/shard_map/ppermute | solution.py:56
  63.2 1.1 collective-permute-done.18
  64.4 15.1 %all_to_all.10.parts = f32[8,16,512]{2,1,0:T(8,128)S(1)} all-to-all(f32[8,16,512]{2,1,0:T(8,128)S(1)} %add.36), channel_id=1, replica_groups=mesh['y'=4,'x'=4,'zl'=2,'zh'=4,'c'=2] {'zl','zh'}, dimensions={0} | all-to-all | bytes 524288 | tf_op jit(solution)/shard_map/all_to_all | solution.py:223
  79.4 1.0 integrate.1
  80.4 23.6 %all_to_all.11 = bf16[128,2,128]{2,1,0:T(2,128)(2,1)S(1)} all-to-all(bf16[128,2,128]{2,1,0:T(2,128)(2,1)S(1)} %bitcast.23), channel_id=1, replica_groups=mesh['y'=4,'x'=4,'zl'=2,'zh'=4,'c'=2] {'y','x','zl','zh'}, dimensions={0} | all-to-all | bytes 131072 | tf_op jit(solution)/shard_map/all_to_all | solution.py:237
  104.6 2.6 %collective-permute-start.19 = (f32[16,256]{1,0:T(8,128)S(1)}, f32[16,256]{1,0:T(8,128)S(1)}, u32[]{:S(2)}, u32[]{:S(2)}) collective-permute-start(f32[16,256]{1,0:T(8,128)S(1)} %fusion.1), channel_id=1, source_target_pairs={{0,1},{1,0},{2,3},{3,2},{4,5},{5,4},{6,7},{7,6},{8,9},{9,8},{10,11... | collective-permute-start | bytes 49160 | tf_op jit(solution)/shard_map/ppermute | solution.py:56
  107.2 0.8 collective-permute-done.19
  108.0 0.6 add_bitcast_fusion
  (59 shorter events, 2.9 us)
Async XLA Ops:
  0.6 1.0 copy-start
  0.6 6.5 %copy-start.2 = (bf16[128,6400]{1,0:T(8,128)(2,1)S(1)}, bf16[128,6400]{1,0:T(8,128)(2,1)}, u32[]{:S(2)}) copy-start(bf16[128,6400]{1,0:T(8,128)(2,1)} %param.10) | copy-start | bytes 4915204
  2.0 12.7 %copy-start.7 = (s32[1,50]{1,0:T(1,128)S(1)}, s32[1,50]{1,0:T(1,128)}, u32[]{:S(2)}) copy-start(s32[1,50]{1,0:T(1,128)} %param.12) | copy-start | bytes 604
  2.0 12.7 %collective-permute-start.3 = (bf16[1,32,3712]{2,1,0:T(8,128)(2,1)S(1)}, bf16[1,32,3712]{2,1,0:T(8,128)(2,1)S(1)}, u32[]{:S(2)}, u32[]{:S(2)}) collective-permute-start(bf16[1,32,3712]{2,1,0:T(8,128)(2,1)S(1)} %pad_maximum_fusion.1), channel_id=1, source_target_pairs={{0,16},{16,32},{32,48},{48,0},{1,17},{17,33},{33,49},{49,1},{2,18}... | collective-permute-start | bytes 712712 | tf_op jit(solution)/shard_map/ppermute | solution.py:40
  4.1 10.6 %collective-permute-start.4 = (bf16[1,32,3712]{2,1,0:T(8,128)(2,1)S(1)}, bf16[1,32,3712]{2,1,0:T(8,128)(2,1)S(1)}, u32[]{:S(2)}, u32[]{:S(2)}) collective-permute-start(bf16[1,32,3712]{2,1,0:T(8,128)(2,1)S(1)} %pad_maximum_fusion.1), channel_id=1, source_target_pairs={{0,48},{16,0},{32,16},{48,32},{1,49},{17,1},{33,17},{49,33},{2,50}... | collective-permute-start | bytes 712712 | tf_op jit(solution)/shard_map/ppermute | solution.py:44
  5.4 5.6 %collective-permute-start = (bf16[1,32,3712]{2,1,0:T(8,128)(2,1)S(1)}, bf16[1,32,3712]{2,1,0:T(8,128)(2,1)S(1)}, u32[]{:S(2)}, u32[]{:S(2)}) collective-permute-start(bf16[1,32,3712]{2,1,0:T(8,128)(2,1)S(1)} %pad_maximum_fusion.2), channel_id=1, source_target_pairs={{0,8},{8,0},{1,9},{9,1},{2,10},{10,2},{3,11},{11,3},{4,12},{12,4},... | collective-permute-start | bytes 712712 | tf_op jit(solution)/shard_map/ppermute | solution.py:56
  11.0 7.1 %collective-permute-start.1 = (bf16[1,32,3712]{2,1,0:T(8,128)(2,1)S(1)}, bf16[1,32,3712]{2,1,0:T(8,128)(2,1)S(1)}, u32[]{:S(2)}, u32[]{:S(2)}) collective-permute-start(bf16[1,32,3712]{2,1,0:T(8,128)(2,1)S(1)} %collective-permute-done), channel_id=1, source_target_pairs={{0,64},{64,128},{128,192},{192,0},{1,65},{65,129},{129,193},{193,1... | collective-permute-start | bytes 712712 | tf_op jit(solution)/shard_map/ppermute | solution.py:40
  13.2 5.4 %collective-permute-start.11 = (bf16[1,32,3712]{2,1,0:T(8,128)(2,1)S(1)}, bf16[1,32,3712]{2,1,0:T(8,128)(2,1)S(1)}, u32[]{:S(2)}, u32[]{:S(2)}) collective-permute-start(bf16[1,32,3712]{2,1,0:T(8,128)(2,1)S(1)} %collective-permute-done), channel_id=1, source_target_pairs={{0,192},{64,0},{128,64},{192,128},{1,193},{65,1},{129,65},{193,129... | collective-permute-start | bytes 712712 | tf_op jit(solution)/shard_map/ppermute | solution.py:44
  14.7 6.3 %collective-permute-start.5 = (bf16[1,16,3712]{2,1,0:T(8,128)(2,1)S(1)}, bf16[1,16,3712]{2,1,0:T(8,128)(2,1)S(1)}, u32[]{:S(2)}, u32[]{:S(2)}) collective-permute-start(bf16[1,16,3712]{2,1,0:T(8,128)(2,1)S(1)} %slice.38), channel_id=1, source_target_pairs={{0,16},{16,32},{32,48},{48,0},{1,17},{17,33},{33,49},{49,1},{2,18}... | collective-permute-start | bytes 356360 | tf_op jit(solution)/shard_map/ppermute | solution.py:40
  14.8 6.2 %collective-permute-start.6 = (bf16[1,16,3712]{2,1,0:T(8,128)(2,1)S(1)}, bf16[1,16,3712]{2,1,0:T(8,128)(2,1)S(1)}, u32[]{:S(2)}, u32[]{:S(2)}) collective-permute-start(bf16[1,16,3712]{2,1,0:T(8,128)(2,1)S(1)} %slice.39), channel_id=1, source_target_pairs={{0,48},{16,0},{32,16},{48,32},{1,49},{17,1},{33,17},{49,33},{2,50}... | collective-permute-start | bytes 356360 | tf_op jit(solution)/shard_map/ppermute | solution.py:44
  18.2 5.3 %collective-permute-start.12 = (bf16[1,16,3712]{2,1,0:T(8,128)(2,1)S(1)}, bf16[1,16,3712]{2,1,0:T(8,128)(2,1)S(1)}, u32[]{:S(2)}, u32[]{:S(2)}) collective-permute-start(bf16[1,16,3712]{2,1,0:T(8,128)(2,1)S(1)} %slice.49), channel_id=1, source_target_pairs={{0,64},{64,128},{128,192},{192,0},{1,65},{65,129},{129,193},{193,1... | collective-permute-start | bytes 356360 | tf_op jit(solution)/shard_map/ppermute | solution.py:40
  18.6 4.8 %collective-permute-start.13 = (bf16[1,16,3712]{2,1,0:T(8,128)(2,1)S(1)}, bf16[1,16,3712]{2,1,0:T(8,128)(2,1)S(1)}, u32[]{:S(2)}, u32[]{:S(2)}) collective-permute-start(bf16[1,16,3712]{2,1,0:T(8,128)(2,1)S(1)} %slice.50), channel_id=1, source_target_pairs={{0,192},{64,0},{128,64},{192,128},{1,193},{65,1},{129,65},{193,129... | collective-permute-start | bytes 356360 | tf_op jit(solution)/shard_map/ppermute | solution.py:44
  21.1 20.8 %collective-permute-start.8 = (bf16[4,32,3712]{2,1,0:T(8,128)(2,1)S(1)}, bf16[4,32,3712]{2,1,0:T(8,128)(2,1)S(1)}, u32[]{:S(2)}, u32[]{:S(2)}) collective-permute-start(bf16[4,32,3712]{2,1,0:T(8,128)(2,1)S(1)} %maximum_maximum_fusion.refs_0_), channel_id=1, source_target_pairs={{0,192},{64,0},{128,64},{192,128},{1,193},{65,1},{129,65},{193,129... | collective-permute-start | bytes 2850824 | tf_op jit(solution)/shard_map/ppermute | solution.py:44
  21.8 22.4 %collective-permute-start.7 = (bf16[4,32,3712]{2,1,0:T(8,128)(2,1)S(1)}, bf16[4,32,3712]{2,1,0:T(8,128)(2,1)S(1)}, u32[]{:S(2)}, u32[]{:S(2)}) collective-permute-start(bf16[4,32,3712]{2,1,0:T(8,128)(2,1)S(1)} %maximum_maximum_fusion.refs_0_), channel_id=1, source_target_pairs={{0,64},{64,128},{128,192},{192,0},{1,65},{65,129},{129,193},{193,1... | collective-permute-start | bytes 2850824 | tf_op jit(solution)/shard_map/ppermute | solution.py:40
  23.5 20.8 %collective-permute-start.14 = (bf16[4,32,3712]{2,1,0:T(8,128)(2,1)S(1)}, bf16[4,32,3712]{2,1,0:T(8,128)(2,1)S(1)}, u32[]{:S(2)}, u32[]{:S(2)}) collective-permute-start(bf16[4,32,3712]{2,1,0:T(8,128)(2,1)S(1)} %maximum_maximum_fusion.1.refs_5_), channel_id=1, source_target_pairs={{0,16},{16,32},{32,48},{48,0},{1,17},{17,33},{33,49},{49,1},{2,18}... | collective-permute-start | bytes 2850824 | tf_op jit(solution)/shard_map/ppermute | solution.py:40
  23.7 21.6 %collective-permute-start.15 = (bf16[4,32,3712]{2,1,0:T(8,128)(2,1)S(1)}, bf16[4,32,3712]{2,1,0:T(8,128)(2,1)S(1)}, u32[]{:S(2)}, u32[]{:S(2)}) collective-permute-start(bf16[4,32,3712]{2,1,0:T(8,128)(2,1)S(1)} %maximum_maximum_fusion.1.refs_5_), channel_id=1, source_target_pairs={{0,48},{16,0},{32,16},{48,32},{1,49},{17,1},{33,17},{49,33},{2,50}... | collective-permute-start | bytes 2850824 | tf_op jit(solution)/shard_map/ppermute | solution.py:44
  26.4 21.1 %collective-permute-start.2 = (bf16[128,3328]{1,0:T(8,128)(2,1)S(1)}, bf16[128,3328]{1,0:T(8,128)(2,1)S(1)}, u32[]{:S(2)}, u32[]{:S(2)}) collective-permute-start(bf16[128,3328]{1,0:T(8,128)(2,1)S(1)} %pad_maximum_fusion), channel_id=1, source_target_pairs={{0,8},{8,0},{1,9},{9,1},{2,10},{10,2},{3,11},{11,3},{4,12},{12,4},... | collective-permute-start | bytes 2555912 | tf_op jit(solution)/shard_map/ppermute | solution.py:56
  42.0 5.5 %copy-start.4 = (s32[32]{0:T(128)S(1)}, s32[32]{0:T(128)}, u32[]{:S(2)}) copy-start(s32[32]{0:T(128)} %constant.46.clone) | copy-start | bytes 388
  42.0 5.4 %copy-start.5 = (s32[32]{0:T(128)S(1)}, s32[32]{0:T(128)}, u32[]{:S(2)}) copy-start(s32[32]{0:T(128)} %constant.47.clone) | copy-start | bytes 388
  42.0 5.4 %copy-start.6 = (s32[32]{0:T(128)S(1)}, s32[32]{0:T(128)}, u32[]{:S(2)}) copy-start(s32[32]{0:T(128)} %constant.48.clone) | copy-start | bytes 388
  42.0 9.3 %collective-permute-start.10 = (bf16[2,32,3712]{2,1,0:T(8,128)(2,1)S(1)}, bf16[2,32,3712]{2,1,0:T(8,128)(2,1)S(1)}, u32[]{:S(2)}, u32[]{:S(2)}) collective-permute-start(bf16[2,32,3712]{2,1,0:T(8,128)(2,1)S(1)} %slice.48), channel_id=1, source_target_pairs={{0,192},{64,0},{128,64},{192,128},{1,193},{65,1},{129,65},{193,129... | collective-permute-start | bytes 1425416 | tf_op jit(solution)/shard_map/ppermute | solution.py:44
  44.3 8.8 %collective-permute-start.9 = (bf16[2,32,3712]{2,1,0:T(8,128)(2,1)S(1)}, bf16[2,32,3712]{2,1,0:T(8,128)(2,1)S(1)}, u32[]{:S(2)}, u32[]{:S(2)}) collective-permute-start(bf16[2,32,3712]{2,1,0:T(8,128)(2,1)S(1)} %slice.47), channel_id=1, source_target_pairs={{0,64},{64,128},{128,192},{192,0},{1,65},{65,129},{129,193},{193,1... | collective-permute-start | bytes 1425416 | tf_op jit(solution)/shard_map/ppermute | solution.py:40
  44.4 8.9 %collective-permute-start.16 = (bf16[2,32,3712]{2,1,0:T(8,128)(2,1)S(1)}, bf16[2,32,3712]{2,1,0:T(8,128)(2,1)S(1)}, u32[]{:S(2)}, u32[]{:S(2)}) collective-permute-start(bf16[2,32,3712]{2,1,0:T(8,128)(2,1)S(1)} %slice.51), channel_id=1, source_target_pairs={{0,16},{16,32},{32,48},{48,0},{1,17},{17,33},{33,49},{49,1},{2,18}... | collective-permute-start | bytes 1425416 | tf_op jit(solution)/shard_map/ppermute | solution.py:40
  45.3 8.0 %collective-permute-start.17 = (bf16[2,32,3712]{2,1,0:T(8,128)(2,1)S(1)}, bf16[2,32,3712]{2,1,0:T(8,128)(2,1)S(1)}, u32[]{:S(2)}, u32[]{:S(2)}) collective-permute-start(bf16[2,32,3712]{2,1,0:T(8,128)(2,1)S(1)} %slice.52), channel_id=1, source_target_pairs={{0,48},{16,0},{32,16},{48,32},{1,49},{17,1},{33,17},{49,33},{2,50}... | collective-permute-start | bytes 1425416 | tf_op jit(solution)/shard_map/ppermute | solution.py:44
  53.3 9.8 %copy-start.3 = (f32[6,32,128]{2,1,0:T(8,128)S(1)}, f32[6,32,128]{2,1,0:T(8,128)}, u32[]{:S(2)}) copy-start(f32[6,32,128]{2,1,0:T(8,128)} %param.15) | copy-start | bytes 294916
  53.3 26.1 %copy-start.1 = (f32[32]{0:T(128)S(1)}, f32[32]{0:T(128)}, u32[]{:S(2)}) copy-start(f32[32]{0:T(128)} %param.14) | copy-start | bytes 388
  57.2 7.2 %collective-permute-start.18 = (f32[8,16,512]{2,1,0:T(8,128)S(1)}, f32[8,16,512]{2,1,0:T(8,128)S(1)}, u32[]{:S(2)}, u32[]{:S(2)}) collective-permute-start(f32[8,16,512]{2,1,0:T(8,128)S(1)} %get-tuple-element.47), channel_id=1, source_target_pairs={{0,1},{1,0},{2,3},{3,2},{4,5},{5,4},{6,7},{7,6},{8,9},{9,8},{10,11... | collective-permute-start | bytes 786440 | tf_op jit(solution)/shard_map/ppermute | solution.py:56
  104.6 3.4 %collective-permute-start.19 = (f32[16,256]{1,0:T(8,128)S(1)}, f32[16,256]{1,0:T(8,128)S(1)}, u32[]{:S(2)}, u32[]{:S(2)}) collective-permute-start(f32[16,256]{1,0:T(8,128)S(1)} %fusion.1), channel_id=1, source_target_pairs={{0,1},{1,0},{2,3},{3,2},{4,5},{5,4},{6,7},{7,6},{8,9},{9,8},{10,11... | collective-permute-start | bytes 49160 | tf_op jit(solution)/shard_map/ppermute | solution.py:56

commit v4 on v3

--- a/solution.py
+++ b/solution.py
@@ -70,7 +70,7 @@
 def coupling_kernel(slots, starts, place, *refs):
     pieces = refs[:10]
     tiles = refs[10:12]
-    keep, send, lead_out, ordered, total, lead, done = refs[12:]
+    keep, send, lead_out, ordered, total, wide, lead, done = refs[12:]
     at = 0
     for ref in pieces:
         for i in range(ref.shape[0]):
@@ -96,20 +96,18 @@
             row = pl.multiple_of(starts[h, b] * MEM, MEM)
             return ordered[pl.ds(row, STEPS * MEM), b * BLOCK:(b + 1) * BLOCK]
 
-        for b in range(0, BLOCKS, 2):
-            if b + 1 < BLOCKS:
-                rates = jnp.concatenate([window(b), window(b + 1)], axis=1)
-                weights = tiles[h][:, b * BLOCK:(b + 2) * BLOCK]
-            else:
-                rates = window(b)
-                weights = tiles[h][:, b * BLOCK:(b + 1) * BLOCK]
+        for b in range(0, BLOCKS, 4):
+            last = min(b + 4, BLOCKS)
+            rates = jnp.concatenate([window(i) for i in range(b, last)], axis=1)
+            weights = tiles[h][:, b * BLOCK:last * BLOCK]
             part = lax.dot_general(
-                weights, rates, (((1,), (1,)), ((), ())), preferred_element_type=jnp.float32
+                rates, weights, (((1,), (1,)), ((), ())), preferred_element_type=jnp.float32
             )
             if b == 0:
-                total[...] = part
+                wide[...] = part
             else:
-                total[...] += part
+                wide[...] += part
+        total[...] = wide[...].T
         z = zl if h == 0 else 1 - zl
         for q in range(4):
             mine = pl.multiple_of(q * 32 + core * 16, 16)
@@ -143,7 +141,7 @@
         y3, y4, y5 = n3, n4, n5
         rows[pl.ds(t, 16, stride=STEPS), :] = y1 - y2
     for i, v in enumerate((y0, y1, y2, y3, y4, y5)):
-        final[i] = v
+        final[i] = v.T
     flat = rows[...].T.astype(jnp.bfloat16)
     for i in range(4):
         potential[:, i, 0, :] = flat[:, :128]
@@ -183,6 +181,7 @@
     slots = ((y + PLACE_Y) & 3) * 8 + ((x + PLACE_X) & 3) * 2 + (zl ^ PLACE_Z)
     place = jnp.stack([zl, core])
     start = (cycle_head[0] - delays) & (SLOTS - 1)
+    own, start = lax.optimization_barrier((own, start))
     start_own = cut(start, near_block, BLOCKS, 1)
     start_far = cut(start, far_block, BLOCKS, 1)
     note = jnp.pad(start_far.astype(jnp.bfloat16), ((0, 0), (0, BLOCK - BLOCKS)))
@@ -211,6 +210,7 @@
         scratch_shapes=[
             pltpu.VMEM(((SLOTS + STEPS) * MEM, HALF), jnp.bfloat16),
             pltpu.VMEM((BLOCK, STEPS * MEM), jnp.float32),
+            pltpu.VMEM((STEPS * MEM, BLOCK), jnp.float32),
             pltpu.VMEM((SLOTS * 64, SENSORS), jnp.bfloat16),
             pltpu.SemaphoreType.DMA,
         ],
@@ -224,7 +224,7 @@
     final, potential = pl.pallas_call(
         integrate_kernel,
         out_shape=(
-            jax.ShapeDtypeStruct((6, 16, MEM), jnp.float32),
+            jax.ShapeDtypeStruct((6, MEM, 16), jnp.float32),
             jax.ShapeDtypeStruct((MEM, 4, 2, 128), jnp.bfloat16),
         ),
         in_specs=vmem(3),
@@ -239,7 +239,7 @@
         got.reshape(SLOTS * 64, STEPS), lead, (((0,), (0,)), ((), ())), preferred_element_type=jnp.float32
     )
     signal = signal + swap(signal, "c")
-    return signal[None], jnp.transpose(final, (0, 2, 1))
+    return signal[None], final
 
 
 def solution(mesh):

time: 109 us -> 107 us (0.982)
    ppermute x8, waiting for transfers between devices: 18.1 us -> 20.8 us  [down(): return lax.ppermute(v, axis, [(i, (i + 3) % 4) for i in range(4)])]
    ppermute x4, waiting for transfers between devices: 4.44 us -> 2.07 us  [swap(): return lax.ppermute(v, axis, [(0, 1), (1, 0)])]
    ppermute x8, starting transfers between devices: 14.8 us -> 12.7 us  [down(): return lax.ppermute(v, axis, [(i, (i + 3) % 4) for i in range(4)])]
    ppermute x8, starting transfers between devices: 6.88 us -> 8.69 us  [up(): return lax.ppermute(v, axis, [(i, (i + 1) % 4) for i in range(4)])]
  transfers between devices with their start and end apart: 20 -> 20, of which waited for: 10 -> 9; matrix products, arithmetic and copies ran while one was open for 1% -> 2% of each run, Pallas kernels for 0% -> 0%
where the time goes in v4:
time: 107 us
  blocking collectives  37.7 us (35%)
  starting transfers between devices  32.4 us (30%)
  waiting for transfers between devices  26.4 us (25%)
  Pallas kernels  4.01 us (4%)
  local copies, waits for them, and re-layouts  3.21 us (3%)
  between operations  1.53 us (1%)
  other arithmetic  1.2 us (1%)
    all_to_all x1, blocking collectives, body(): lax.all_to_all(potential.reshape(MEM * 4, 2, 128), TGT + ('zh',), 0, 0, t...  22.9 us
    ppermute x8, waiting for transfers between devices, down(): return lax.ppermute(v, axis, [(i, (i + 3) % 4) for i in range(4)])  20.8 us
    all_to_all x1, blocking collectives, body(): parts = lax.all_to_all(joined, ('zl', 'zh'), 0, 0, tiled=True)  14.8 us
    ppermute x8, starting transfers between devices, down(): return lax.ppermute(v, axis, [(i, (i + 3) % 4) for i in range(4)])  12.7 us
    ppermute x4, starting transfers between devices, swap(): return lax.ppermute(v, axis, [(0, 1), (1, 0)])  11 us
    ppermute x8, starting transfers between devices, up(): return lax.ppermute(v, axis, [(i, (i + 1) % 4) for i in range(4)])  8.69 us
    ppermute x8, waiting for transfers between devices, up(): return lax.ppermute(v, axis, [(i, (i + 1) % 4) for i in range(4)])  3.52 us
    pallas_call x1, Pallas kernels, body(): pl.pallas_call(coupling_kernel, out_shape=(jax.ShapeDtypeStruct((8, 16, S...  3.5 us
  transfers between devices with their start and end apart: 20, of which 9 were waited for; matrix products, arithmetic and copies ran while one was open for 2% of the time, Pallas kernels for 0%

profile of v4, /device:TPU:1, one launch (start us, length us, event | category | flops | bytes accessed | tf_op | source)
XLA Modules:
  0.0 106.7 jit_solution(17913966494261807677)
XLA Ops:
  0.7 0.9 constant_dynamic-slice_fusion
  1.8 2.6 %collective-permute-start = (bf16[1,32,3712]{2,1,0:T(8,128)(2,1)S(1)}, bf16[1,32,3712]{2,1,0:T(8,128)(2,1)S(1)}, u32[]{:S(2)}, u32[]{:S(2)}) collective-permute-start(bf16[1,32,3712]{2,1,0:T(8,128)(2,1)S(1)} %pad_maximum_fusion.2), channel_id=1, source_target_pairs={{0,8},{8,0},{1,9},{9,1},{2,10},{10,2},{3,11},{11,3},{4,12},{12,4},... | collective-permute-start | bytes 712712 | tf_op jit(solution)/shard_map/ppermute | solution.py:56
  5.2 1.3 %collective-permute-start.3 = (bf16[1,32,3712]{2,1,0:T(8,128)(2,1)S(1)}, bf16[1,32,3712]{2,1,0:T(8,128)(2,1)S(1)}, u32[]{:S(2)}, u32[]{:S(2)}) collective-permute-start(bf16[1,32,3712]{2,1,0:T(8,128)(2,1)S(1)} %pad_maximum_fusion.1), channel_id=1, source_target_pairs={{0,16},{16,32},{32,48},{48,0},{1,17},{17,33},{33,49},{49,1},{2,18}... | collective-permute-start | bytes 712712 | tf_op jit(solution)/shard_map/ppermute | solution.py:40
  6.5 1.5 %collective-permute-start.4 = (bf16[1,32,3712]{2,1,0:T(8,128)(2,1)S(1)}, bf16[1,32,3712]{2,1,0:T(8,128)(2,1)S(1)}, u32[]{:S(2)}, u32[]{:S(2)}) collective-permute-start(bf16[1,32,3712]{2,1,0:T(8,128)(2,1)S(1)} %pad_maximum_fusion.1), channel_id=1, source_target_pairs={{0,48},{16,0},{32,16},{48,32},{1,49},{17,1},{33,17},{49,33},{2,50}... | collective-permute-start | bytes 712712 | tf_op jit(solution)/shard_map/ppermute | solution.py:44
  7.9 0.9 collective-permute-done
  8.8 2.2 %collective-permute-start.1 = (bf16[1,32,3712]{2,1,0:T(8,128)(2,1)S(1)}, bf16[1,32,3712]{2,1,0:T(8,128)(2,1)S(1)}, u32[]{:S(2)}, u32[]{:S(2)}) collective-permute-start(bf16[1,32,3712]{2,1,0:T(8,128)(2,1)S(1)} %collective-permute-done), channel_id=1, source_target_pairs={{0,64},{64,128},{128,192},{192,0},{1,65},{65,129},{129,193},{193,1... | collective-permute-start | bytes 712712 | tf_op jit(solution)/shard_map/ppermute | solution.py:40
  11.0 1.4 %collective-permute-start.11 = (bf16[1,32,3712]{2,1,0:T(8,128)(2,1)S(1)}, bf16[1,32,3712]{2,1,0:T(8,128)(2,1)S(1)}, u32[]{:S(2)}, u32[]{:S(2)}) collective-permute-start(bf16[1,32,3712]{2,1,0:T(8,128)(2,1)S(1)} %collective-permute-done), channel_id=1, source_target_pairs={{0,192},{64,0},{128,64},{192,128},{1,193},{65,1},{129,65},{193,129... | collective-permute-start | bytes 712712 | tf_op jit(solution)/shard_map/ppermute | solution.py:44
  12.5 0.6 constant_dynamic-slice_fusion.2
  13.2 1.3 %collective-permute-start.5 = (bf16[1,16,3712]{2,1,0:T(8,128)(2,1)S(1)}, bf16[1,16,3712]{2,1,0:T(8,128)(2,1)S(1)}, u32[]{:S(2)}, u32[]{:S(2)}) collective-permute-start(bf16[1,16,3712]{2,1,0:T(8,128)(2,1)S(1)} %slice.38), channel_id=1, source_target_pairs={{0,16},{16,32},{32,48},{48,0},{1,17},{17,33},{33,49},{49,1},{2,18}... | collective-permute-start | bytes 356360 | tf_op jit(solution)/shard_map/ppermute | solution.py:40
  14.5 1.5 %collective-permute-start.6 = (bf16[1,16,3712]{2,1,0:T(8,128)(2,1)S(1)}, bf16[1,16,3712]{2,1,0:T(8,128)(2,1)S(1)}, u32[]{:S(2)}, u32[]{:S(2)}) collective-permute-start(bf16[1,16,3712]{2,1,0:T(8,128)(2,1)S(1)} %slice.39), channel_id=1, source_target_pairs={{0,48},{16,0},{32,16},{48,32},{1,49},{17,1},{33,17},{49,33},{2,50}... | collective-permute-start | bytes 356360 | tf_op jit(solution)/shard_map/ppermute | solution.py:44
  16.1 0.7 collective-permute-done.1
  17.2 2.5 %collective-permute-start.13 = (bf16[1,16,3712]{2,1,0:T(8,128)(2,1)S(1)}, bf16[1,16,3712]{2,1,0:T(8,128)(2,1)S(1)}, u32[]{:S(2)}, u32[]{:S(2)}) collective-permute-start(bf16[1,16,3712]{2,1,0:T(8,128)(2,1)S(1)} %slice.50), channel_id=1, source_target_pairs={{0,192},{64,0},{128,64},{192,128},{1,193},{65,1},{129,65},{193,129... | collective-permute-start | bytes 356360 | tf_op jit(solution)/shard_map/ppermute | solution.py:44
  19.8 1.2 %collective-permute-start.8 = (bf16[4,32,3712]{2,1,0:T(8,128)(2,1)S(1)}, bf16[4,32,3712]{2,1,0:T(8,128)(2,1)S(1)}, u32[]{:S(2)}, u32[]{:S(2)}) collective-permute-start(bf16[4,32,3712]{2,1,0:T(8,128)(2,1)S(1)} %maximum_maximum_fusion.refs_0_), channel_id=1, source_target_pairs={{0,192},{64,0},{128,64},{192,128},{1,193},{65,1},{129,65},{193,129... | collective-permute-start | bytes 2850824 | tf_op jit(solution)/shard_map/ppermute | solution.py:44
  21.9 1.4 %collective-permute-start.14 = (bf16[4,32,3712]{2,1,0:T(8,128)(2,1)S(1)}, bf16[4,32,3712]{2,1,0:T(8,128)(2,1)S(1)}, u32[]{:S(2)}, u32[]{:S(2)}) collective-permute-start(bf16[4,32,3712]{2,1,0:T(8,128)(2,1)S(1)} %maximum_maximum_fusion.1.refs_5_), channel_id=1, source_target_pairs={{0,16},{16,32},{32,48},{48,0},{1,17},{17,33},{33,49},{49,1},{2,18}... | collective-permute-start | bytes 2850824 | tf_op jit(solution)/shard_map/ppermute | solution.py:40
  23.4 1.4 %collective-permute-start.15 = (bf16[4,32,3712]{2,1,0:T(8,128)(2,1)S(1)}, bf16[4,32,3712]{2,1,0:T(8,128)(2,1)S(1)}, u32[]{:S(2)}, u32[]{:S(2)}) collective-permute-start(bf16[4,32,3712]{2,1,0:T(8,128)(2,1)S(1)} %maximum_maximum_fusion.1.refs_5_), channel_id=1, source_target_pairs={{0,48},{16,0},{32,16},{48,32},{1,49},{17,1},{33,17},{49,33},{2,50}... | collective-permute-start | bytes 2850824 | tf_op jit(solution)/shard_map/ppermute | solution.py:44
  24.9 1.3 %collective-permute-start.2 = (bf16[128,3328]{1,0:T(8,128)(2,1)S(1)}, bf16[128,3328]{1,0:T(8,128)(2,1)S(1)}, u32[]{:S(2)}, u32[]{:S(2)}) collective-permute-start(bf16[128,3328]{1,0:T(8,128)(2,1)S(1)} %pad_maximum_fusion), channel_id=1, source_target_pairs={{0,8},{8,0},{1,9},{9,1},{2,10},{10,2},{3,11},{11,3},{4,12},{12,4},... | collective-permute-start | bytes 2555912 | tf_op jit(solution)/shard_map/ppermute | solution.py:56
  26.1 15.9 %collective-permute-done.8.refs_2_ = bf16[4,32,3712]{2,1,0:T(8,128)(2,1)S(1)} collective-permute-done((bf16[4,32,3712]{2,1,0:T(8,128)(2,1)S(1)}, bf16[4,32,3712]{2,1,0:T(8,128)(2,1)S(1)}, u32[]{:S(2)}, u32[]{:S(2)}) %collective-permute-start.8) | collective-permute-done | bytes 950304 | tf_op jit(solution)/shard_map/ppermute | solution.py:44
  42.1 1.6 %collective-permute-start.10 = (bf16[2,32,3712]{2,1,0:T(8,128)(2,1)S(1)}, bf16[2,32,3712]{2,1,0:T(8,128)(2,1)S(1)}, u32[]{:S(2)}, u32[]{:S(2)}) collective-permute-start(bf16[2,32,3712]{2,1,0:T(8,128)(2,1)S(1)} %slice.48), channel_id=1, source_target_pairs={{0,192},{64,0},{128,64},{192,128},{1,193},{65,1},{129,65},{193,129... | collective-permute-start | bytes 1425416 | tf_op jit(solution)/shard_map/ppermute | solution.py:44
  44.0 1.6 %collective-permute-start.16 = (bf16[2,32,3712]{2,1,0:T(8,128)(2,1)S(1)}, bf16[2,32,3712]{2,1,0:T(8,128)(2,1)S(1)}, u32[]{:S(2)}, u32[]{:S(2)}) collective-permute-start(bf16[2,32,3712]{2,1,0:T(8,128)(2,1)S(1)} %slice.51), channel_id=1, source_target_pairs={{0,16},{16,32},{32,48},{48,0},{1,17},{17,33},{33,49},{49,1},{2,18}... | collective-permute-start | bytes 1425416 | tf_op jit(solution)/shard_map/ppermute | solution.py:40
  45.6 1.5 %collective-permute-start.17 = (bf16[2,32,3712]{2,1,0:T(8,128)(2,1)S(1)}, bf16[2,32,3712]{2,1,0:T(8,128)(2,1)S(1)}, u32[]{:S(2)}, u32[]{:S(2)}) collective-permute-start(bf16[2,32,3712]{2,1,0:T(8,128)(2,1)S(1)} %slice.52), channel_id=1, source_target_pairs={{0,48},{16,0},{32,16},{48,32},{1,49},{17,1},{33,17},{49,33},{2,50}... | collective-permute-start | bytes 1425416 | tf_op jit(solution)/shard_map/ppermute | solution.py:44
  47.3 4.9 %collective-permute-done.10.refs_4_ = bf16[2,32,3712]{2,1,0:T(8,128)(2,1)S(1)} collective-permute-done((bf16[2,32,3712]{2,1,0:T(8,128)(2,1)S(1)}, bf16[2,32,3712]{2,1,0:T(8,128)(2,1)S(1)}, u32[]{:S(2)}, u32[]{:S(2)}) %collective-permute-start.10) | collective-permute-done | bytes 475168 | tf_op jit(solution)/shard_map/ppermute | solution.py:44
  52.2 1.4 %collective-permute-done.9.refs_3_ = bf16[2,32,3712]{2,1,0:T(8,128)(2,1)S(1)} collective-permute-done((bf16[2,32,3712]{2,1,0:T(8,128)(2,1)S(1)}, bf16[2,32,3712]{2,1,0:T(8,128)(2,1)S(1)}, u32[]{:S(2)}, u32[]{:S(2)}) %collective-permute-start.9) | collective-permute-done | bytes 475168 | tf_op jit(solution)/shard_map/ppermute | solution.py:40
  53.6 0.9 collective-permute-done.16.refs_8_
  54.5 3.5 %coupling.1 = (f32[8,16,512]{2,1,0:T(8,128)S(1)}, f32[8,16,512]{2,1,0:T(8,128)S(1)}, bf16[2048,256]{1,0:T(8,128)(2,1)S(1)}) custom-call(s32[32]{0:T(128)S(1)} %xor_add_fusion.slots, s32[2,25]{1,0:T(2,128)S(1)} %pad_add_fusion.starts, s32[2]{0:T(128)S(1)} %pad_add_fusion.1.place, bf16[4,32,3712]{2,1,0:T(8,128)(2,1)S(1)} %maximum_maximum_fusion.refs_0_, ...), custom_call_target="tpu_custom_call" | custom-call | tf_op jit(solution)/shard_map/coupling/pallas_call | solution.py:201
  58.0 4.6 %collective-permute-start.18 = (f32[8,16,512]{2,1,0:T(8,128)S(1)}, f32[8,16,512]{2,1,0:T(8,128)S(1)}, u32[]{:S(2)}, u32[]{:S(2)}) collective-permute-start(f32[8,16,512]{2,1,0:T(8,128)S(1)} %get-tuple-element.51), channel_id=1, source_target_pairs={{0,1},{1,0},{2,3},{3,2},{4,5},{5,4},{6,7},{7,6},{8,9},{9,8},{10,11... | collective-permute-start | bytes 786440 | tf_op jit(solution)/shard_map/ppermute | solution.py:56
  62.7 1.1 %collective-permute-done.18 = f32[8,16,512]{2,1,0:T(8,128)S(1)} collective-permute-done((f32[8,16,512]{2,1,0:T(8,128)S(1)}, f32[8,16,512]{2,1,0:T(8,128)S(1)}, u32[]{:S(2)}, u32[]{:S(2)}) %collective-permute-start.18) | collective-permute-done | bytes 262176 | tf_op jit(solution)/shard_map/ppermute | solution.py:56
  63.8 14.8 %all_to_all.10.parts = f32[8,16,512]{2,1,0:T(8,128)S(1)} all-to-all(f32[8,16,512]{2,1,0:T(8,128)S(1)} %add.36), channel_id=1, replica_groups=mesh['y'=4,'x'=4,'zl'=2,'zh'=4,'c'=2] {'zl','zh'}, dimensions={0} | all-to-all | bytes 524288 | tf_op jit(solution)/shard_map/all_to_all | solution.py:223
  78.6 0.5 integrate.1
  79.1 22.9 %all_to_all.11 = bf16[128,2,128]{2,1,0:T(2,128)(2,1)S(1)} all-to-all(bf16[128,2,128]{2,1,0:T(2,128)(2,1)S(1)} %bitcast.22), channel_id=1, replica_groups=mesh['y'=4,'x'=4,'zl'=2,'zh'=4,'c'=2] {'y','x','zl','zh'}, dimensions={0} | all-to-all | bytes 131072 | tf_op jit(solution)/shard_map/all_to_all | solution.py:237
  102.7 2.6 %collective-permute-start.19 = (f32[16,256]{1,0:T(8,128)S(1)}, f32[16,256]{1,0:T(8,128)S(1)}, u32[]{:S(2)}, u32[]{:S(2)}) collective-permute-start(f32[16,256]{1,0:T(8,128)S(1)} %fusion.1), channel_id=1, source_target_pairs={{0,1},{1,0},{2,3},{3,2},{4,5},{5,4},{6,7},{7,6},{8,9},{9,8},{10,11... | collective-permute-start | bytes 49160 | tf_op jit(solution)/shard_map/ppermute | solution.py:56
  105.2 0.7 copy.15
  106.1 0.6 add_bitcast_fusion
  (60 shorter events, 3.3 us)
Async XLA Ops:
  0.6 1.0 copy-start
  0.6 11.8 %copy-start.2 = (bf16[128,6400]{1,0:T(8,128)(2,1)S(1)}, bf16[128,6400]{1,0:T(8,128)(2,1)}, u32[]{:S(2)}) copy-start(bf16[128,6400]{1,0:T(8,128)(2,1)} %param.10) | copy-start | bytes 4915204
  0.7 4.5 %copy-start.7 = (s32[1,50]{1,0:T(1,128)S(1)}, s32[1,50]{1,0:T(1,128)}, u32[]{:S(2)}) copy-start(s32[1,50]{1,0:T(1,128)} %param.12) | copy-start | bytes 604
  1.8 7.0 %collective-permute-start = (bf16[1,32,3712]{2,1,0:T(8,128)(2,1)S(1)}, bf16[1,32,3712]{2,1,0:T(8,128)(2,1)S(1)}, u32[]{:S(2)}, u32[]{:S(2)}) collective-permute-start(bf16[1,32,3712]{2,1,0:T(8,128)(2,1)S(1)} %pad_maximum_fusion.2), channel_id=1, source_target_pairs={{0,8},{8,0},{1,9},{9,1},{2,10},{10,2},{3,11},{11,3},{4,12},{12,4},... | collective-permute-start | bytes 712712 | tf_op jit(solution)/shard_map/ppermute | solution.py:56
  5.2 8.0 %collective-permute-start.3 = (bf16[1,32,3712]{2,1,0:T(8,128)(2,1)S(1)}, bf16[1,32,3712]{2,1,0:T(8,128)(2,1)S(1)}, u32[]{:S(2)}, u32[]{:S(2)}) collective-permute-start(bf16[1,32,3712]{2,1,0:T(8,128)(2,1)S(1)} %pad_maximum_fusion.1), channel_id=1, source_target_pairs={{0,16},{16,32},{32,48},{48,0},{1,17},{17,33},{33,49},{49,1},{2,18}... | collective-permute-start | bytes 712712 | tf_op jit(solution)/shard_map/ppermute | solution.py:40
  6.5 6.7 %collective-permute-start.4 = (bf16[1,32,3712]{2,1,0:T(8,128)(2,1)S(1)}, bf16[1,32,3712]{2,1,0:T(8,128)(2,1)S(1)}, u32[]{:S(2)}, u32[]{:S(2)}) collective-permute-start(bf16[1,32,3712]{2,1,0:T(8,128)(2,1)S(1)} %pad_maximum_fusion.1), channel_id=1, source_target_pairs={{0,48},{16,0},{32,16},{48,32},{1,49},{17,1},{33,17},{49,33},{2,50}... | collective-permute-start | bytes 712712 | tf_op jit(solution)/shard_map/ppermute | solution.py:44
  8.8 8.0 %collective-permute-start.1 = (bf16[1,32,3712]{2,1,0:T(8,128)(2,1)S(1)}, bf16[1,32,3712]{2,1,0:T(8,128)(2,1)S(1)}, u32[]{:S(2)}, u32[]{:S(2)}) collective-permute-start(bf16[1,32,3712]{2,1,0:T(8,128)(2,1)S(1)} %collective-permute-done), channel_id=1, source_target_pairs={{0,64},{64,128},{128,192},{192,0},{1,65},{65,129},{129,193},{193,1... | collective-permute-start | bytes 712712 | tf_op jit(solution)/shard_map/ppermute | solution.py:40
  11.0 6.1 %collective-permute-start.11 = (bf16[1,32,3712]{2,1,0:T(8,128)(2,1)S(1)}, bf16[1,32,3712]{2,1,0:T(8,128)(2,1)S(1)}, u32[]{:S(2)}, u32[]{:S(2)}) collective-permute-start(bf16[1,32,3712]{2,1,0:T(8,128)(2,1)S(1)} %collective-permute-done), channel_id=1, source_target_pairs={{0,192},{64,0},{128,64},{192,128},{1,193},{65,1},{129,65},{193,129... | collective-permute-start | bytes 712712 | tf_op jit(solution)/shard_map/ppermute | solution.py:44
  13.2 6.5 %collective-permute-start.5 = (bf16[1,16,3712]{2,1,0:T(8,128)(2,1)S(1)}, bf16[1,16,3712]{2,1,0:T(8,128)(2,1)S(1)}, u32[]{:S(2)}, u32[]{:S(2)}) collective-permute-start(bf16[1,16,3712]{2,1,0:T(8,128)(2,1)S(1)} %slice.38), channel_id=1, source_target_pairs={{0,16},{16,32},{32,48},{48,0},{1,17},{17,33},{33,49},{49,1},{2,18}... | collective-permute-start | bytes 356360 | tf_op jit(solution)/shard_map/ppermute | solution.py:40
  14.5 5.2 %collective-permute-start.6 = (bf16[1,16,3712]{2,1,0:T(8,128)(2,1)S(1)}, bf16[1,16,3712]{2,1,0:T(8,128)(2,1)S(1)}, u32[]{:S(2)}, u32[]{:S(2)}) collective-permute-start(bf16[1,16,3712]{2,1,0:T(8,128)(2,1)S(1)} %slice.39), channel_id=1, source_target_pairs={{0,48},{16,0},{32,16},{48,32},{1,49},{17,1},{33,17},{49,33},{2,50}... | collective-permute-start | bytes 356360 | tf_op jit(solution)/shard_map/ppermute | solution.py:44
  16.9 5.0 %collective-permute-start.12 = (bf16[1,16,3712]{2,1,0:T(8,128)(2,1)S(1)}, bf16[1,16,3712]{2,1,0:T(8,128)(2,1)S(1)}, u32[]{:S(2)}, u32[]{:S(2)}) collective-permute-start(bf16[1,16,3712]{2,1,0:T(8,128)(2,1)S(1)} %slice.49), channel_id=1, source_target_pairs={{0,64},{64,128},{128,192},{192,0},{1,65},{65,129},{129,193},{193,1... | collective-permute-start | bytes 356360 | tf_op jit(solution)/shard_map/ppermute | solution.py:40
  17.2 4.7 %collective-permute-start.13 = (bf16[1,16,3712]{2,1,0:T(8,128)(2,1)S(1)}, bf16[1,16,3712]{2,1,0:T(8,128)(2,1)S(1)}, u32[]{:S(2)}, u32[]{:S(2)}) collective-permute-start(bf16[1,16,3712]{2,1,0:T(8,128)(2,1)S(1)} %slice.50), channel_id=1, source_target_pairs={{0,192},{64,0},{128,64},{192,128},{1,193},{65,1},{129,65},{193,129... | collective-permute-start | bytes 356360 | tf_op jit(solution)/shard_map/ppermute | solution.py:44
  19.8 22.3 %collective-permute-start.8 = (bf16[4,32,3712]{2,1,0:T(8,128)(2,1)S(1)}, bf16[4,32,3712]{2,1,0:T(8,128)(2,1)S(1)}, u32[]{:S(2)}, u32[]{:S(2)}) collective-permute-start(bf16[4,32,3712]{2,1,0:T(8,128)(2,1)S(1)} %maximum_maximum_fusion.refs_0_), channel_id=1, source_target_pairs={{0,192},{64,0},{128,64},{192,128},{1,193},{65,1},{129,65},{193,129... | collective-permute-start | bytes 2850824 | tf_op jit(solution)/shard_map/ppermute | solution.py:44
  21.0 22.7 %collective-permute-start.7 = (bf16[4,32,3712]{2,1,0:T(8,128)(2,1)S(1)}, bf16[4,32,3712]{2,1,0:T(8,128)(2,1)S(1)}, u32[]{:S(2)}, u32[]{:S(2)}) collective-permute-start(bf16[4,32,3712]{2,1,0:T(8,128)(2,1)S(1)} %maximum_maximum_fusion.refs_0_), channel_id=1, source_target_pairs={{0,64},{64,128},{128,192},{192,0},{1,65},{65,129},{129,193},{193,1... | collective-permute-start | bytes 2850824 | tf_op jit(solution)/shard_map/ppermute | solution.py:40
  21.9 22.0 %collective-permute-start.14 = (bf16[4,32,3712]{2,1,0:T(8,128)(2,1)S(1)}, bf16[4,32,3712]{2,1,0:T(8,128)(2,1)S(1)}, u32[]{:S(2)}, u32[]{:S(2)}) collective-permute-start(bf16[4,32,3712]{2,1,0:T(8,128)(2,1)S(1)} %maximum_maximum_fusion.1.refs_5_), channel_id=1, source_target_pairs={{0,16},{16,32},{32,48},{48,0},{1,17},{17,33},{33,49},{49,1},{2,18}... | collective-permute-start | bytes 2850824 | tf_op jit(solution)/shard_map/ppermute | solution.py:40
  23.4 22.2 %collective-permute-start.15 = (bf16[4,32,3712]{2,1,0:T(8,128)(2,1)S(1)}, bf16[4,32,3712]{2,1,0:T(8,128)(2,1)S(1)}, u32[]{:S(2)}, u32[]{:S(2)}) collective-permute-start(bf16[4,32,3712]{2,1,0:T(8,128)(2,1)S(1)} %maximum_maximum_fusion.1.refs_5_), channel_id=1, source_target_pairs={{0,48},{16,0},{32,16},{48,32},{1,49},{17,1},{33,17},{49,33},{2,50}... | collective-permute-start | bytes 2850824 | tf_op jit(solution)/shard_map/ppermute | solution.py:44
  24.9 22.4 %collective-permute-start.2 = (bf16[128,3328]{1,0:T(8,128)(2,1)S(1)}, bf16[128,3328]{1,0:T(8,128)(2,1)S(1)}, u32[]{:S(2)}, u32[]{:S(2)}) collective-permute-start(bf16[128,3328]{1,0:T(8,128)(2,1)S(1)} %pad_maximum_fusion), channel_id=1, source_target_pairs={{0,8},{8,0},{1,9},{9,1},{2,10},{10,2},{3,11},{11,3},{4,12},{12,4},... | collective-permute-start | bytes 2555912 | tf_op jit(solution)/shard_map/ppermute | solution.py:56
  42.1 5.1 %copy-start.4 = (s32[32]{0:T(128)S(1)}, s32[32]{0:T(128)}, u32[]{:S(2)}) copy-start(s32[32]{0:T(128)} %constant.46.clone) | copy-start | bytes 388
  42.1 5.1 %copy-start.5 = (s32[32]{0:T(128)S(1)}, s32[32]{0:T(128)}, u32[]{:S(2)}) copy-start(s32[32]{0:T(128)} %constant.47.clone) | copy-start | bytes 388
  42.1 5.1 %copy-start.6 = (s32[32]{0:T(128)S(1)}, s32[32]{0:T(128)}, u32[]{:S(2)}) copy-start(s32[32]{0:T(128)} %constant.48.clone) | copy-start | bytes 388
  42.1 10.1 %collective-permute-start.10 = (bf16[2,32,3712]{2,1,0:T(8,128)(2,1)S(1)}, bf16[2,32,3712]{2,1,0:T(8,128)(2,1)S(1)}, u32[]{:S(2)}, u32[]{:S(2)}) collective-permute-start(bf16[2,32,3712]{2,1,0:T(8,128)(2,1)S(1)} %slice.48), channel_id=1, source_target_pairs={{0,192},{64,0},{128,64},{192,128},{1,193},{65,1},{129,65},{193,129... | collective-permute-start | bytes 1425416 | tf_op jit(solution)/shard_map/ppermute | solution.py:44
  43.8 9.8 %collective-permute-start.9 = (bf16[2,32,3712]{2,1,0:T(8,128)(2,1)S(1)}, bf16[2,32,3712]{2,1,0:T(8,128)(2,1)S(1)}, u32[]{:S(2)}, u32[]{:S(2)}) collective-permute-start(bf16[2,32,3712]{2,1,0:T(8,128)(2,1)S(1)} %slice.47), channel_id=1, source_target_pairs={{0,64},{64,128},{128,192},{192,0},{1,65},{65,129},{129,193},{193,1... | collective-permute-start | bytes 1425416 | tf_op jit(solution)/shard_map/ppermute | solution.py:40
  44.0 10.5 %collective-permute-start.16 = (bf16[2,32,3712]{2,1,0:T(8,128)(2,1)S(1)}, bf16[2,32,3712]{2,1,0:T(8,128)(2,1)S(1)}, u32[]{:S(2)}, u32[]{:S(2)}) collective-permute-start(bf16[2,32,3712]{2,1,0:T(8,128)(2,1)S(1)} %slice.51), channel_id=1, source_target_pairs={{0,16},{16,32},{32,48},{48,0},{1,17},{17,33},{33,49},{49,1},{2,18}... | collective-permute-start | bytes 1425416 | tf_op jit(solution)/shard_map/ppermute | solution.py:40
  45.6 8.8 %collective-permute-start.17 = (bf16[2,32,3712]{2,1,0:T(8,128)(2,1)S(1)}, bf16[2,32,3712]{2,1,0:T(8,128)(2,1)S(1)}, u32[]{:S(2)}, u32[]{:S(2)}) collective-permute-start(bf16[2,32,3712]{2,1,0:T(8,128)(2,1)S(1)} %slice.52), channel_id=1, source_target_pairs={{0,48},{16,0},{32,16},{48,32},{1,49},{17,1},{33,17},{49,33},{2,50}... | collective-permute-start | bytes 1425416 | tf_op jit(solution)/shard_map/ppermute | solution.py:44
  54.5 8.1 %copy-start.3 = (f32[6,32,128]{2,1,0:T(8,128)S(1)}, f32[6,32,128]{2,1,0:T(8,128)}, u32[]{:S(2)}) copy-start(f32[6,32,128]{2,1,0:T(8,128)} %param.15) | copy-start | bytes 294916
  54.5 24.1 %copy-start.1 = (f32[32]{0:T(128)S(1)}, f32[32]{0:T(128)}, u32[]{:S(2)}) copy-start(f32[32]{0:T(128)} %param.14) | copy-start | bytes 388
  58.0 5.8 %collective-permute-start.18 = (f32[8,16,512]{2,1,0:T(8,128)S(1)}, f32[8,16,512]{2,1,0:T(8,128)S(1)}, u32[]{:S(2)}, u32[]{:S(2)}) collective-permute-start(f32[8,16,512]{2,1,0:T(8,128)S(1)} %get-tuple-element.51), channel_id=1, source_target_pairs={{0,1},{1,0},{2,3},{3,2},{4,5},{5,4},{6,7},{7,6},{8,9},{9,8},{10,11... | collective-permute-start | bytes 786440 | tf_op jit(solution)/shard_map/ppermute | solution.py:56
  102.7 3.4 %collective-permute-start.19 = (f32[16,256]{1,0:T(8,128)S(1)}, f32[16,256]{1,0:T(8,128)S(1)}, u32[]{:S(2)}, u32[]{:S(2)}) collective-permute-start(f32[16,256]{1,0:T(8,128)S(1)} %fusion.1), channel_id=1, source_target_pairs={{0,1},{1,0},{2,3},{3,2},{4,5},{5,4},{6,7},{7,6},{8,9},{9,8},{10,11... | collective-permute-start | bytes 49160 | tf_op jit(solution)/shard_map/ppermute | solution.py:56

commit v5 on v4

--- a/solution.py
+++ b/solution.py
@@ -31,8 +31,8 @@
 
 
 OUTER, INNER = np.repeat(OFFSETS, 4), np.tile(OFFSETS, 4)
-PLACE_Y = np.concatenate([OUTER, INNER]).astype(np.int32)
-PLACE_X = np.concatenate([INNER, OUTER]).astype(np.int32)
+PLACE_Y = np.concatenate([INNER, OUTER]).astype(np.int32)
+PLACE_X = np.concatenate([OUTER, INNER]).astype(np.int32)
 PLACE_Z = np.repeat(np.arange(2), 16).astype(np.int32)
 
 
@@ -62,30 +62,45 @@
         left, right, _ = lax.optimization_barrier((left, right, mark))
     low, high = up(left[:, :16], first), down(right[:, 16:], first)
     row = jnp.concatenate([piece, left, right, jnp.concatenate([low, high], axis=1)], axis=0)
-    row_left, row_right = up(row, second), down(row, second)
-    far_low, far_high = up(row_left[:2], second), down(row_right[2:], second)
+    row_right = down(row, second)
+    row_left = up(row, second)
+    far_high = down(row_right[2:], second)
+    far_low = up(row_left[:2], second)
     return [row, row_left, row_right, far_low, far_high], left
 
 
+FIRST = (0, 1, 2, 3, 8, 9, 10, 11, 4, 5, 6, 7) + tuple(range(16, 28))
+LAST = (14, 15, 12, 13) + tuple(range(28, 32))
+
+
+def put(ref, i, slot, ordered, lead):
+    row = pl.multiple_of(slot * MEM, MEM)
+    ordered[pl.ds(row, MEM), :] = ref[i, :, :HALF]
+
+    @pl.when(slot < STEPS)
+    def _():
+        ordered[pl.ds(row + SLOTS * MEM, MEM), :] = ref[i, :, :HALF]
+
+    tg = pl.multiple_of(slot * 64, 64)
+    lead[pl.ds(tg, MEM), :] = ref[i, :, HALF:HALF + SENSORS]
+    lead[pl.ds(tg + MEM, MEM), :] = ref[i, :, HALF + SENSORS:]
+
+
+def put_all(slots, order, pieces, ordered, lead):
+    where = [(ref, i) for ref in pieces for i in range(ref.shape[0])]
+    for at, (ref, i) in zip(order, where, strict=True):
+        put(ref, i, slots[at], ordered, lead)
+
+
+def place_kernel(slots, *refs):
+    put_all(slots, FIRST, refs[:6], refs[6], refs[7])
+
+
 def coupling_kernel(slots, starts, place, *refs):
-    pieces = refs[:10]
-    tiles = refs[10:12]
-    keep, send, lead_out, ordered, total, wide, lead, done = refs[12:]
-    at = 0
-    for ref in pieces:
-        for i in range(ref.shape[0]):
-            slot = slots[at]
-            row = pl.multiple_of(slot * MEM, MEM)
-            ordered[pl.ds(row, MEM), :] = ref[i, :, :HALF]
-
-            @pl.when(slot < STEPS)
-            def _():
-                ordered[pl.ds(row + SLOTS * MEM, MEM), :] = ref[i, :, :HALF]
-
-            tg = pl.multiple_of(slot * 64, 64)
-            lead[pl.ds(tg, MEM), :] = ref[i, :, HALF:HALF + SENSORS]
-            lead[pl.ds(tg + MEM, MEM), :] = ref[i, :, HALF + SENSORS:]
-            at += 1
+    pieces = refs[:4]
+    tiles = refs[4:6]
+    _, _, keep, send, ordered, lead, lead_out, total, wide, done = refs[6:]
+    put_all(slots, LAST, pieces, ordered, lead)
     store = pltpu.make_async_copy(lead, lead_out, done)
     store.start()
     zl = place[0]
@@ -190,33 +205,48 @@
     tile_far = cut(connectome, far, HALF, 1)
     tile_far = jnp.concatenate([tile_far, jnp.broadcast_to(note, (BLOCK, BLOCK))], axis=1)
 
-    own_pieces, _ = ring_gather(own, "x", "y", partner)
-    other_pieces, early = ring_gather(partner, "y", "x")
+    own_pieces, _ = ring_gather(own, "y", "x", partner)
+    other_pieces, early = ring_gather(partner, "x", "y")
     pieces = own_pieces + other_pieces
     tile_far, _ = lax.optimization_barrier((tile_far, early))
     tile_other = swap(tile_far, "zl")
     start_other = tile_other[:1, HALF:HALF + BLOCKS].astype(jnp.int32)
     starts = jnp.concatenate([start_own, start_other], axis=0)
 
-    keep, send, lead = pl.pallas_call(
+    first = [own_pieces[0], own_pieces[2], own_pieces[1], *other_pieces[:3]]
+    last = [own_pieces[4], own_pieces[3], *other_pieces[3:]]
+    ordered, lead = pl.pallas_call(
+        place_kernel,
+        out_shape=(
+            jax.ShapeDtypeStruct(((SLOTS + STEPS) * MEM, HALF), jnp.bfloat16),
+            jax.ShapeDtypeStruct((SLOTS * 64, SENSORS), jnp.bfloat16),
+        ),
+        in_specs=smem(1) + vmem(6),
+        out_specs=tuple(vmem(2)),
+        compiler_params=pltpu.CompilerParams(vmem_limit_bytes=24 << 20),
+        name="place",
+    )(slots, *first)
+    keep, send, ordered, lead, lead_out = pl.pallas_call(
         coupling_kernel,
         out_shape=(
             jax.ShapeDtypeStruct((8, 16, STEPS * MEM), jnp.float32),
             jax.ShapeDtypeStruct((8, 16, STEPS * MEM), jnp.float32),
+            jax.ShapeDtypeStruct(((SLOTS + STEPS) * MEM, HALF), jnp.bfloat16),
+            jax.ShapeDtypeStruct((SLOTS * 64, SENSORS), jnp.bfloat16),
             jax.ShapeDtypeStruct((SLOTS * 64, SENSORS), jnp.bfloat16),
         ),
-        in_specs=smem(3) + vmem(12),
-        out_specs=(*vmem(2), pl.BlockSpec(memory_space=pl.ANY)),
+        in_specs=smem(3) + vmem(8),
+        out_specs=(*vmem(4), pl.BlockSpec(memory_space=pl.ANY)),
         scratch_shapes=[
-            pltpu.VMEM(((SLOTS + STEPS) * MEM, HALF), jnp.bfloat16),
             pltpu.VMEM((BLOCK, STEPS * MEM), jnp.float32),
             pltpu.VMEM((STEPS * MEM, BLOCK), jnp.float32),
-            pltpu.VMEM((SLOTS * 64, SENSORS), jnp.bfloat16),
             pltpu.SemaphoreType.DMA,
         ],
+        input_output_aliases={9: 2, 10: 3},
         compiler_params=pltpu.CompilerParams(vmem_limit_bytes=24 << 20),
         name="coupling",
-    )(slots, starts, place, *pieces, tile_own, tile_other)
+    )(slots, starts, place, *last, tile_own, tile_other, ordered, lead)
+    lead = lead_out
 
     joined = keep + swap(send, "c")
     joined, begin, outside = lax.optimization_barrier((joined, begin, outside_afferent[None, :]))

time: 107 us -> 105 us (0.981)
  waiting for transfers between devices: 26.4 us -> 22.8 us
  starting transfers between devices: 32.4 us -> 35.5 us
  blocking collectives: 37.7 us -> 36.1 us
    ppermute x8, waiting for transfers between devices: 20.8 us -> 0.22 us  [down(): return lax.ppermute(v, axis, [(i, (i + 3) % 4) for i in range(4)])]
    ppermute x8, waiting for transfers between devices: 3.52 us -> 20.7 us  [up(): return lax.ppermute(v, axis, [(i, (i + 1) % 4) for i in range(4)])]
    all_to_all x1, blocking collectives: 22.9 us -> 20.6 us  [body(): lax.all_to_all(potential.reshape(MEM * 4, 2, 128), TGT + ('zh',), 0, 0, t...]
    ppermute x8, starting transfers between devices: 8.69 us -> 9.96 us  [up(): return lax.ppermute(v, axis, [(i, (i + 1) % 4) for i in range(4)])]
    pallas_call x0 -> x1, Pallas kernels: none -> 1.23 us  [body(): pl.pallas_call(place_kernel, out_shape=(jax.ShapeDtypeStruct(((SLOTS + ST...]
  transfers between devices with their start and end apart: 20 -> 20, of which waited for: 9 -> 9; matrix products, arithmetic and copies ran while one was open for 2% -> 2% of each run, Pallas kernels for 0% -> 1%
where the time goes in v5:
time: 105 us
  blocking collectives  36.1 us (34%)
  starting transfers between devices  35.5 us (34%)
  waiting for transfers between devices  22.8 us (22%)
  Pallas kernels  4.55 us (4%)
  local copies, waits for them, and re-layouts  3.21 us (3%)
  between operations  1.54 us (1%)
  other arithmetic  1.2 us (1%)
    ppermute x8, waiting for transfers between devices, up(): return lax.ppermute(v, axis, [(i, (i + 1) % 4) for i in range(4)])  20.7 us
    all_to_all x1, blocking collectives, body(): lax.all_to_all(potential.reshape(MEM * 4, 2, 128), TGT + ('zh',), 0, 0, t...  20.6 us
    all_to_all x1, blocking collectives, body(): parts = lax.all_to_all(joined, ('zl', 'zh'), 0, 0, tiled=True)  15.5 us
    ppermute x8, starting transfers between devices, down(): return lax.ppermute(v, axis, [(i, (i + 3) % 4) for i in range(4)])  13.5 us
    ppermute x4, starting transfers between devices, swap(): return lax.ppermute(v, axis, [(0, 1), (1, 0)])  12 us
    ppermute x8, starting transfers between devices, up(): return lax.ppermute(v, axis, [(i, (i + 1) % 4) for i in range(4)])  9.96 us
    pallas_call x1, Pallas kernels, body(): pl.pallas_call(coupling_kernel, out_shape=(jax.ShapeDtypeStruct((8, 16, S...  2.81 us
  transfers between devices with their start and end apart: 20, of which 9 were waited for; matrix products, arithmetic and copies ran while one was open for 2% of the time, Pallas kernels for 1%

profile of v5, /device:TPU:1, one launch (start us, length us, event | category | flops | bytes accessed | tf_op | source)
XLA Modules:
  0.0 105.2 jit_solution(11370856736730994046)
XLA Ops:
  0.7 0.9 constant_dynamic-slice_fusion
  1.8 2.6 %collective-permute-start = (bf16[1,32,3712]{2,1,0:T(8,128)(2,1)S(1)}, bf16[1,32,3712]{2,1,0:T(8,128)(2,1)S(1)}, u32[]{:S(2)}, u32[]{:S(2)}) collective-permute-start(bf16[1,32,3712]{2,1,0:T(8,128)(2,1)S(1)} %pad_maximum_fusion.2), channel_id=1, source_target_pairs={{0,8},{8,0},{1,9},{9,1},{2,10},{10,2},{3,11},{11,3},{4,12},{12,4},... | collective-permute-start | bytes 712712 | tf_op jit(solution)/shard_map/ppermute | solution.py:56
  5.2 1.4 %collective-permute-start.3 = (bf16[1,32,3712]{2,1,0:T(8,128)(2,1)S(1)}, bf16[1,32,3712]{2,1,0:T(8,128)(2,1)S(1)}, u32[]{:S(2)}, u32[]{:S(2)}) collective-permute-start(bf16[1,32,3712]{2,1,0:T(8,128)(2,1)S(1)} %pad_maximum_fusion.1), channel_id=1, source_target_pairs={{0,64},{64,128},{128,192},{192,0},{1,65},{65,129},{129,193},{193,1... | collective-permute-start | bytes 712712 | tf_op jit(solution)/shard_map/ppermute | solution.py:40
  6.5 1.5 %collective-permute-start.4 = (bf16[1,32,3712]{2,1,0:T(8,128)(2,1)S(1)}, bf16[1,32,3712]{2,1,0:T(8,128)(2,1)S(1)}, u32[]{:S(2)}, u32[]{:S(2)}) collective-permute-start(bf16[1,32,3712]{2,1,0:T(8,128)(2,1)S(1)} %pad_maximum_fusion.1), channel_id=1, source_target_pairs={{0,192},{64,0},{128,64},{192,128},{1,193},{65,1},{129,65},{193,129... | collective-permute-start | bytes 712712 | tf_op jit(solution)/shard_map/ppermute | solution.py:44
  8.1 0.7 collective-permute-done
  8.8 2.1 %collective-permute-start.1 = (bf16[1,32,3712]{2,1,0:T(8,128)(2,1)S(1)}, bf16[1,32,3712]{2,1,0:T(8,128)(2,1)S(1)}, u32[]{:S(2)}, u32[]{:S(2)}) collective-permute-start(bf16[1,32,3712]{2,1,0:T(8,128)(2,1)S(1)} %collective-permute-done), channel_id=1, source_target_pairs={{0,16},{16,32},{32,48},{48,0},{1,17},{17,33},{33,49},{49,1},{2,18}... | collective-permute-start | bytes 712712 | tf_op jit(solution)/shard_map/ppermute | solution.py:40
  10.9 1.3 %collective-permute-start.11 = (bf16[1,32,3712]{2,1,0:T(8,128)(2,1)S(1)}, bf16[1,32,3712]{2,1,0:T(8,128)(2,1)S(1)}, u32[]{:S(2)}, u32[]{:S(2)}) collective-permute-start(bf16[1,32,3712]{2,1,0:T(8,128)(2,1)S(1)} %collective-permute-done), channel_id=1, source_target_pairs={{0,48},{16,0},{32,16},{48,32},{1,49},{17,1},{33,17},{49,33},{2,50}... | collective-permute-start | bytes 712712 | tf_op jit(solution)/shard_map/ppermute | solution.py:44
  12.2 0.6 constant_dynamic-slice_fusion.2
  12.9 1.5 %collective-permute-start.5 = (bf16[1,16,3712]{2,1,0:T(8,128)(2,1)S(1)}, bf16[1,16,3712]{2,1,0:T(8,128)(2,1)S(1)}, u32[]{:S(2)}, u32[]{:S(2)}) collective-permute-start(bf16[1,16,3712]{2,1,0:T(8,128)(2,1)S(1)} %slice.38), channel_id=1, source_target_pairs={{0,64},{64,128},{128,192},{192,0},{1,65},{65,129},{129,193},{193,1... | collective-permute-start | bytes 356360 | tf_op jit(solution)/shard_map/ppermute | solution.py:40
  14.5 1.5 %collective-permute-start.6 = (bf16[1,16,3712]{2,1,0:T(8,128)(2,1)S(1)}, bf16[1,16,3712]{2,1,0:T(8,128)(2,1)S(1)}, u32[]{:S(2)}, u32[]{:S(2)}) collective-permute-start(bf16[1,16,3712]{2,1,0:T(8,128)(2,1)S(1)} %slice.39), channel_id=1, source_target_pairs={{0,192},{64,0},{128,64},{192,128},{1,193},{65,1},{129,65},{193,129... | collective-permute-start | bytes 356360 | tf_op jit(solution)/shard_map/ppermute | solution.py:44
  16.3 0.8 collective-permute-start.12
  17.2 2.0 %collective-permute-start.13 = (bf16[1,16,3712]{2,1,0:T(8,128)(2,1)S(1)}, bf16[1,16,3712]{2,1,0:T(8,128)(2,1)S(1)}, u32[]{:S(2)}, u32[]{:S(2)}) collective-permute-start(bf16[1,16,3712]{2,1,0:T(8,128)(2,1)S(1)} %slice.50), channel_id=1, source_target_pairs={{0,48},{16,0},{32,16},{48,32},{1,49},{17,1},{33,17},{49,33},{2,50}... | collective-permute-start | bytes 356360 | tf_op jit(solution)/shard_map/ppermute | solution.py:44
  19.3 1.6 %collective-permute-start.7 = (bf16[4,32,3712]{2,1,0:T(8,128)(2,1)S(1)}, bf16[4,32,3712]{2,1,0:T(8,128)(2,1)S(1)}, u32[]{:S(2)}, u32[]{:S(2)}) collective-permute-start(bf16[4,32,3712]{2,1,0:T(8,128)(2,1)S(1)} %maximum_maximum_fusion.refs_0_), channel_id=1, source_target_pairs={{0,48},{16,0},{32,16},{48,32},{1,49},{17,1},{33,17},{49,33},{2,50}... | collective-permute-start | bytes 2850824 | tf_op jit(solution)/shard_map/ppermute | solution.py:44
  21.4 1.9 %collective-permute-start.14 = (bf16[4,32,3712]{2,1,0:T(8,128)(2,1)S(1)}, bf16[4,32,3712]{2,1,0:T(8,128)(2,1)S(1)}, u32[]{:S(2)}, u32[]{:S(2)}) collective-permute-start(bf16[4,32,3712]{2,1,0:T(8,128)(2,1)S(1)} %maximum_maximum_fusion.1.refs_3_), channel_id=1, source_target_pairs={{0,64},{64,128},{128,192},{192,0},{1,65},{65,129},{129,193},{193,1... | collective-permute-start | bytes 2850824 | tf_op jit(solution)/shard_map/ppermute | solution.py:40
  23.3 1.5 %collective-permute-start.16 = (bf16[4,32,3712]{2,1,0:T(8,128)(2,1)S(1)}, bf16[4,32,3712]{2,1,0:T(8,128)(2,1)S(1)}, u32[]{:S(2)}, u32[]{:S(2)}) collective-permute-start(bf16[4,32,3712]{2,1,0:T(8,128)(2,1)S(1)} %maximum_maximum_fusion.1.refs_3_), channel_id=1, source_target_pairs={{0,192},{64,0},{128,64},{192,128},{1,193},{65,1},{129,65},{193,129... | collective-permute-start | bytes 2850824 | tf_op jit(solution)/shard_map/ppermute | solution.py:44
  25.0 1.1 %collective-permute-start.2 = (bf16[128,3328]{1,0:T(8,128)(2,1)S(1)}, bf16[128,3328]{1,0:T(8,128)(2,1)S(1)}, u32[]{:S(2)}, u32[]{:S(2)}) collective-permute-start(bf16[128,3328]{1,0:T(8,128)(2,1)S(1)} %pad_maximum_fusion), channel_id=1, source_target_pairs={{0,8},{8,0},{1,9},{9,1},{2,10},{10,2},{3,11},{11,3},{4,12},{12,4},... | collective-permute-start | bytes 2555912 | tf_op jit(solution)/shard_map/ppermute | solution.py:56
  26.2 15.0 %collective-permute-done.9.refs_2_ = bf16[4,32,3712]{2,1,0:T(8,128)(2,1)S(1)} collective-permute-done((bf16[4,32,3712]{2,1,0:T(8,128)(2,1)S(1)}, bf16[4,32,3712]{2,1,0:T(8,128)(2,1)S(1)}, u32[]{:S(2)}, u32[]{:S(2)}) %collective-permute-start.9) | collective-permute-done | bytes 950304 | tf_op jit(solution)/shard_map/ppermute | solution.py:40
  41.6 2.7 %collective-permute-start.8 = (bf16[2,32,3712]{2,1,0:T(8,128)(2,1)S(1)}, bf16[2,32,3712]{2,1,0:T(8,128)(2,1)S(1)}, u32[]{:S(2)}, u32[]{:S(2)}) collective-permute-start(bf16[2,32,3712]{2,1,0:T(8,128)(2,1)S(1)} %slice.47), channel_id=1, source_target_pairs={{0,48},{16,0},{32,16},{48,32},{1,49},{17,1},{33,17},{49,33},{2,50}... | collective-permute-start | bytes 1425416 | tf_op jit(solution)/shard_map/ppermute | solution.py:44
  44.3 1.9 %collective-permute-start.15 = (bf16[2,32,3712]{2,1,0:T(8,128)(2,1)S(1)}, bf16[2,32,3712]{2,1,0:T(8,128)(2,1)S(1)}, u32[]{:S(2)}, u32[]{:S(2)}) collective-permute-start(bf16[2,32,3712]{2,1,0:T(8,128)(2,1)S(1)} %slice.51), channel_id=1, source_target_pairs={{0,64},{64,128},{128,192},{192,0},{1,65},{65,129},{129,193},{193,1... | collective-permute-start | bytes 1425416 | tf_op jit(solution)/shard_map/ppermute | solution.py:40
  46.3 1.4 %collective-permute-start.17 = (bf16[2,32,3712]{2,1,0:T(8,128)(2,1)S(1)}, bf16[2,32,3712]{2,1,0:T(8,128)(2,1)S(1)}, u32[]{:S(2)}, u32[]{:S(2)}) collective-permute-start(bf16[2,32,3712]{2,1,0:T(8,128)(2,1)S(1)} %slice.52), channel_id=1, source_target_pairs={{0,192},{64,0},{128,64},{192,128},{1,193},{65,1},{129,65},{193,129... | collective-permute-start | bytes 1425416 | tf_op jit(solution)/shard_map/ppermute | solution.py:44
  47.8 1.2 %place.1 = (bf16[1536,3200]{1,0:T(8,128)(2,1)S(1)}, bf16[2048,256]{1,0:T(8,128)(2,1)S(1)}) custom-call(s32[32]{0:T(128)S(1)} %xor_add_fusion.slots, bf16[4,32,3712]{2,1,0:T(8,128)(2,1)S(1)} %maximum_maximum_fusion.refs_0_, bf16[4,32,3712]{2,1,0:T(8,128)(2,1)S(1)} %collective-permute-done.7.refs_1_, bf16[4,32,3712]{2,1,0:T(8,128)(2,1)S(1)} %collective-permute-done.9.refs_2_, ...), custom_call_target="tpu_custom_call" | custom-call | tf_op jit(solution)/shard_map/place/pallas_call | solution.py:218
  49.0 1.8 %collective-permute-done.10.refs_1_ = bf16[2,32,3712]{2,1,0:T(8,128)(2,1)S(1)} collective-permute-done((bf16[2,32,3712]{2,1,0:T(8,128)(2,1)S(1)}, bf16[2,32,3712]{2,1,0:T(8,128)(2,1)S(1)}, u32[]{:S(2)}, u32[]{:S(2)}) %collective-permute-start.10) | collective-permute-done | bytes 475168 | tf_op jit(solution)/shard_map/ppermute | solution.py:40
  50.8 3.2 %collective-permute-done.15.refs_2_ = bf16[2,32,3712]{2,1,0:T(8,128)(2,1)S(1)} collective-permute-done((bf16[2,32,3712]{2,1,0:T(8,128)(2,1)S(1)}, bf16[2,32,3712]{2,1,0:T(8,128)(2,1)S(1)}, u32[]{:S(2)}, u32[]{:S(2)}) %collective-permute-start.15) | collective-permute-done | bytes 475168 | tf_op jit(solution)/shard_map/ppermute | solution.py:40
  54.1 2.8 %coupling.1 = (f32[8,16,512]{2,1,0:T(8,128)S(1)}, f32[8,16,512]{2,1,0:T(8,128)S(1)}, bf16[1536,3200]{1,0:T(8,128)(2,1)S(1)}, bf16[2048,256]{1,0:T(8,128)(2,1)S(1)}, bf16[2048,256]{1,0:T(8,128)(2,1)S(1)}) custom-call(s32[32]{0:T(128)S(1)} %xor_add_fusion.slots, s32[2,25]{1,0:T(2,128)S(1)} %pad_add_fusion.starts, ...), custom_call_target="tpu_custom_call", output_to_operand_aliasing={{2}: (9, {}), {3}: (10, {})} | custom-call | tf_op jit(solution)/shard_map/coupling/pallas_call | solution.py:229
  57.0 5.7 %collective-permute-start.18 = (f32[8,16,512]{2,1,0:T(8,128)S(1)}, f32[8,16,512]{2,1,0:T(8,128)S(1)}, u32[]{:S(2)}, u32[]{:S(2)}) collective-permute-start(f32[8,16,512]{2,1,0:T(8,128)S(1)} %get-tuple-element.55), channel_id=1, source_target_pairs={{0,1},{1,0},{2,3},{3,2},{4,5},{5,4},{6,7},{7,6},{8,9},{9,8},{10,11... | collective-permute-start | bytes 786440 | tf_op jit(solution)/shard_map/ppermute | solution.py:56
  62.8 1.1 %collective-permute-done.18 = f32[8,16,512]{2,1,0:T(8,128)S(1)} collective-permute-done((f32[8,16,512]{2,1,0:T(8,128)S(1)}, f32[8,16,512]{2,1,0:T(8,128)S(1)}, u32[]{:S(2)}, u32[]{:S(2)}) %collective-permute-start.18) | collective-permute-done | bytes 262176 | tf_op jit(solution)/shard_map/ppermute | solution.py:56
  63.9 15.5 %all_to_all.10.parts = f32[8,16,512]{2,1,0:T(8,128)S(1)} all-to-all(f32[8,16,512]{2,1,0:T(8,128)S(1)} %add.36), channel_id=1, replica_groups=mesh['y'=4,'x'=4,'zl'=2,'zh'=4,'c'=2] {'zl','zh'}, dimensions={0} | all-to-all | bytes 524288 | tf_op jit(solution)/shard_map/all_to_all | solution.py:253
  79.4 0.5 integrate.1
  79.9 20.6 %all_to_all.11 = bf16[128,2,128]{2,1,0:T(2,128)(2,1)S(1)} all-to-all(bf16[128,2,128]{2,1,0:T(2,128)(2,1)S(1)} %bitcast.22), channel_id=1, replica_groups=mesh['y'=4,'x'=4,'zl'=2,'zh'=4,'c'=2] {'y','x','zl','zh'}, dimensions={0} | all-to-all | bytes 131072 | tf_op jit(solution)/shard_map/all_to_all | solution.py:267
  101.2 2.6 %collective-permute-start.19 = (f32[16,256]{1,0:T(8,128)S(1)}, f32[16,256]{1,0:T(8,128)S(1)}, u32[]{:S(2)}, u32[]{:S(2)}) collective-permute-start(f32[16,256]{1,0:T(8,128)S(1)} %fusion.1), channel_id=1, source_target_pairs={{0,1},{1,0},{2,3},{3,2},{4,5},{5,4},{6,7},{7,6},{8,9},{9,8},{10,11... | collective-permute-start | bytes 49160 | tf_op jit(solution)/shard_map/ppermute | solution.py:56
  103.8 0.7 copy.17
  104.6 0.6 add_bitcast_fusion
  (61 shorter events, 3.2 us)
Async XLA Ops:
  0.6 1.0 copy-start
  0.6 11.6 %copy-start.2 = (bf16[128,6400]{1,0:T(8,128)(2,1)S(1)}, bf16[128,6400]{1,0:T(8,128)(2,1)}, u32[]{:S(2)}) copy-start(bf16[128,6400]{1,0:T(8,128)(2,1)} %param.10) | copy-start | bytes 4915204
  0.7 4.5 %copy-start.7 = (s32[1,50]{1,0:T(1,128)S(1)}, s32[1,50]{1,0:T(1,128)}, u32[]{:S(2)}) copy-start(s32[1,50]{1,0:T(1,128)} %param.12) | copy-start | bytes 604
  1.8 7.0 %collective-permute-start = (bf16[1,32,3712]{2,1,0:T(8,128)(2,1)S(1)}, bf16[1,32,3712]{2,1,0:T(8,128)(2,1)S(1)}, u32[]{:S(2)}, u32[]{:S(2)}) collective-permute-start(bf16[1,32,3712]{2,1,0:T(8,128)(2,1)S(1)} %pad_maximum_fusion.2), channel_id=1, source_target_pairs={{0,8},{8,0},{1,9},{9,1},{2,10},{10,2},{3,11},{11,3},{4,12},{12,4},... | collective-permute-start | bytes 712712 | tf_op jit(solution)/shard_map/ppermute | solution.py:56
  5.2 7.7 %collective-permute-start.3 = (bf16[1,32,3712]{2,1,0:T(8,128)(2,1)S(1)}, bf16[1,32,3712]{2,1,0:T(8,128)(2,1)S(1)}, u32[]{:S(2)}, u32[]{:S(2)}) collective-permute-start(bf16[1,32,3712]{2,1,0:T(8,128)(2,1)S(1)} %pad_maximum_fusion.1), channel_id=1, source_target_pairs={{0,64},{64,128},{128,192},{192,0},{1,65},{65,129},{129,193},{193,1... | collective-permute-start | bytes 712712 | tf_op jit(solution)/shard_map/ppermute | solution.py:40
  6.5 6.4 %collective-permute-start.4 = (bf16[1,32,3712]{2,1,0:T(8,128)(2,1)S(1)}, bf16[1,32,3712]{2,1,0:T(8,128)(2,1)S(1)}, u32[]{:S(2)}, u32[]{:S(2)}) collective-permute-start(bf16[1,32,3712]{2,1,0:T(8,128)(2,1)S(1)} %pad_maximum_fusion.1), channel_id=1, source_target_pairs={{0,192},{64,0},{128,64},{192,128},{1,193},{65,1},{129,65},{193,129... | collective-permute-start | bytes 712712 | tf_op jit(solution)/shard_map/ppermute | solution.py:44
  8.8 7.5 %collective-permute-start.1 = (bf16[1,32,3712]{2,1,0:T(8,128)(2,1)S(1)}, bf16[1,32,3712]{2,1,0:T(8,128)(2,1)S(1)}, u32[]{:S(2)}, u32[]{:S(2)}) collective-permute-start(bf16[1,32,3712]{2,1,0:T(8,128)(2,1)S(1)} %collective-permute-done), channel_id=1, source_target_pairs={{0,16},{16,32},{32,48},{48,0},{1,17},{17,33},{33,49},{49,1},{2,18}... | collective-permute-start | bytes 712712 | tf_op jit(solution)/shard_map/ppermute | solution.py:40
  10.9 6.2 %collective-permute-start.11 = (bf16[1,32,3712]{2,1,0:T(8,128)(2,1)S(1)}, bf16[1,32,3712]{2,1,0:T(8,128)(2,1)S(1)}, u32[]{:S(2)}, u32[]{:S(2)}) collective-permute-start(bf16[1,32,3712]{2,1,0:T(8,128)(2,1)S(1)} %collective-permute-done), channel_id=1, source_target_pairs={{0,48},{16,0},{32,16},{48,32},{1,49},{17,1},{33,17},{49,33},{2,50}... | collective-permute-start | bytes 712712 | tf_op jit(solution)/shard_map/ppermute | solution.py:44
  12.9 6.3 %collective-permute-start.5 = (bf16[1,16,3712]{2,1,0:T(8,128)(2,1)S(1)}, bf16[1,16,3712]{2,1,0:T(8,128)(2,1)S(1)}, u32[]{:S(2)}, u32[]{:S(2)}) collective-permute-start(bf16[1,16,3712]{2,1,0:T(8,128)(2,1)S(1)} %slice.38), channel_id=1, source_target_pairs={{0,64},{64,128},{128,192},{192,0},{1,65},{65,129},{129,193},{193,1... | collective-permute-start | bytes 356360 | tf_op jit(solution)/shard_map/ppermute | solution.py:40
  14.5 4.7 %collective-permute-start.6 = (bf16[1,16,3712]{2,1,0:T(8,128)(2,1)S(1)}, bf16[1,16,3712]{2,1,0:T(8,128)(2,1)S(1)}, u32[]{:S(2)}, u32[]{:S(2)}) collective-permute-start(bf16[1,16,3712]{2,1,0:T(8,128)(2,1)S(1)} %slice.39), channel_id=1, source_target_pairs={{0,192},{64,0},{128,64},{192,128},{1,193},{65,1},{129,65},{193,129... | collective-permute-start | bytes 356360 | tf_op jit(solution)/shard_map/ppermute | solution.py:44
  16.3 5.0 %collective-permute-start.12 = (bf16[1,16,3712]{2,1,0:T(8,128)(2,1)S(1)}, bf16[1,16,3712]{2,1,0:T(8,128)(2,1)S(1)}, u32[]{:S(2)}, u32[]{:S(2)}) collective-permute-start(bf16[1,16,3712]{2,1,0:T(8,128)(2,1)S(1)} %slice.49), channel_id=1, source_target_pairs={{0,16},{16,32},{32,48},{48,0},{1,17},{17,33},{33,49},{49,1},{2,18}... | collective-permute-start | bytes 356360 | tf_op jit(solution)/shard_map/ppermute | solution.py:40
  17.2 4.1 %collective-permute-start.13 = (bf16[1,16,3712]{2,1,0:T(8,128)(2,1)S(1)}, bf16[1,16,3712]{2,1,0:T(8,128)(2,1)S(1)}, u32[]{:S(2)}, u32[]{:S(2)}) collective-permute-start(bf16[1,16,3712]{2,1,0:T(8,128)(2,1)S(1)} %slice.50), channel_id=1, source_target_pairs={{0,48},{16,0},{32,16},{48,32},{1,49},{17,1},{33,17},{49,33},{2,50}... | collective-permute-start | bytes 356360 | tf_op jit(solution)/shard_map/ppermute | solution.py:44
  19.3 22.2 %collective-permute-start.7 = (bf16[4,32,3712]{2,1,0:T(8,128)(2,1)S(1)}, bf16[4,32,3712]{2,1,0:T(8,128)(2,1)S(1)}, u32[]{:S(2)}, u32[]{:S(2)}) collective-permute-start(bf16[4,32,3712]{2,1,0:T(8,128)(2,1)S(1)} %maximum_maximum_fusion.refs_0_), channel_id=1, source_target_pairs={{0,48},{16,0},{32,16},{48,32},{1,49},{17,1},{33,17},{49,33},{2,50}... | collective-permute-start | bytes 2850824 | tf_op jit(solution)/shard_map/ppermute | solution.py:44
  20.9 20.4 %collective-permute-start.9 = (bf16[4,32,3712]{2,1,0:T(8,128)(2,1)S(1)}, bf16[4,32,3712]{2,1,0:T(8,128)(2,1)S(1)}, u32[]{:S(2)}, u32[]{:S(2)}) collective-permute-start(bf16[4,32,3712]{2,1,0:T(8,128)(2,1)S(1)} %maximum_maximum_fusion.refs_0_), channel_id=1, source_target_pairs={{0,16},{16,32},{32,48},{48,0},{1,17},{17,33},{33,49},{49,1},{2,18}... | collective-permute-start | bytes 2850824 | tf_op jit(solution)/shard_map/ppermute | solution.py:40
  21.4 22.9 %collective-permute-start.14 = (bf16[4,32,3712]{2,1,0:T(8,128)(2,1)S(1)}, bf16[4,32,3712]{2,1,0:T(8,128)(2,1)S(1)}, u32[]{:S(2)}, u32[]{:S(2)}) collective-permute-start(bf16[4,32,3712]{2,1,0:T(8,128)(2,1)S(1)} %maximum_maximum_fusion.1.refs_3_), channel_id=1, source_target_pairs={{0,64},{64,128},{128,192},{192,0},{1,65},{65,129},{129,193},{193,1... | collective-permute-start | bytes 2850824 | tf_op jit(solution)/shard_map/ppermute | solution.py:40
  23.3 22.9 %collective-permute-start.16 = (bf16[4,32,3712]{2,1,0:T(8,128)(2,1)S(1)}, bf16[4,32,3712]{2,1,0:T(8,128)(2,1)S(1)}, u32[]{:S(2)}, u32[]{:S(2)}) collective-permute-start(bf16[4,32,3712]{2,1,0:T(8,128)(2,1)S(1)} %maximum_maximum_fusion.1.refs_3_), channel_id=1, source_target_pairs={{0,192},{64,0},{128,64},{192,128},{1,193},{65,1},{129,65},{193,129... | collective-permute-start | bytes 2850824 | tf_op jit(solution)/shard_map/ppermute | solution.py:44
  25.0 22.6 %copy-start.4 = (s32[32]{0:T(128)S(1)}, s32[32]{0:T(128)}, u32[]{:S(2)}) copy-start(s32[32]{0:T(128)} %constant.46.clone) | copy-start | bytes 388
  25.0 22.6 %copy-start.5 = (s32[32]{0:T(128)S(1)}, s32[32]{0:T(128)}, u32[]{:S(2)}) copy-start(s32[32]{0:T(128)} %constant.47.clone) | copy-start | bytes 388
  25.0 22.6 %copy-start.6 = (s32[32]{0:T(128)S(1)}, s32[32]{0:T(128)}, u32[]{:S(2)}) copy-start(s32[32]{0:T(128)} %constant.48.clone) | copy-start | bytes 388
  25.0 22.7 %collective-permute-start.2 = (bf16[128,3328]{1,0:T(8,128)(2,1)S(1)}, bf16[128,3328]{1,0:T(8,128)(2,1)S(1)}, u32[]{:S(2)}, u32[]{:S(2)}) collective-permute-start(bf16[128,3328]{1,0:T(8,128)(2,1)S(1)} %pad_maximum_fusion), channel_id=1, source_target_pairs={{0,8},{8,0},{1,9},{9,1},{2,10},{10,2},{3,11},{11,3},{4,12},{12,4},... | collective-permute-start | bytes 2555912 | tf_op jit(solution)/shard_map/ppermute | solution.py:56
  41.2 9.5 %collective-permute-start.10 = (bf16[2,32,3712]{2,1,0:T(8,128)(2,1)S(1)}, bf16[2,32,3712]{2,1,0:T(8,128)(2,1)S(1)}, u32[]{:S(2)}, u32[]{:S(2)}) collective-permute-start(bf16[2,32,3712]{2,1,0:T(8,128)(2,1)S(1)} %slice.48), channel_id=1, source_target_pairs={{0,16},{16,32},{32,48},{48,0},{1,17},{17,33},{33,49},{49,1},{2,18}... | collective-permute-start | bytes 1425416 | tf_op jit(solution)/shard_map/ppermute | solution.py:40
  41.6 9.2 %collective-permute-start.8 = (bf16[2,32,3712]{2,1,0:T(8,128)(2,1)S(1)}, bf16[2,32,3712]{2,1,0:T(8,128)(2,1)S(1)}, u32[]{:S(2)}, u32[]{:S(2)}) collective-permute-start(bf16[2,32,3712]{2,1,0:T(8,128)(2,1)S(1)} %slice.47), channel_id=1, source_target_pairs={{0,48},{16,0},{32,16},{48,32},{1,49},{17,1},{33,17},{49,33},{2,50}... | collective-permute-start | bytes 1425416 | tf_op jit(solution)/shard_map/ppermute | solution.py:44
  44.3 9.6 %collective-permute-start.15 = (bf16[2,32,3712]{2,1,0:T(8,128)(2,1)S(1)}, bf16[2,32,3712]{2,1,0:T(8,128)(2,1)S(1)}, u32[]{:S(2)}, u32[]{:S(2)}) collective-permute-start(bf16[2,32,3712]{2,1,0:T(8,128)(2,1)S(1)} %slice.51), channel_id=1, source_target_pairs={{0,64},{64,128},{128,192},{192,0},{1,65},{65,129},{129,193},{193,1... | collective-permute-start | bytes 1425416 | tf_op jit(solution)/shard_map/ppermute | solution.py:40
  46.3 7.9 %collective-permute-start.17 = (bf16[2,32,3712]{2,1,0:T(8,128)(2,1)S(1)}, bf16[2,32,3712]{2,1,0:T(8,128)(2,1)S(1)}, u32[]{:S(2)}, u32[]{:S(2)}) collective-permute-start(bf16[2,32,3712]{2,1,0:T(8,128)(2,1)S(1)} %slice.52), channel_id=1, source_target_pairs={{0,192},{64,0},{128,64},{192,128},{1,193},{65,1},{129,65},{193,129... | collective-permute-start | bytes 1425416 | tf_op jit(solution)/shard_map/ppermute | solution.py:44
  54.1 8.5 %copy-start.3 = (f32[6,32,128]{2,1,0:T(8,128)S(1)}, f32[6,32,128]{2,1,0:T(8,128)}, u32[]{:S(2)}) copy-start(f32[6,32,128]{2,1,0:T(8,128)} %param.15) | copy-start | bytes 294916
  54.1 25.3 %copy-start.1 = (f32[32]{0:T(128)S(1)}, f32[32]{0:T(128)}, u32[]{:S(2)}) copy-start(f32[32]{0:T(128)} %param.14) | copy-start | bytes 388
  57.0 6.9 %collective-permute-start.18 = (f32[8,16,512]{2,1,0:T(8,128)S(1)}, f32[8,16,512]{2,1,0:T(8,128)S(1)}, u32[]{:S(2)}, u32[]{:S(2)}) collective-permute-start(f32[8,16,512]{2,1,0:T(8,128)S(1)} %get-tuple-element.55), channel_id=1, source_target_pairs={{0,1},{1,0},{2,3},{3,2},{4,5},{5,4},{6,7},{7,6},{8,9},{9,8},{10,11... | collective-permute-start | bytes 786440 | tf_op jit(solution)/shard_map/ppermute | solution.py:56
  101.2 3.4 %collective-permute-start.19 = (f32[16,256]{1,0:T(8,128)S(1)}, f32[16,256]{1,0:T(8,128)S(1)}, u32[]{:S(2)}, u32[]{:S(2)}) collective-permute-start(f32[16,256]{1,0:T(8,128)S(1)} %fusion.1), channel_id=1, source_target_pairs={{0,1},{1,0},{2,3},{3,2},{4,5},{5,4},{6,7},{7,6},{8,9},{9,8},{10,11... | collective-permute-start | bytes 49160 | tf_op jit(solution)/shard_map/ppermute | solution.py:56

commit v6 on v5

--- a/solution.py
+++ b/solution.py
@@ -205,7 +205,7 @@
     tile_far = cut(connectome, far, HALF, 1)
     tile_far = jnp.concatenate([tile_far, jnp.broadcast_to(note, (BLOCK, BLOCK))], axis=1)
 
-    own_pieces, _ = ring_gather(own, "y", "x", partner)
+    own_pieces, _ = ring_gather(own, "y", "x")
     other_pieces, early = ring_gather(partner, "x", "y")
     pieces = own_pieces + other_pieces
     tile_far, _ = lax.optimization_barrier((tile_far, early))

time: 105 us -> 105 us (level)
  waiting for transfers between devices: 22.8 us -> 24.5 us
  starting transfers between devices: 35.5 us -> 34.4 us
    ppermute x8, waiting for transfers between devices: 0.22 us -> 1.35 us  [down(): return lax.ppermute(v, axis, [(i, (i + 3) % 4) for i in range(4)])]
where the time goes in v6:
time: 105 us
  blocking collectives  35.6 us (34%)
  starting transfers between devices  34.4 us (33%)
  waiting for transfers between devices  24.5 us (23%)
  Pallas kernels  4.55 us (4%)
  local copies, waits for them, and re-layouts  3.21 us (3%)
  between operations  1.54 us (1%)
  other arithmetic  1.2 us (1%)
    ppermute x8, waiting for transfers between devices, up(): return lax.ppermute(v, axis, [(i, (i + 1) % 4) for i in range(4)])  21.2 us
    all_to_all x1, blocking collectives, body(): lax.all_to_all(potential.reshape(MEM * 4, 2, 128), TGT + ('zh',), 0, 0, t...  20.5 us
    all_to_all x1, blocking collectives, body(): parts = lax.all_to_all(joined, ('zl', 'zh'), 0, 0, tiled=True)  15.1 us
    ppermute x8, starting transfers between devices, down(): return lax.ppermute(v, axis, [(i, (i + 3) % 4) for i in range(4)])  12.9 us
    ppermute x4, starting transfers between devices, swap(): return lax.ppermute(v, axis, [(0, 1), (1, 0)])  11.3 us
    ppermute x8, starting transfers between devices, up(): return lax.ppermute(v, axis, [(i, (i + 1) % 4) for i in range(4)])  10.1 us
    pallas_call x1, Pallas kernels, body(): pl.pallas_call(coupling_kernel, out_shape=(jax.ShapeDtypeStruct((8, 16, S...  2.81 us
  transfers between devices with their start and end apart: 20, of which 9 were waited for; matrix products, arithmetic and copies ran while one was open for 2% of the time, Pallas kernels for 1%

profile of v6, /device:TPU:1, one launch (start us, length us, event | category | flops | bytes accessed | tf_op | source)
XLA Modules:
  0.0 105.2 jit_solution(11107347564276513315)
XLA Ops:
  0.7 0.9 constant_dynamic-slice_fusion
  1.8 2.6 %collective-permute-start = (bf16[1,32,3712]{2,1,0:T(8,128)(2,1)S(1)}, bf16[1,32,3712]{2,1,0:T(8,128)(2,1)S(1)}, u32[]{:S(2)}, u32[]{:S(2)}) collective-permute-start(bf16[1,32,3712]{2,1,0:T(8,128)(2,1)S(1)} %pad_maximum_fusion.2), channel_id=1, source_target_pairs={{0,8},{8,0},{1,9},{9,1},{2,10},{10,2},{3,11},{11,3},{4,12},{12,4},... | collective-permute-start | bytes 712712 | tf_op jit(solution)/shard_map/ppermute | solution.py:56
  5.2 1.4 %collective-permute-start.3 = (bf16[1,32,3712]{2,1,0:T(8,128)(2,1)S(1)}, bf16[1,32,3712]{2,1,0:T(8,128)(2,1)S(1)}, u32[]{:S(2)}, u32[]{:S(2)}) collective-permute-start(bf16[1,32,3712]{2,1,0:T(8,128)(2,1)S(1)} %pad_maximum_fusion.1), channel_id=1, source_target_pairs={{0,64},{64,128},{128,192},{192,0},{1,65},{65,129},{129,193},{193,1... | collective-permute-start | bytes 712712 | tf_op jit(solution)/shard_map/ppermute | solution.py:40
  6.5 1.5 %collective-permute-start.4 = (bf16[1,32,3712]{2,1,0:T(8,128)(2,1)S(1)}, bf16[1,32,3712]{2,1,0:T(8,128)(2,1)S(1)}, u32[]{:S(2)}, u32[]{:S(2)}) collective-permute-start(bf16[1,32,3712]{2,1,0:T(8,128)(2,1)S(1)} %pad_maximum_fusion.1), channel_id=1, source_target_pairs={{0,192},{64,0},{128,64},{192,128},{1,193},{65,1},{129,65},{193,129... | collective-permute-start | bytes 712712 | tf_op jit(solution)/shard_map/ppermute | solution.py:44
  8.1 0.7 collective-permute-done
  8.8 2.1 %collective-permute-start.1 = (bf16[1,32,3712]{2,1,0:T(8,128)(2,1)S(1)}, bf16[1,32,3712]{2,1,0:T(8,128)(2,1)S(1)}, u32[]{:S(2)}, u32[]{:S(2)}) collective-permute-start(bf16[1,32,3712]{2,1,0:T(8,128)(2,1)S(1)} %collective-permute-done), channel_id=1, source_target_pairs={{0,16},{16,32},{32,48},{48,0},{1,17},{17,33},{33,49},{49,1},{2,18}... | collective-permute-start | bytes 712712 | tf_op jit(solution)/shard_map/ppermute | solution.py:40
  10.9 1.3 %collective-permute-start.11 = (bf16[1,32,3712]{2,1,0:T(8,128)(2,1)S(1)}, bf16[1,32,3712]{2,1,0:T(8,128)(2,1)S(1)}, u32[]{:S(2)}, u32[]{:S(2)}) collective-permute-start(bf16[1,32,3712]{2,1,0:T(8,128)(2,1)S(1)} %collective-permute-done), channel_id=1, source_target_pairs={{0,48},{16,0},{32,16},{48,32},{1,49},{17,1},{33,17},{49,33},{2,50}... | collective-permute-start | bytes 712712 | tf_op jit(solution)/shard_map/ppermute | solution.py:44
  12.2 0.6 constant_dynamic-slice_fusion.2
  12.9 1.5 %collective-permute-start.5 = (bf16[1,16,3712]{2,1,0:T(8,128)(2,1)S(1)}, bf16[1,16,3712]{2,1,0:T(8,128)(2,1)S(1)}, u32[]{:S(2)}, u32[]{:S(2)}) collective-permute-start(bf16[1,16,3712]{2,1,0:T(8,128)(2,1)S(1)} %slice.47), channel_id=1, source_target_pairs={{0,64},{64,128},{128,192},{192,0},{1,65},{65,129},{129,193},{193,1... | collective-permute-start | bytes 356360 | tf_op jit(solution)/shard_map/ppermute | solution.py:40
  14.5 1.5 %collective-permute-start.6 = (bf16[1,16,3712]{2,1,0:T(8,128)(2,1)S(1)}, bf16[1,16,3712]{2,1,0:T(8,128)(2,1)S(1)}, u32[]{:S(2)}, u32[]{:S(2)}) collective-permute-start(bf16[1,16,3712]{2,1,0:T(8,128)(2,1)S(1)} %slice.48), channel_id=1, source_target_pairs={{0,192},{64,0},{128,64},{192,128},{1,193},{65,1},{129,65},{193,129... | collective-permute-start | bytes 356360 | tf_op jit(solution)/shard_map/ppermute | solution.py:44
  16.3 0.8 collective-permute-start.12
  17.2 2.0 %collective-permute-start.13 = (bf16[1,16,3712]{2,1,0:T(8,128)(2,1)S(1)}, bf16[1,16,3712]{2,1,0:T(8,128)(2,1)S(1)}, u32[]{:S(2)}, u32[]{:S(2)}) collective-permute-start(bf16[1,16,3712]{2,1,0:T(8,128)(2,1)S(1)} %slice.52), channel_id=1, source_target_pairs={{0,48},{16,0},{32,16},{48,32},{1,49},{17,1},{33,17},{49,33},{2,50}... | collective-permute-start | bytes 356360 | tf_op jit(solution)/shard_map/ppermute | solution.py:44
  19.3 1.6 %collective-permute-start.7 = (bf16[4,32,3712]{2,1,0:T(8,128)(2,1)S(1)}, bf16[4,32,3712]{2,1,0:T(8,128)(2,1)S(1)}, u32[]{:S(2)}, u32[]{:S(2)}) collective-permute-start(bf16[4,32,3712]{2,1,0:T(8,128)(2,1)S(1)} %maximum_maximum_fusion.refs_0_), channel_id=1, source_target_pairs={{0,48},{16,0},{32,16},{48,32},{1,49},{17,1},{33,17},{49,33},{2,50}... | collective-permute-start | bytes 2850824 | tf_op jit(solution)/shard_map/ppermute | solution.py:44
  21.4 1.9 %collective-permute-start.14 = (bf16[4,32,3712]{2,1,0:T(8,128)(2,1)S(1)}, bf16[4,32,3712]{2,1,0:T(8,128)(2,1)S(1)}, u32[]{:S(2)}, u32[]{:S(2)}) collective-permute-start(bf16[4,32,3712]{2,1,0:T(8,128)(2,1)S(1)} %maximum_maximum_fusion.1.refs_3_), channel_id=1, source_target_pairs={{0,64},{64,128},{128,192},{192,0},{1,65},{65,129},{129,193},{193,1... | collective-permute-start | bytes 2850824 | tf_op jit(solution)/shard_map/ppermute | solution.py:40
  23.3 1.5 %collective-permute-start.16 = (bf16[4,32,3712]{2,1,0:T(8,128)(2,1)S(1)}, bf16[4,32,3712]{2,1,0:T(8,128)(2,1)S(1)}, u32[]{:S(2)}, u32[]{:S(2)}) collective-permute-start(bf16[4,32,3712]{2,1,0:T(8,128)(2,1)S(1)} %maximum_maximum_fusion.1.refs_3_), channel_id=1, source_target_pairs={{0,192},{64,0},{128,64},{192,128},{1,193},{65,1},{129,65},{193,129... | collective-permute-start | bytes 2850824 | tf_op jit(solution)/shard_map/ppermute | solution.py:44
  25.0 1.1 %collective-permute-start.2 = (bf16[128,3328]{1,0:T(8,128)(2,1)S(1)}, bf16[128,3328]{1,0:T(8,128)(2,1)S(1)}, u32[]{:S(2)}, u32[]{:S(2)}) collective-permute-start(bf16[128,3328]{1,0:T(8,128)(2,1)S(1)} %pad_maximum_fusion), channel_id=1, source_target_pairs={{0,8},{8,0},{1,9},{9,1},{2,10},{10,2},{3,11},{11,3},{4,12},{12,4},... | collective-permute-start | bytes 2555912 | tf_op jit(solution)/shard_map/ppermute | solution.py:56
  26.2 15.5 %collective-permute-done.9.refs_2_ = bf16[4,32,3712]{2,1,0:T(8,128)(2,1)S(1)} collective-permute-done((bf16[4,32,3712]{2,1,0:T(8,128)(2,1)S(1)}, bf16[4,32,3712]{2,1,0:T(8,128)(2,1)S(1)}, u32[]{:S(2)}, u32[]{:S(2)}) %collective-permute-start.9) | collective-permute-done | bytes 950304 | tf_op jit(solution)/shard_map/ppermute | solution.py:40
  42.0 2.7 %collective-permute-start.8 = (bf16[2,32,3712]{2,1,0:T(8,128)(2,1)S(1)}, bf16[2,32,3712]{2,1,0:T(8,128)(2,1)S(1)}, u32[]{:S(2)}, u32[]{:S(2)}) collective-permute-start(bf16[2,32,3712]{2,1,0:T(8,128)(2,1)S(1)} %slice.49), channel_id=1, source_target_pairs={{0,48},{16,0},{32,16},{48,32},{1,49},{17,1},{33,17},{49,33},{2,50}... | collective-permute-start | bytes 1425416 | tf_op jit(solution)/shard_map/ppermute | solution.py:44
  44.8 2.1 %collective-permute-start.15 = (bf16[2,32,3712]{2,1,0:T(8,128)(2,1)S(1)}, bf16[2,32,3712]{2,1,0:T(8,128)(2,1)S(1)}, u32[]{:S(2)}, u32[]{:S(2)}) collective-permute-start(bf16[2,32,3712]{2,1,0:T(8,128)(2,1)S(1)} %slice.53), channel_id=1, source_target_pairs={{0,64},{64,128},{128,192},{192,0},{1,65},{65,129},{129,193},{193,1... | collective-permute-start | bytes 1425416 | tf_op jit(solution)/shard_map/ppermute | solution.py:40
  46.9 0.8 collective-permute-start.17
  47.8 1.2 %place.1 = (bf16[1536,3200]{1,0:T(8,128)(2,1)S(1)}, bf16[2048,256]{1,0:T(8,128)(2,1)S(1)}) custom-call(s32[32]{0:T(128)S(1)} %xor_add_fusion.slots, bf16[4,32,3712]{2,1,0:T(8,128)(2,1)S(1)} %maximum_maximum_fusion.refs_0_, bf16[4,32,3712]{2,1,0:T(8,128)(2,1)S(1)} %collective-permute-done.7.refs_1_, bf16[4,32,3712]{2,1,0:T(8,128)(2,1)S(1)} %collective-permute-done.9.refs_2_, ...), custom_call_target="tpu_custom_call" | custom-call | tf_op jit(solution)/shard_map/place/pallas_call | solution.py:218
  49.0 2.7 %collective-permute-done.10.refs_1_ = bf16[2,32,3712]{2,1,0:T(8,128)(2,1)S(1)} collective-permute-done((bf16[2,32,3712]{2,1,0:T(8,128)(2,1)S(1)}, bf16[2,32,3712]{2,1,0:T(8,128)(2,1)S(1)}, u32[]{:S(2)}, u32[]{:S(2)}) %collective-permute-start.10) | collective-permute-done | bytes 475168 | tf_op jit(solution)/shard_map/ppermute | solution.py:40
  51.7 2.4 %collective-permute-done.15.refs_2_ = bf16[2,32,3712]{2,1,0:T(8,128)(2,1)S(1)} collective-permute-done((bf16[2,32,3712]{2,1,0:T(8,128)(2,1)S(1)}, bf16[2,32,3712]{2,1,0:T(8,128)(2,1)S(1)}, u32[]{:S(2)}, u32[]{:S(2)}) %collective-permute-start.15) | collective-permute-done | bytes 475168 | tf_op jit(solution)/shard_map/ppermute | solution.py:40
  54.0 1.3 %collective-permute-done.17.refs_3_ = bf16[2,32,3712]{2,1,0:T(8,128)(2,1)S(1)} collective-permute-done((bf16[2,32,3712]{2,1,0:T(8,128)(2,1)S(1)}, bf16[2,32,3712]{2,1,0:T(8,128)(2,1)S(1)}, u32[]{:S(2)}, u32[]{:S(2)}) %collective-permute-start.17) | collective-permute-done | bytes 475168 | tf_op jit(solution)/shard_map/ppermute | solution.py:44
  55.4 2.8 %coupling.1 = (f32[8,16,512]{2,1,0:T(8,128)S(1)}, f32[8,16,512]{2,1,0:T(8,128)S(1)}, bf16[1536,3200]{1,0:T(8,128)(2,1)S(1)}, bf16[2048,256]{1,0:T(8,128)(2,1)S(1)}, bf16[2048,256]{1,0:T(8,128)(2,1)S(1)}) custom-call(s32[32]{0:T(128)S(1)} %xor_add_fusion.slots, s32[2,25]{1,0:T(2,128)S(1)} %pad_add_fusion.starts, ...), custom_call_target="tpu_custom_call", output_to_operand_aliasing={{2}: (9, {}), {3}: (10, {})} | custom-call | tf_op jit(solution)/shard_map/coupling/pallas_call | solution.py:229
  58.2 5.0 %collective-permute-start.18 = (f32[8,16,512]{2,1,0:T(8,128)S(1)}, f32[8,16,512]{2,1,0:T(8,128)S(1)}, u32[]{:S(2)}, u32[]{:S(2)}) collective-permute-start(f32[8,16,512]{2,1,0:T(8,128)S(1)} %get-tuple-element.51), channel_id=1, source_target_pairs={{0,1},{1,0},{2,3},{3,2},{4,5},{5,4},{6,7},{7,6},{8,9},{9,8},{10,11... | collective-permute-start | bytes 786440 | tf_op jit(solution)/shard_map/ppermute | solution.py:56
  63.3 1.1 %collective-permute-done.18 = f32[8,16,512]{2,1,0:T(8,128)S(1)} collective-permute-done((f32[8,16,512]{2,1,0:T(8,128)S(1)}, f32[8,16,512]{2,1,0:T(8,128)S(1)}, u32[]{:S(2)}, u32[]{:S(2)}) %collective-permute-start.18) | collective-permute-done | bytes 262176 | tf_op jit(solution)/shard_map/ppermute | solution.py:56
  64.5 15.1 %all_to_all.10.parts = f32[8,16,512]{2,1,0:T(8,128)S(1)} all-to-all(f32[8,16,512]{2,1,0:T(8,128)S(1)} %add.36), channel_id=1, replica_groups=mesh['y'=4,'x'=4,'zl'=2,'zh'=4,'c'=2] {'zl','zh'}, dimensions={0} | all-to-all | bytes 524288 | tf_op jit(solution)/shard_map/all_to_all | solution.py:253
  80.0 20.5 %all_to_all.11 = bf16[128,2,128]{2,1,0:T(2,128)(2,1)S(1)} all-to-all(bf16[128,2,128]{2,1,0:T(2,128)(2,1)S(1)} %bitcast.22), channel_id=1, replica_groups=mesh['y'=4,'x'=4,'zl'=2,'zh'=4,'c'=2] {'y','x','zl','zh'}, dimensions={0} | all-to-all | bytes 131072 | tf_op jit(solution)/shard_map/all_to_all | solution.py:267
  101.2 2.6 %collective-permute-start.19 = (f32[16,256]{1,0:T(8,128)S(1)}, f32[16,256]{1,0:T(8,128)S(1)}, u32[]{:S(2)}, u32[]{:S(2)}) collective-permute-start(f32[16,256]{1,0:T(8,128)S(1)} %fusion.1), channel_id=1, source_target_pairs={{0,1},{1,0},{2,3},{3,2},{4,5},{5,4},{6,7},{7,6},{8,9},{9,8},{10,11... | collective-permute-start | bytes 49160 | tf_op jit(solution)/shard_map/ppermute | solution.py:56
  103.8 0.7 copy.17
  104.6 0.6 add_bitcast_fusion
  (61 shorter events, 3.5 us)
Async XLA Ops:
  0.6 1.0 copy-start
  0.6 11.6 %copy-start.2 = (bf16[128,6400]{1,0:T(8,128)(2,1)S(1)}, bf16[128,6400]{1,0:T(8,128)(2,1)}, u32[]{:S(2)}) copy-start(bf16[128,6400]{1,0:T(8,128)(2,1)} %param.10) | copy-start | bytes 4915204
  0.7 4.5 %copy-start.7 = (s32[1,50]{1,0:T(1,128)S(1)}, s32[1,50]{1,0:T(1,128)}, u32[]{:S(2)}) copy-start(s32[1,50]{1,0:T(1,128)} %param.12) | copy-start | bytes 604
  1.8 7.0 %collective-permute-start = (bf16[1,32,3712]{2,1,0:T(8,128)(2,1)S(1)}, bf16[1,32,3712]{2,1,0:T(8,128)(2,1)S(1)}, u32[]{:S(2)}, u32[]{:S(2)}) collective-permute-start(bf16[1,32,3712]{2,1,0:T(8,128)(2,1)S(1)} %pad_maximum_fusion.2), channel_id=1, source_target_pairs={{0,8},{8,0},{1,9},{9,1},{2,10},{10,2},{3,11},{11,3},{4,12},{12,4},... | collective-permute-start | bytes 712712 | tf_op jit(solution)/shard_map/ppermute | solution.py:56
  5.2 7.7 %collective-permute-start.3 = (bf16[1,32,3712]{2,1,0:T(8,128)(2,1)S(1)}, bf16[1,32,3712]{2,1,0:T(8,128)(2,1)S(1)}, u32[]{:S(2)}, u32[]{:S(2)}) collective-permute-start(bf16[1,32,3712]{2,1,0:T(8,128)(2,1)S(1)} %pad_maximum_fusion.1), channel_id=1, source_target_pairs={{0,64},{64,128},{128,192},{192,0},{1,65},{65,129},{129,193},{193,1... | collective-permute-start | bytes 712712 | tf_op jit(solution)/shard_map/ppermute | solution.py:40
  6.5 7.9 %collective-permute-start.4 = (bf16[1,32,3712]{2,1,0:T(8,128)(2,1)S(1)}, bf16[1,32,3712]{2,1,0:T(8,128)(2,1)S(1)}, u32[]{:S(2)}, u32[]{:S(2)}) collective-permute-start(bf16[1,32,3712]{2,1,0:T(8,128)(2,1)S(1)} %pad_maximum_fusion.1), channel_id=1, source_target_pairs={{0,192},{64,0},{128,64},{192,128},{1,193},{65,1},{129,65},{193,129... | collective-permute-start | bytes 712712 | tf_op jit(solution)/shard_map/ppermute | solution.py:44
  8.8 7.5 %collective-permute-start.1 = (bf16[1,32,3712]{2,1,0:T(8,128)(2,1)S(1)}, bf16[1,32,3712]{2,1,0:T(8,128)(2,1)S(1)}, u32[]{:S(2)}, u32[]{:S(2)}) collective-permute-start(bf16[1,32,3712]{2,1,0:T(8,128)(2,1)S(1)} %collective-permute-done), channel_id=1, source_target_pairs={{0,16},{16,32},{32,48},{48,0},{1,17},{17,33},{33,49},{49,1},{2,18}... | collective-permute-start | bytes 712712 | tf_op jit(solution)/shard_map/ppermute | solution.py:40
  10.9 6.2 %collective-permute-start.11 = (bf16[1,32,3712]{2,1,0:T(8,128)(2,1)S(1)}, bf16[1,32,3712]{2,1,0:T(8,128)(2,1)S(1)}, u32[]{:S(2)}, u32[]{:S(2)}) collective-permute-start(bf16[1,32,3712]{2,1,0:T(8,128)(2,1)S(1)} %collective-permute-done), channel_id=1, source_target_pairs={{0,48},{16,0},{32,16},{48,32},{1,49},{17,1},{33,17},{49,33},{2,50}... | collective-permute-start | bytes 712712 | tf_op jit(solution)/shard_map/ppermute | solution.py:44
  12.9 6.3 %collective-permute-start.5 = (bf16[1,16,3712]{2,1,0:T(8,128)(2,1)S(1)}, bf16[1,16,3712]{2,1,0:T(8,128)(2,1)S(1)}, u32[]{:S(2)}, u32[]{:S(2)}) collective-permute-start(bf16[1,16,3712]{2,1,0:T(8,128)(2,1)S(1)} %slice.47), channel_id=1, source_target_pairs={{0,64},{64,128},{128,192},{192,0},{1,65},{65,129},{129,193},{193,1... | collective-permute-start | bytes 356360 | tf_op jit(solution)/shard_map/ppermute | solution.py:40
  14.5 4.7 %collective-permute-start.6 = (bf16[1,16,3712]{2,1,0:T(8,128)(2,1)S(1)}, bf16[1,16,3712]{2,1,0:T(8,128)(2,1)S(1)}, u32[]{:S(2)}, u32[]{:S(2)}) collective-permute-start(bf16[1,16,3712]{2,1,0:T(8,128)(2,1)S(1)} %slice.48), channel_id=1, source_target_pairs={{0,192},{64,0},{128,64},{192,128},{1,193},{65,1},{129,65},{193,129... | collective-permute-start | bytes 356360 | tf_op jit(solution)/shard_map/ppermute | solution.py:44
  16.3 5.0 %collective-permute-start.12 = (bf16[1,16,3712]{2,1,0:T(8,128)(2,1)S(1)}, bf16[1,16,3712]{2,1,0:T(8,128)(2,1)S(1)}, u32[]{:S(2)}, u32[]{:S(2)}) collective-permute-start(bf16[1,16,3712]{2,1,0:T(8,128)(2,1)S(1)} %slice.51), channel_id=1, source_target_pairs={{0,16},{16,32},{32,48},{48,0},{1,17},{17,33},{33,49},{49,1},{2,18}... | collective-permute-start | bytes 356360 | tf_op jit(solution)/shard_map/ppermute | solution.py:40
  17.2 4.1 %collective-permute-start.13 = (bf16[1,16,3712]{2,1,0:T(8,128)(2,1)S(1)}, bf16[1,16,3712]{2,1,0:T(8,128)(2,1)S(1)}, u32[]{:S(2)}, u32[]{:S(2)}) collective-permute-start(bf16[1,16,3712]{2,1,0:T(8,128)(2,1)S(1)} %slice.52), channel_id=1, source_target_pairs={{0,48},{16,0},{32,16},{48,32},{1,49},{17,1},{33,17},{49,33},{2,50}... | collective-permute-start | bytes 356360 | tf_op jit(solution)/shard_map/ppermute | solution.py:44
  19.3 22.7 %collective-permute-start.7 = (bf16[4,32,3712]{2,1,0:T(8,128)(2,1)S(1)}, bf16[4,32,3712]{2,1,0:T(8,128)(2,1)S(1)}, u32[]{:S(2)}, u32[]{:S(2)}) collective-permute-start(bf16[4,32,3712]{2,1,0:T(8,128)(2,1)S(1)} %maximum_maximum_fusion.refs_0_), channel_id=1, source_target_pairs={{0,48},{16,0},{32,16},{48,32},{1,49},{17,1},{33,17},{49,33},{2,50}... | collective-permute-start | bytes 2850824 | tf_op jit(solution)/shard_map/ppermute | solution.py:44
  20.9 20.8 %collective-permute-start.9 = (bf16[4,32,3712]{2,1,0:T(8,128)(2,1)S(1)}, bf16[4,32,3712]{2,1,0:T(8,128)(2,1)S(1)}, u32[]{:S(2)}, u32[]{:S(2)}) collective-permute-start(bf16[4,32,3712]{2,1,0:T(8,128)(2,1)S(1)} %maximum_maximum_fusion.refs_0_), channel_id=1, source_target_pairs={{0,16},{16,32},{32,48},{48,0},{1,17},{17,33},{33,49},{49,1},{2,18}... | collective-permute-start | bytes 2850824 | tf_op jit(solution)/shard_map/ppermute | solution.py:40
  21.4 23.4 %collective-permute-start.14 = (bf16[4,32,3712]{2,1,0:T(8,128)(2,1)S(1)}, bf16[4,32,3712]{2,1,0:T(8,128)(2,1)S(1)}, u32[]{:S(2)}, u32[]{:S(2)}) collective-permute-start(bf16[4,32,3712]{2,1,0:T(8,128)(2,1)S(1)} %maximum_maximum_fusion.1.refs_3_), channel_id=1, source_target_pairs={{0,64},{64,128},{128,192},{192,0},{1,65},{65,129},{129,193},{193,1... | collective-permute-start | bytes 2850824 | tf_op jit(solution)/shard_map/ppermute | solution.py:40
  23.3 23.5 %collective-permute-start.16 = (bf16[4,32,3712]{2,1,0:T(8,128)(2,1)S(1)}, bf16[4,32,3712]{2,1,0:T(8,128)(2,1)S(1)}, u32[]{:S(2)}, u32[]{:S(2)}) collective-permute-start(bf16[4,32,3712]{2,1,0:T(8,128)(2,1)S(1)} %maximum_maximum_fusion.1.refs_3_), channel_id=1, source_target_pairs={{0,192},{64,0},{128,64},{192,128},{1,193},{65,1},{129,65},{193,129... | collective-permute-start | bytes 2850824 | tf_op jit(solution)/shard_map/ppermute | solution.py:44
  25.0 22.7 %copy-start.4 = (s32[32]{0:T(128)S(1)}, s32[32]{0:T(128)}, u32[]{:S(2)}) copy-start(s32[32]{0:T(128)} %constant.46.clone) | copy-start | bytes 388
  25.0 22.7 %copy-start.5 = (s32[32]{0:T(128)S(1)}, s32[32]{0:T(128)}, u32[]{:S(2)}) copy-start(s32[32]{0:T(128)} %constant.47.clone) | copy-start | bytes 388
  25.0 22.7 %copy-start.6 = (s32[32]{0:T(128)S(1)}, s32[32]{0:T(128)}, u32[]{:S(2)}) copy-start(s32[32]{0:T(128)} %constant.48.clone) | copy-start | bytes 388
  25.0 22.7 %collective-permute-start.2 = (bf16[128,3328]{1,0:T(8,128)(2,1)S(1)}, bf16[128,3328]{1,0:T(8,128)(2,1)S(1)}, u32[]{:S(2)}, u32[]{:S(2)}) collective-permute-start(bf16[128,3328]{1,0:T(8,128)(2,1)S(1)} %pad_maximum_fusion), channel_id=1, source_target_pairs={{0,8},{8,0},{1,9},{9,1},{2,10},{10,2},{3,11},{11,3},{4,12},{12,4},... | collective-permute-start | bytes 2555912 | tf_op jit(solution)/shard_map/ppermute | solution.py:56
  41.7 10.0 %collective-permute-start.10 = (bf16[2,32,3712]{2,1,0:T(8,128)(2,1)S(1)}, bf16[2,32,3712]{2,1,0:T(8,128)(2,1)S(1)}, u32[]{:S(2)}, u32[]{:S(2)}) collective-permute-start(bf16[2,32,3712]{2,1,0:T(8,128)(2,1)S(1)} %slice.50), channel_id=1, source_target_pairs={{0,16},{16,32},{32,48},{48,0},{1,17},{17,33},{33,49},{49,1},{2,18}... | collective-permute-start | bytes 1425416 | tf_op jit(solution)/shard_map/ppermute | solution.py:40
  42.0 9.7 %collective-permute-start.8 = (bf16[2,32,3712]{2,1,0:T(8,128)(2,1)S(1)}, bf16[2,32,3712]{2,1,0:T(8,128)(2,1)S(1)}, u32[]{:S(2)}, u32[]{:S(2)}) collective-permute-start(bf16[2,32,3712]{2,1,0:T(8,128)(2,1)S(1)} %slice.49), channel_id=1, source_target_pairs={{0,48},{16,0},{32,16},{48,32},{1,49},{17,1},{33,17},{49,33},{2,50}... | collective-permute-start | bytes 1425416 | tf_op jit(solution)/shard_map/ppermute | solution.py:44
  44.8 9.2 %collective-permute-start.15 = (bf16[2,32,3712]{2,1,0:T(8,128)(2,1)S(1)}, bf16[2,32,3712]{2,1,0:T(8,128)(2,1)S(1)}, u32[]{:S(2)}, u32[]{:S(2)}) collective-permute-start(bf16[2,32,3712]{2,1,0:T(8,128)(2,1)S(1)} %slice.53), channel_id=1, source_target_pairs={{0,64},{64,128},{128,192},{192,0},{1,65},{65,129},{129,193},{193,1... | collective-permute-start | bytes 1425416 | tf_op jit(solution)/shard_map/ppermute | solution.py:40
  46.9 8.5 %collective-permute-start.17 = (bf16[2,32,3712]{2,1,0:T(8,128)(2,1)S(1)}, bf16[2,32,3712]{2,1,0:T(8,128)(2,1)S(1)}, u32[]{:S(2)}, u32[]{:S(2)}) collective-permute-start(bf16[2,32,3712]{2,1,0:T(8,128)(2,1)S(1)} %slice.54), channel_id=1, source_target_pairs={{0,192},{64,0},{128,64},{192,128},{1,193},{65,1},{129,65},{193,129... | collective-permute-start | bytes 1425416 | tf_op jit(solution)/shard_map/ppermute | solution.py:44
  55.4 7.9 %copy-start.3 = (f32[6,32,128]{2,1,0:T(8,128)S(1)}, f32[6,32,128]{2,1,0:T(8,128)}, u32[]{:S(2)}) copy-start(f32[6,32,128]{2,1,0:T(8,128)} %param.15) | copy-start | bytes 294916
  55.4 24.1 %copy-start.1 = (f32[32]{0:T(128)S(1)}, f32[32]{0:T(128)}, u32[]{:S(2)}) copy-start(f32[32]{0:T(128)} %param.14) | copy-start | bytes 388
  58.2 6.2 %collective-permute-start.18 = (f32[8,16,512]{2,1,0:T(8,128)S(1)}, f32[8,16,512]{2,1,0:T(8,128)S(1)}, u32[]{:S(2)}, u32[]{:S(2)}) collective-permute-start(f32[8,16,512]{2,1,0:T(8,128)S(1)} %get-tuple-element.51), channel_id=1, source_target_pairs={{0,1},{1,0},{2,3},{3,2},{4,5},{5,4},{6,7},{7,6},{8,9},{9,8},{10,11... | collective-permute-start | bytes 786440 | tf_op jit(solution)/shard_map/ppermute | solution.py:56
  101.2 3.4 %collective-permute-start.19 = (f32[16,256]{1,0:T(8,128)S(1)}, f32[16,256]{1,0:T(8,128)S(1)}, u32[]{:S(2)}, u32[]{:S(2)}) collective-permute-start(f32[16,256]{1,0:T(8,128)S(1)} %fusion.1), channel_id=1, source_target_pairs={{0,1},{1,0},{2,3},{3,2},{4,5},{5,4},{6,7},{7,6},{8,9},{9,8},{10,11... | collective-permute-start | bytes 49160 | tf_op jit(solution)/shard_map/ppermute | solution.py:56
